TPU v7x, 128 devices: a whole 4x4x4 slice. The times are simulated.
128 devices in a mesh: gx: 4 (over y), gy: 8 (over z, core), sa: 4 (over x).
Axes of the slice: x: 4, y: 4, z: 4, core: 2. Of those that a mesh axis runs over, the one named last changes fastest.
Arguments:
- pixels: bfloat16 [16, 2048, 8192], P('sa', 'gy', 'gx'), may hold values from -6 to 6
- peak_offsets: int32 [16, 2, 32, 128], P('sa', None, 'gy', 'gx'), may hold values from -2 to 2
- validity: int32 [16, 32, 128], P('sa', 'gy', 'gx'), may hold values 0 or 1
Outputs:
- flow_field: float32 [16, 2, 32, 128], P('sa', None, 'gy', 'gx')
- mesh_field: float32 [16, 2, 32, 128], P('sa', None, 'gy', 'gx')
All inputs are finite; a program needn't handle non-finite values. No bound on the sum of `validity` on one device may be relied on, other than what follows from the above.
Results may differ from a plain program's by a relative error of at most 0.0035.
Values may be sent and summed in bfloat16 or wider, within the bound.
No kernel may reach another device: no remote copies, remote signals or barrier semaphores. Data moves between devices by JAX's collectives and lax.ppermute only.
A program may use at most 192 MiB of HBM per device.

v0:
```python
import math

import jax
import jax.numpy as jnp
from jax import lax
from jax.sharding import PartitionSpec as P

PATCH = 64
RELAX = 8


spring_plane = 0.5
spring_stack = 1.0
step_size = 0.2
damping = 0.6
whiten_floor = 1024.0


def shifted(block, axis, distance):
    devices = range(lax.axis_size(axis))
    route = [(i - distance, i) for i in devices if i - distance in devices]
    return lax.ppermute(block, axis, route)


def laid_out(parts, dim):
    dims = list(parts.shape[1:])
    dims[dim] *= parts.shape[0]
    return jnp.moveaxis(parts, 0, dim).reshape(dims)


def gather_together(arrays, axis, dims):
    ravelled = jnp.concatenate([a.reshape(-1) for a in arrays])
    lines, at, gathered = (lax.all_gather(ravelled, axis), 0, [])
    for a, dim in zip(arrays, dims):
        parts = lines[:, at : at + a.size].reshape(-1, *a.shape)
        gathered.append(laid_out(parts, dim))
        at += a.size
    return tuple(gathered)


def dft_tables():
    frequency = jnp.arange(PATCH, dtype=jnp.int32)
    phases = frequency[:, None] * frequency[None, :] % PATCH
    angles = phases.astype(jnp.float32) * (2.0 * math.pi / PATCH)
    return (jnp.cos(angles).astype(jnp.bfloat16), jnp.sin(angles).astype(jnp.bfloat16))


def column_tables():
    position = jnp.arange(2 * PATCH, dtype=jnp.int32)
    same_block = position[:, None] // PATCH == position[None, :] // PATCH
    phases = position[:, None] % PATCH * (position[None, :] % PATCH) % PATCH
    angles = phases.astype(jnp.float32) * (2.0 * math.pi / PATCH)
    cosine = jnp.where(same_block, jnp.cos(angles).astype(jnp.bfloat16).astype(jnp.float32), 0.0)
    sine_table = jnp.where(
        same_block, jnp.sin(angles).astype(jnp.bfloat16).astype(jnp.float32), 0.0
    )
    return (cosine.astype(jnp.bfloat16), (-sine_table).astype(jnp.bfloat16))


def transform_rows(row_table, blocks):
    return jnp.einsum("kx,axc->akc", row_table, blocks, preferred_element_type=jnp.float32)


def spectra(section_image):
    height, breadth = section_image.shape
    cosine_cols, sine_cols = column_tables()
    flat = section_image.reshape(-1, 2 * PATCH)
    col_real = (
        jnp.dot(flat, cosine_cols, preferred_element_type=jnp.float32)
        .astype(jnp.bfloat16)
        .reshape(height // PATCH, PATCH, breadth)
    )
    col_imag = (
        jnp.dot(flat, sine_cols, preferred_element_type=jnp.float32)
        .astype(jnp.bfloat16)
        .reshape(height // PATCH, PATCH, breadth)
    )
    cosine, sine_table = dft_tables()
    spec_real = transform_rows(cosine, col_real) + transform_rows(sine_table, col_imag)
    spec_imag = transform_rows(cosine, col_imag) - transform_rows(sine_table, col_real)
    return (
        spec_real.reshape(height, breadth).astype(jnp.bfloat16),
        spec_imag.reshape(height, breadth).astype(jnp.bfloat16),
    )


def phase_tables(offsets):
    frequency = jnp.arange(PATCH, dtype=jnp.int32)
    nearby = jnp.arange(3, dtype=jnp.int32) - 1
    phases = (
        frequency[None, None, :, None]
        * (offsets[:, :, None, None] + nearby[None, None, None, :])
        % PATCH
    )
    angles = phases.astype(jnp.float32) * (2.0 * math.pi / PATCH)
    return (jnp.cos(angles).astype(jnp.bfloat16), jnp.sin(angles).astype(jnp.bfloat16))


def subpixel(correlation, offsets):
    center = correlation[..., 1, 1]
    row_low = correlation[..., 0, 1]
    row_high = correlation[..., 2, 1]
    col_low = correlation[..., 1, 0]
    col_high = correlation[..., 1, 2]
    row_step = (row_low - row_high) / (
        2.0 * jnp.maximum(jnp.abs(row_low - 2.0 * center + row_high), 1.0)
    )
    col_step = (col_low - col_high) / (
        2.0 * jnp.maximum(jnp.abs(col_low - 2.0 * center + col_high), 1.0)
    )
    return jnp.stack(
        [offsets[0].astype(jnp.float32) + row_step, offsets[1].astype(jnp.float32) + col_step], 0
    )


def refine(current, previous, offsets):
    patch_rows, patch_cols = (offsets.shape[1], offsets.shape[2])
    layout = (patch_rows, PATCH, patch_cols, PATCH)
    now_real = current[0].astype(jnp.float32).reshape(layout)
    now_imag = current[1].astype(jnp.float32).reshape(layout)
    old_real = previous[0].astype(jnp.float32).reshape(layout)
    old_imag = previous[1].astype(jnp.float32).reshape(layout)
    cross_real = now_real * old_real + now_imag * old_imag
    cross_imag = now_imag * old_real - now_real * old_imag
    scale = jnp.sqrt(
        cross_real * cross_real + cross_imag * cross_imag + whiten_floor * whiten_floor
    )
    prod_real = (cross_real / scale).astype(jnp.bfloat16)
    prod_imag = (cross_imag / scale).astype(jnp.bfloat16)
    col_cos, col_sin = phase_tables(offsets[1])
    row_cos, row_sin = phase_tables(offsets[0])
    wide = jnp.float32
    half_real = (
        jnp.einsum("akbj,abjd->akbd", prod_real, col_cos, preferred_element_type=wide)
        - jnp.einsum("akbj,abjd->akbd", prod_imag, col_sin, preferred_element_type=wide)
    ).astype(jnp.bfloat16)
    half_imag = (
        jnp.einsum("akbj,abjd->akbd", prod_real, col_sin, preferred_element_type=wide)
        + jnp.einsum("akbj,abjd->akbd", prod_imag, col_cos, preferred_element_type=wide)
    ).astype(jnp.bfloat16)
    correlation = (
        jnp.einsum("akbd,abke->abed", half_real, row_cos, preferred_element_type=wide)
        - jnp.einsum("akbd,abke->abed", half_imag, row_sin, preferred_element_type=wide)
    ) / float(PATCH)
    return subpixel(correlation, offsets)


def edge_degree(row_index, col_index, total_rows, total_cols):
    return (
        4.0
        - (row_index == 0).astype(jnp.float32)
        - (row_index == total_rows - 1).astype(jnp.float32)
        - (col_index == 0).astype(jnp.float32)
        - (col_index == total_cols - 1).astype(jnp.float32)
    )


def spring_step(state, velocity, padded, weight, flow_field, weight_next, flow_next, degree):
    neighbours = (
        padded[1:-1, :, :-2, 1:-1]
        + padded[1:-1, :, 2:, 1:-1]
        + padded[1:-1, :, 1:-1, :-2]
        + padded[1:-1, :, 1:-1, 2:]
    )
    lower_mesh = padded[:-2, :, 1:-1, 1:-1]
    upper_mesh = padded[2:, :, 1:-1, 1:-1]
    here_term = weight * (state - lower_mesh - flow_field)
    next_term = weight_next * (upper_mesh - state - flow_next)
    gradient = spring_plane * (degree * state - neighbours) + spring_stack * (here_term - next_term)
    velocity = damping * velocity - step_size * gradient
    return (state + velocity, velocity)


def arrange_whole(gathered, count_x, count_y, count_s):
    shape = gathered.shape
    blocks = gathered.reshape((count_x, count_y, count_s) + shape[1:])
    blocks = jnp.transpose(blocks, (2, 3, 4, 1, 5, 0, 6))
    return blocks.reshape(count_s * shape[1], shape[2], count_y * shape[3], count_x * shape[4])


def per_device(pixels, peak_offsets, validity):
    count = pixels.shape[0]
    last_spectra = None
    last_spectra = spectra(pixels[count - 1])
    earlier = shifted((last_spectra[0], last_spectra[1]), "sa", 1)
    flows = []
    for section in range(count):
        if last_spectra is not None and section == count - 1:
            current = last_spectra
        else:
            current = spectra(pixels[section])
        flows.append(refine(current, earlier, peak_offsets[section]))
        earlier = current
    flow_field = jnp.stack(flows, 0)
    weight = validity.astype(jnp.float32)[:, None]
    patch_rows, patch_cols = (flow_field.shape[2], flow_field.shape[3])
    count_x, count_y, count_s = (lax.axis_size("gx"), lax.axis_size("gy"), lax.axis_size("sa"))
    total_rows = patch_rows * count_y
    total_cols = patch_cols * count_x
    whole_flow, whole_weight = gather_together(
        (flow_field[None], weight[None]), ("gx", "gy", "sa"), (0, 0)
    )
    all_flow = arrange_whole(whole_flow, count_x, count_y, count_s)
    all_weight = arrange_whole(whole_weight, count_x, count_y, count_s)
    all_state = jnp.cumsum(all_flow, axis=0)
    weight_next = jnp.concatenate([all_weight[1:], jnp.zeros_like(all_weight[:1])], 0)
    flow_next = jnp.concatenate([all_flow[1:], jnp.zeros_like(all_flow[:1])], 0)
    row_index = jnp.arange(total_rows, dtype=jnp.int32)[:, None]
    col_index = jnp.arange(total_cols, dtype=jnp.int32)[None, :]
    degree = edge_degree(row_index, col_index, total_rows, total_cols)

    def relax_whole(carry, unused):
        state, velocity = carry
        padded = jnp.pad(state, ((1, 1), (0, 0), (1, 1), (1, 1)))
        return (
            spring_step(
                state, velocity, padded, all_weight, all_flow, weight_next, flow_next, degree
            ),
            None,
        )

    final, unused_out = lax.scan(
        relax_whole, (all_state, jnp.zeros_like(all_state)), None, length=RELAX
    )
    zero = jnp.zeros((), jnp.int32)
    starts = (
        lax.axis_index("sa") * count,
        zero,
        lax.axis_index("gy") * patch_rows,
        lax.axis_index("gx") * patch_cols,
    )
    mesh_field = lax.dynamic_slice(final[0], starts, flow_field.shape)
    return (flow_field, mesh_field)


def solution(mesh):
    return jax.shard_map(
        per_device,
        mesh=mesh,
        in_specs=(P("sa", "gy", "gx"), P("sa", None, "gy", "gx"), P("sa", "gy", "gx")),
        out_specs=(P("sa", None, "gy", "gx"), P("sa", None, "gy", "gx")),
        check_vma=False,
    )
```

profile of v0, /device:TPU:1, one launch (start us, length us, event | category | flops | bytes accessed | tf_op | source)
XLA Modules:
  0.0 334.7 jit_solution(13951213057219353038)
XLA Ops:
  0.6 4.0 %fusion.499 = (bf16[1,256,2048]{2,1,0:T(8,128)(2,1)}, bf16[1,256,2048]{2,1,0:T(8,128)(2,1)S(1)}, bf16[1,256,2048]{2,1,0:T(8,128)(2,1)}, bf16[1,256,2048]{2,1,0:T(8,128)(2,1)}) fusion(bf16[4,256,2048]{2,1,0:T(8,128)(2,1)} %param.5), kind=kLoop, calls=%fused_computation.551 | loop fusion | bytes 8388608 | tf_op jit(solution)/shard_map/slice | solution.py:191
  12.6 3.9 %bitcast_convert_fusion.1 = (f32[4,64,2048]{2,1,0:T(8,128)}, bf16[4,2048,64]{1,2,0:T(8,128)(2,1)}) fusion(f32[4,2048,64]{1,2,0:T(8,128)} %fusion.241, bf16[4,64,2048]{2,1,0:T(8,128)(2,1)S(1)} %reshape.863), kind=kOutput, calls=%fused_computation.157 | convolution fusion | flops 68743168 | bytes 6291456 | tf_op jit(solution)/shard_map/kx,axc->akc/dot_general | solution.py:61
  16.5 4.9 %collective-permute-start = (bf16[256,2048]{1,0:T(8,128)(2,1)}, bf16[256,2048]{1,0:T(8,128)(2,1)}, u32[]{:S(2)}, u32[]{:S(2)}) collective-permute-start(bf16[256,2048]{1,0:T(8,128)(2,1)} %bitcast.11), channel_id=1, source_target_pairs={{0,1},{1,2},{2,3},{4,5},{5,6},{6,7},{8,9},{9,10},{10,11},{12,13},{... | collective-permute-start | bytes 3145736 | tf_op jit(solution)/shard_map/ppermute | solution.py:22
  24.1 3.4 %collective-permute-start.1 = (bf16[256,2048]{1,0:T(8,128)(2,1)}, bf16[256,2048]{1,0:T(8,128)(2,1)}, u32[]{:S(2)}, u32[]{:S(2)}) collective-permute-start(bf16[256,2048]{1,0:T(8,128)(2,1)} %bitcast.14), channel_id=1, source_target_pairs={{0,1},{1,2},{2,3},{4,5},{5,6},{6,7},{8,9},{9,10},{10,11},{12,13},{... | collective-permute-start | bytes 3145736 | tf_op jit(solution)/shard_map/ppermute | solution.py:22
  38.7 4.9 %reshape.884 = f32[4,64,32,64]{3,2,1,0:T(8,128)} reshape(f32[4,64,2048]{2,1,0:T(8,128)} %get-tuple-element.237) | data formatting | bytes 4194304 | tf_op jit(solution)/shard_map/convert_element_type | solution.py:119
  43.6 4.9 %reshape.885 = f32[4,64,32,64]{3,2,1,0:T(8,128)} reshape(f32[4,64,2048]{2,1,0:T(8,128)} %get-tuple-element.239) | data formatting | bytes 4194304 | tf_op jit(solution)/shard_map/convert_element_type | solution.py:120
  60.0 4.9 %reshape.880 = f32[4,64,32,64]{3,2,1,0:T(8,128)} reshape(f32[4,64,2048]{2,1,0:T(8,128)} %fusion.35) | data formatting | bytes 4194304 | tf_op jit(solution)/shard_map/convert_element_type | solution.py:119
  64.9 3.5 %fusion.38 = f32[4,64,2048]{2,1,0:T(8,128)} fusion(f32[4,2048,64]{1,2,0:T(8,128)} %fusion.249, bf16[4,64,2048]{2,1,0:T(8,128)(2,1)S(1)} %reshape.868), kind=kOutput, calls=%fused_computation.81 | convolution fusion | flops 68743168 | bytes 5242880 | tf_op jit(solution)/shard_map/kx,axc->akc/dot_general | solution.py:61
  68.4 5.4 %reshape.881 = f32[4,64,32,64]{3,2,1,0:T(8,128)} reshape(f32[4,64,2048]{2,1,0:T(8,128)} %fusion.38) | data formatting | bytes 4194304 | tf_op jit(solution)/shard_map/convert_element_type | solution.py:120
  83.5 4.9 %reshape.882 = f32[4,64,32,64]{3,2,1,0:T(8,128)} reshape(f32[4,64,2048]{2,1,0:T(8,128)} %fusion.41) | data formatting | bytes 4194304 | tf_op jit(solution)/shard_map/convert_element_type | solution.py:119
  88.4 3.5 %fusion.44 = f32[4,64,2048]{2,1,0:T(8,128)} fusion(f32[4,2048,64]{1,2,0:T(8,128)} %fusion.253, bf16[4,64,2048]{2,1,0:T(8,128)(2,1)S(1)} %reshape.870), kind=kOutput, calls=%fused_computation.87 | convolution fusion | flops 68743168 | bytes 5242880 | tf_op jit(solution)/shard_map/kx,axc->akc/dot_general | solution.py:61
  91.9 5.0 %reshape.883 = f32[4,64,32,64]{3,2,1,0:T(8,128)} reshape(f32[4,64,2048]{2,1,0:T(8,128)} %fusion.44) | data formatting | bytes 4194304 | tf_op jit(solution)/shard_map/convert_element_type | solution.py:120
  106.6 4.8 %reshape.874 = f32[4,64,32,64]{3,2,1,0:T(8,128)} reshape(f32[4,64,2048]{2,1,0:T(8,128)} %fusion.27) | data formatting | bytes 4194304 | tf_op jit(solution)/shard_map/convert_element_type | solution.py:119
  111.4 3.5 %fusion.31 = f32[4,64,2048]{2,1,0:T(8,128)} fusion(f32[4,2048,64]{1,2,0:T(8,128)} %fusion.243, bf16[4,64,2048]{2,1,0:T(8,128)(2,1)S(1)} %reshape.860), kind=kOutput, calls=%fused_computation.74 | convolution fusion | flops 68743168 | bytes 5242880 | tf_op jit(solution)/shard_map/kx,axc->akc/dot_general | solution.py:61
  114.9 4.9 %reshape.877 = f32[4,64,32,64]{3,2,1,0:T(8,128)} reshape(f32[4,64,2048]{2,1,0:T(8,128)} %fusion.31) | data formatting | bytes 4194304 | tf_op jit(solution)/shard_map/convert_element_type | solution.py:120
  120.2 4.7 %reshape.876 = f32[4,64,32,64]{3,2,1,0:T(8,128)} reshape(bf16[256,2048]{1,0:T(8,128)(2,1)} %collective-permute-done) | data formatting | bytes 3145728 | tf_op jit(solution)/shard_map/reshape | solution.py:121
  124.9 4.5 %reshape.879 = f32[4,64,32,64]{3,2,1,0:T(8,128)} reshape(bf16[256,2048]{1,0:T(8,128)(2,1)} %collective-permute-done.1) | data formatting | bytes 3145728 | tf_op jit(solution)/shard_map/reshape | solution.py:122
  129.4 27.3 %divide_convert_fusion.7 = (bf16[4,64,32,64]{3,2,1,0:T(8,128)(2,1)}, f32[4,64,32,64]{3,2,1,0:T(8,128)}, f32[4,64,32,64]{3,2,1,0:T(8,128)}, bf16[4,64,32,64]{3,2,...) fusion(f32[4,64,32,64]{3,2,1,0:T(8,128)} %reshape.877, ...), kind=kLoop, calls=%fused_computation.56 | loop fusion | flops 25165824 | bytes 41943040 | tf_op jit(solution)/shard_map/convert_element_type | solution.py:128
  156.7 5.4 %divide_convert_fusion.2 = bf16[4,64,32,64]{3,2,1,0:T(8,128)(2,1)S(1)} fusion(f32[4,64,32,64]{3,2,1,0:T(8,128)} %get-tuple-element.200, f32[4,64,32,64]{3,2,1,0:T(8,128)} %get-tuple-element.201), kind=kLoop, calls=%fused_computation.45 | loop fusion | flops 3145728 | bytes 5242880 | tf_op jit(solution)/shard_map/convert_element_type | solution.py:129
  162.1 3.4 %fusion.53 = f32[4,32,3,64]{3,2,1,0:T(4,128)} fusion(bf16[4,64,32,64]{3,2,1,0:T(8,128)(2,1)S(1)} %divide_convert_fusion.2, s32[4,32,3]{2,1,0:T(8,128)S(1)} %get-tuple-element.234), kind=kOutput, calls=%fused_computation.96 | convolution fusion | flops 3514368 | bytes 1148416 | tf_op jit(solution)/shard_map/akbj,abjd->akbd/dot_general | solution.py:139
  165.4 3.7 %fusion.55 = f32[4,32,3,64]{3,2,1,0:T(4,128)} fusion(bf16[4,64,32,64]{3,2,1,0:T(8,128)(2,1)S(1)} %divide_convert_fusion.2, s32[4,32,3]{2,1,0:T(8,128)S(1)} %get-tuple-element.234), kind=kOutput, calls=%fused_computation.98 | convolution fusion | flops 3514368 | bytes 1148416 | tf_op jit(solution)/shard_map/akbj,abjd->akbd/dot_general | solution.py:135
  192.0 6.7 %fusion.155 = f32[4,32,3,3]{3,2,1,0:T(4,128)} fusion(f32[4,32,3,64]{3,2,1,0:T(4,128)S(1)} %copy-done.19, bf16[4,64,32,64]{3,2,1,0:T(8,128)(2,1)} %get-tuple-element.199, s32[4,32,3]{2,1,0:T(8,128)S(1)} %get-tuple-element.233, s32[4,32,3]{2,1,0:T(8,128)S(1)} %get-tuple-element.234), kind=kOutput, calls=%fused_computation.151 | convolution fusion | flops 4079616 | bytes 1154560 | tf_op jit(solution)/shard_map/akbd,abke->abed/dot_general | solution.py:142
  198.7 6.1 %fusion.102 = f32[4,32,3,3]{3,2,1,0:T(4,128)S(1)} fusion(f32[4,32,3,3]{3,2,1,0:T(4,128)} %fusion.155, f32[4,32,3,64]{3,2,1,0:T(4,128)S(1)} %copy-done.18, bf16[4,64,32,64]{3,2,1,0:T(8,128)(2,1)} %get-tuple-element.199, s32[4,32,3]{2,1,0:T(8,128)S(1)} %get-tuple-element.233, s32[4,32,3]{2,1,0:T(8,128)S(1)} %get-tuple-element.234), kind=kOutput, calls=%fused_computation.131 | convolution fusion | flops 4081920 | bytes 1159168 | tf_op jit(solution)/shard_map/akbd,abke->abed/dot_general | solution.py:143
  207.1 6.2 %fusion.133 = f32[4,32,3,3]{3,2,1,0:T(4,128)S(1)} fusion(f32[4,32,3,64]{3,2,1,0:T(4,128)S(1)} %copy-done.17, bf16[4,64,32,64]{3,2,1,0:T(8,128)(2,1)} %get-tuple-element.184, s32[4,32,3]{2,1,0:T(8,128)S(1)} %get-tuple-element.229, s32[4,32,3]{2,1,0:T(8,128)S(1)} %get-tuple-element.230), kind=kOutput, calls=%fused_computation.145 | convolution fusion | flops 4079616 | bytes 1154560 | tf_op jit(solution)/shard_map/akbd,abke->abed/dot_general | solution.py:142
  213.2 6.1 %fusion.104 = f32[4,32,3,3]{3,2,1,0:T(4,128)S(1)} fusion(f32[4,32,3,3]{3,2,1,0:T(4,128)S(1)} %fusion.133, f32[4,32,3,64]{3,2,1,0:T(4,128)S(1)} %fusion.69, bf16[4,64,32,64]{3,2,1,0:T(8,128)(2,1)} %get-tuple-element.184, s32[4,32,3]{2,1,0:T(8,128)S(1)} %get-tuple-element.229, s32[4,32,3]{2,1,0:T(8,128)S(1)} %get-tuple-element.230), kind=kOutput, calls=%fused_computation.135 | convolution fusion | flops 4081920 | bytes 1159168 | tf_op jit(solution)/shard_map/akbd,abke->abed/dot_general | solution.py:143
  221.6 6.4 %fusion.166 = f32[4,32,3,3]{3,2,1,0:T(4,128)S(1)} fusion(f32[4,32,3,64]{3,2,1,0:T(4,128)S(1)} %fusion.47, bf16[4,64,32,64]{3,2,1,0:T(8,128)(2,1)} %get-tuple-element.202, s32[4,32,3]{2,1,0:T(8,128)S(1)} %get-tuple-element.235, s32[4,32,3]{2,1,0:T(8,128)S(1)} %get-tuple-element.236), kind=kOutput, calls=%fused_computation.154 | convolution fusion | flops 4079616 | bytes 1154560 | tf_op jit(solution)/shard_map/akbd,abke->abed/dot_general | solution.py:142
  227.9 6.0 %fusion.101 = f32[4,32,3,3]{3,2,1,0:T(4,128)S(1)} fusion(f32[4,32,3,3]{3,2,1,0:T(4,128)S(1)} %fusion.166, f32[4,32,3,64]{3,2,1,0:T(4,128)S(1)} %fusion.45, bf16[4,64,32,64]{3,2,1,0:T(8,128)(2,1)} %get-tuple-element.202, s32[4,32,3]{2,1,0:T(8,128)S(1)} %get-tuple-element.235, s32[4,32,3]{2,1,0:T(8,128)S(1)} %get-tuple-element.236), kind=kOutput, calls=%fused_computation.129 | convolution fusion | flops 4081920 | bytes 1159168 | tf_op jit(solution)/shard_map/akbd,abke->abed/dot_general | solution.py:143
  236.3 6.2 %fusion.144 = f32[4,32,3,3]{3,2,1,0:T(4,128)S(1)} fusion(f32[4,32,3,64]{3,2,1,0:T(4,128)S(1)} %fusion.63, bf16[4,64,32,64]{3,2,1,0:T(8,128)(2,1)} %get-tuple-element.196, s32[4,32,3]{2,1,0:T(8,128)S(1)} %get-tuple-element.231, s32[4,32,3]{2,1,0:T(8,128)S(1)} %get-tuple-element.232), kind=kOutput, calls=%fused_computation.148 | convolution fusion | flops 4079616 | bytes 1154560 | tf_op jit(solution)/shard_map/akbd,abke->abed/dot_general | solution.py:142
  242.4 6.1 %fusion.103 = f32[4,32,3,3]{3,2,1,0:T(4,128)S(1)} fusion(f32[4,32,3,3]{3,2,1,0:T(4,128)S(1)} %fusion.144, f32[4,32,3,64]{3,2,1,0:T(4,128)S(1)} %fusion.61, bf16[4,64,32,64]{3,2,1,0:T(8,128)(2,1)} %get-tuple-element.196, s32[4,32,3]{2,1,0:T(8,128)S(1)} %get-tuple-element.231, s32[4,32,3]{2,1,0:T(8,128)S(1)} %get-tuple-element.232), kind=kOutput, calls=%fused_computation.133 | convolution fusion | flops 4081920 | bytes 1159168 | tf_op jit(solution)/shard_map/akbd,abke->abed/dot_general | solution.py:143
  251.0 59.7 %all-gather.1 = f32[128,1,1536]{2,1,0:T(1,128)S(1)} all-gather(f32[1,1,1536]{2,1,0:T(1,128)S(1)} %reshape.887), channel_id=2, replica_groups=mesh['gx'=4,'gy'=8,'sa'=4] {'gx','gy','sa'}, dimensions={0}, use_global_device_ids=true | all-gather | bytes 792576 | tf_op jit(solution)/shard_map/all_gather | solution.py:33
  313.3 4.2 %copy.101 = f32[4,4,2,8,4,4,32]{6,5,4,3,2,1,0:T(4,128)} copy(f32[4,4,2,8,4,4,32]{6,4,2,1,0,3,5:T(4,128)} %bitcast.356) | data formatting | bytes 1048576 | tf_op jit(solution)/shard_map/transpose | solution.py:177
  327.5 6.3 %while.15 = (s32[]{:T(128)}, f32[16,2,32,128]{3,2,1,0:T(8,128)S(1)}, f32[16,2,32,128]{3,2,1,0:T(8,128)S(1)}, f32[16,1,32,128]{3,2,0,1:T(8,128)S(1)}, f32[16,2,32...) while((s32[]{:T(128)}, ...), condition=%wide.region_2.3_spmd.clone, body=%wide.region_1.2_spmd.clone.sunk | while | flops 2498563 | bytes 4752639 | solution.py:222
  (152 shorter events, 104.2 us)
Async XLA Ops:
  16.5 103.7 %collective-permute-start = (bf16[256,2048]{1,0:T(8,128)(2,1)}, bf16[256,2048]{1,0:T(8,128)(2,1)}, u32[]{:S(2)}, u32[]{:S(2)}) collective-permute-start(bf16[256,2048]{1,0:T(8,128)(2,1)} %bitcast.11), channel_id=1, source_target_pairs={{0,1},{1,2},{2,3},{4,5},{5,6},{6,7},{8,9},{9,10},{10,11},{12,13},{... | collective-permute-start | bytes 3145736 | tf_op jit(solution)/shard_map/ppermute | solution.py:22
  21.9 5.7 %copy-start.13 = (bf16[1,256,2048]{2,1,0:T(8,128)(2,1)S(1)}, bf16[1,256,2048]{2,1,0:T(8,128)(2,1)}, u32[]{:S(2)}) copy-start(bf16[1,256,2048]{2,1,0:T(8,128)(2,1)} %get-tuple-element.208) | copy-start | bytes 3145732
  24.1 100.8 %collective-permute-start.1 = (bf16[256,2048]{1,0:T(8,128)(2,1)}, bf16[256,2048]{1,0:T(8,128)(2,1)}, u32[]{:S(2)}, u32[]{:S(2)}) collective-permute-start(bf16[256,2048]{1,0:T(8,128)(2,1)} %bitcast.14), channel_id=1, source_target_pairs={{0,1},{1,2},{2,3},{4,5},{5,6},{6,7},{8,9},{9,10},{10,11},{12,13},{... | collective-permute-start | bytes 3145736 | tf_op jit(solution)/shard_map/ppermute | solution.py:22
  28.1 2.6 copy-start.12
  31.2 3.5 %copy-start.11 = (bf16[1,256,2048]{2,1,0:T(8,128)(2,1)S(1)}, bf16[1,256,2048]{2,1,0:T(8,128)(2,1)}, u32[]{:S(2)}) copy-start(bf16[1,256,2048]{2,1,0:T(8,128)(2,1)} %get-tuple-element.205) | copy-start | bytes 3145732
  43.6 5.0 %copy-start.10 = (bf16[4096,128]{0,1:T(8,128)(2,1)S(1)}, bf16[4096,128]{0,1:T(8,128)(2,1)}, u32[]{:S(2)}) copy-start(bf16[4096,128]{0,1:T(8,128)(2,1)} %fusion.21) | copy-start | bytes 3145732
  56.2 1.9 copy-start.3
  68.4 5.4 %copy-start.9 = (bf16[4096,128]{0,1:T(8,128)(2,1)S(1)}, bf16[4096,128]{0,1:T(8,128)(2,1)}, u32[]{:S(2)}) copy-start(bf16[4096,128]{0,1:T(8,128)(2,1)} %fusion.23) | copy-start | bytes 3145732
  74.9 1.9 copy-start.8
  79.7 1.9 copy-start.4
  91.9 5.0 %copy-start.7 = (bf16[4096,128]{0,1:T(8,128)(2,1)S(1)}, bf16[4096,128]{0,1:T(8,128)(2,1)}, u32[]{:S(2)}) copy-start(bf16[4096,128]{0,1:T(8,128)(2,1)} %fusion.17) | copy-start | bytes 3145732
  98.0 1.9 copy-start.6
  102.8 1.9 copy-start.5
  114.9 4.9 %copy-start.16 = (s32[4,4,32]{2,1,0:T(4,128)S(1)}, s32[4,4,32]{2,1,0:T(4,128)}, u32[]{:S(2)}) copy-start(s32[4,4,32]{2,1,0:T(4,128)} %param.7) | copy-start | bytes 6148
  114.9 5.0 %copy-start.15 = (s32[4,2,4,32]{3,2,1,0:T(4,128)S(1)}, s32[4,2,4,32]{3,2,1,0:T(4,128)}, u32[]{:S(2)}) copy-start(s32[4,2,4,32]{3,2,1,0:T(4,128)} %param.6) | copy-start | bytes 12292
  162.1 7.1 %copy-start.2 = (f32[4,64,32,64]{3,2,1,0:T(8,128)S(1)}, f32[4,64,32,64]{3,2,1,0:T(8,128)}, u32[]{:S(2)}) copy-start(f32[4,64,32,64]{3,2,1,0:T(8,128)} %get-tuple-element.186) | copy-start | bytes 6291460
  165.4 3.8 %copy-start.1 = (f32[4,64,32,64]{3,2,1,0:T(8,128)S(1)}, f32[4,64,32,64]{3,2,1,0:T(8,128)}, u32[]{:S(2)}) copy-start(f32[4,64,32,64]{3,2,1,0:T(8,128)} %get-tuple-element.185) | copy-start | bytes 6291460
  173.8 3.4 %copy-start = (f32[4,64,32,64]{3,2,1,0:T(8,128)S(1)}, f32[4,64,32,64]{3,2,1,0:T(8,128)}, u32[]{:S(2)}) copy-start(f32[4,64,32,64]{3,2,1,0:T(8,128)} %get-tuple-element.204) | copy-start | bytes 6291460
  189.1 2.9 copy-start.19
  191.9 6.7 %copy-start.18 = (f32[4,32,3,64]{3,2,1,0:T(4,128)S(1)}, f32[4,32,3,64]{3,2,1,0:T(4,128)}, u32[]{:S(2)}) copy-start(f32[4,32,3,64]{3,2,1,0:T(4,128)} %fusion.53) | copy-start | bytes 294916
  198.7 8.4 %copy-start.17 = (f32[4,32,3,64]{3,2,1,0:T(4,128)S(1)}, f32[4,32,3,64]{3,2,1,0:T(4,128)}, u32[]{:S(2)}) copy-start(f32[4,32,3,64]{3,2,1,0:T(4,128)} %fusion.71) | copy-start | bytes 294916
  250.9 62.4 %copy-start.14 = (f32[4,2,4,32]{3,2,1,0:T(4,128)}, f32[4,2,4,32]{3,2,1,0:T(4,128)S(1)}, u32[]{:S(2)}) copy-start(f32[4,2,4,32]{3,2,1,0:T(4,128)S(1)} %pad_maximum_fusion) | copy-start | bytes 12292
where the time goes:
time: 340 us; the launch traced here: 335 us
  matrix products  121 us (36%)
  local copies, waits for them, and re-layouts  89 us (26%)
  blocking collectives  59.7 us (18%)
  other arithmetic  55 us (16%)
  starting transfers between devices  8.3 us (2%)
    all_gather x1, blocking collectives, gather_together(): lines, at, gathered = (lax.all_gather(ravelled, axis), 0, [])  59.7 us
    dot_general x16, matrix products, transform_rows(): jnp.einsum('kx,axc->akc', row_table, blocks, preferred_element_type=jnp.f...  36.2 us
    convert_element_type x1, other arithmetic, refine(): prod_real = (cross_real / scale).astype(jnp.bfloat16)  27.3 us
    dot_general x4, matrix products, refine(): jnp.einsum('akbd,abke->abed', half_real, row_cos, preferred_element_type=...  25.5 us
    dot_general x4, matrix products, refine(): jnp.einsum('akbd,abke->abed', half_imag, row_sin, preferred_element_type=...  24.2 us
    convert_element_type x4, local copies, waits for them, and re-layouts, refine(): now_imag = current[1].astype(jnp.float32).reshape(layout)  20.2 us
    convert_element_type x4, local copies, waits for them, and re-layouts, refine(): now_real = current[0].astype(jnp.float32).reshape(layout)  19.4 us
    dot_general x4, matrix products, refine(): jnp.einsum('akbj,abjd->akbd', prod_imag, col_sin, preferred_element_type=...  12.5 us
  transfers between devices with their start and end apart: 2, of which 0 were waited for; matrix products, arithmetic and copies ran while one was open for 30% of the time, Pallas kernels for 0%

commit v1 on v0

v1 whole, which is shorter than its diff:
```python
import functools
import math

import jax
import jax.numpy as jnp
import numpy as np
from jax import lax
from jax.experimental import pallas as pl
from jax.experimental.pallas import tpu as pltpu
from jax.sharding import PartitionSpec as P

PATCH = 64
RELAX = 8
HALF = PATCH // 2 + 1
PR = 4
KROWS = 144
LANES = 256
REACH = 3
SPAN = 2 * REACH + 1
AXES = ("gx", "gy", "sa")

spring_plane = 0.5
spring_stack = 1.0
step_size = 0.2
damping = 0.6
whiten_floor = 1024.0

BF = jnp.bfloat16
F32 = jnp.float32


def wave_tables():
    angles = np.arange(PATCH, dtype=np.float32) * np.float32(2.0 * math.pi / PATCH)
    cosine = np.cos(angles).astype(BF).astype(np.float32)
    sine = np.sin(angles).astype(BF).astype(np.float32)
    return cosine, sine


def row_matrix():
    cosine, sine = wave_tables()
    out = np.zeros((2, KROWS, PR * PATCH), np.float32)
    phase = np.arange(HALF)[:, None] * np.arange(PATCH)[None, :] % PATCH
    for pr in range(PR):
        rows = slice(pr * HALF, (pr + 1) * HALF)
        cols = slice(pr * PATCH, (pr + 1) * PATCH)
        out[0, rows, cols] = cosine[phase]
        out[1, rows, cols] = -sine[phase]
    return out.reshape(2 * KROWS, PR * PATCH).astype(BF)


def col_matrix():
    cosine, sine = wave_tables()
    phase = np.arange(PATCH)[:, None] * np.arange(PATCH)[None, :] % PATCH
    out = np.zeros((2, 2, PATCH, 2, 2, PATCH), np.float32)
    for p in range(2):
        out[0, p, :, 0, p] = cosine[phase]
        out[1, p, :, 0, p] = sine[phase]
        out[0, p, :, 1, p] = -sine[phase]
        out[1, p, :, 1, p] = cosine[phase]
    return out.reshape(256, 256).astype(BF)


def first_matrix(flip):
    cosine, sine = wave_tables()
    out = np.zeros((2, 32, 2, KROWS), np.float32)
    k1 = np.arange(HALF)
    weight = np.where((k1 == 0) | (k1 == PATCH // 2), 1.0, 2.0)
    for p1 in range(SPAN):
        phase = k1 * (p1 - REACH) % PATCH
        for pr in range(PR):
            sign = -1.0 if flip and pr >= PR // 2 else 1.0
            row, cols = p1 * PR + pr, slice(pr * HALF, (pr + 1) * HALF)
            out[0, row, 0, cols] = weight * cosine[phase]
            out[0, row, 1, cols] = -sign * weight * sine[phase]
            out[1, row, 0, cols] = weight * sine[phase]
            out[1, row, 1, cols] = sign * weight * cosine[phase]
    return out.reshape(64, 2 * KROWS).astype(BF)


def second_matrix(blocks):
    cosine, sine = wave_tables()
    out = np.zeros((blocks, 2, 4, PATCH, 8, blocks, 4), np.float32)
    k2 = np.arange(PATCH)
    for p2 in range(SPAN):
        phase = k2 * (p2 - REACH) % PATCH
        for j in range(blocks):
            for p in range(4):
                out[j, 0, p, :, p2, j, p] = cosine[phase]
                out[j, 1, p, :, p2, j, p] = -sine[phase]
    return out.reshape(blocks, 512, 8 * blocks * 4).astype(BF)


def spectrum(strips, rows_ref, cols_ref):
    half = jnp.dot(rows_ref[...], strips, preferred_element_type=F32).astype(BF)
    out = []
    for b in range(LANES // 128):
        lanes = slice(b * 128, (b + 1) * 128)
        both = jnp.concatenate([half[:KROWS, lanes], half[KROWS:, lanes]], axis=1)
        spec = jnp.dot(both, cols_ref[...], preferred_element_type=F32)
        out.append((spec[:, :128], spec[:, 128:]))
    return out


def whiten(now, old):
    real, imag = [], []
    for (now_real, now_imag), (old_real, old_imag) in zip(now, old):
        cross_real = now_real * old_real + now_imag * old_imag
        cross_imag = now_imag * old_real - now_real * old_imag
        power = cross_real * cross_real + cross_imag * cross_imag
        inverse = lax.rsqrt(power + whiten_floor * whiten_floor)
        real.append((cross_real * inverse).astype(BF))
        imag.append((cross_imag * inverse).astype(BF))
    return jnp.concatenate(
        [jnp.concatenate(real, axis=1), jnp.concatenate(imag, axis=1)], axis=0
    )


def first_sum(table_ref, prod):
    both = jnp.dot(table_ref[...], prod, preferred_element_type=F32)
    return jnp.concatenate([both[:32], both[32:]], axis=1)


def inner_kernel(px_ref, rows_ref, cols_ref, first_ref, second_ref, corr_ref, mix_ref):
    count = px_ref.shape[0]
    old, sums, edge = None, [], None
    for s in range(count):
        now = spectrum(px_ref[s], rows_ref, cols_ref)
        if s == 0:
            edge = now
        else:
            sums.append(first_sum(first_ref, whiten(now, old)).astype(BF))
        old = now
    low = lax.broadcasted_iota(jnp.int32, (KROWS, 128), 0) < 2 * HALF
    for b in range(LANES // 128):
        for part in range(2):
            mix_ref[part * KROWS : (part + 1) * KROWS, b * 128 : (b + 1) * 128] = jnp.where(
                low, edge[b][part], old[b][part]
            ).astype(BF)
    term = jnp.dot(jnp.concatenate(sums, axis=0), second_ref[0], preferred_element_type=F32)

    @pl.when(pl.program_id(0) == 0)
    def _():
        corr_ref[...] = term

    @pl.when(pl.program_id(0) > 0)
    def _():
        corr_ref[...] += term


def pick(pieces, offset):
    value = pieces[0]
    for i in range(1, 5):
        value = jnp.where(offset == i - 2, pieces[i], value)
    return value


def peak_step(low, center, high):
    bend = jnp.maximum(jnp.abs(low - 2.0 * center + high), 1.0)
    return (low - high) / (2.0 * bend)


def edge_kernel(
    up_ref, down_ref, extra_ref, mix_ref, rows_ref, cols_ref, first_ref, second_ref,
    inner_ref, offs_ref, valid_ref, flow_ref, load_ref, corr, picked, offs,
):
    sa = lax.axis_index("sa")
    step = pl.program_id(0)
    strips = jnp.concatenate([up_ref[...], down_ref[...]], axis=0)
    there = spectrum(strips, rows_ref, cols_ref)
    here = []
    for b in range(LANES // 128):
        lanes = slice(b * 128, (b + 1) * 128)
        here.append((mix_ref[:KROWS, lanes].astype(F32), mix_ref[KROWS:, lanes].astype(F32)))
    sums = first_sum(first_ref, whiten(here, there))
    pr = lax.broadcasted_iota(jnp.int32, sums.shape, 0) % PR
    dropped = ((sa == 0) & (pr < 2)) | ((sa == lax.axis_size("sa") - 1) & (pr >= 2))
    sums = jnp.where(dropped, 0.0, sums).astype(BF)
    term = jnp.dot(sums, second_ref[0], preferred_element_type=F32)

    @pl.when(step == 0)
    def _():
        corr[...] = term

    @pl.when(step > 0)
    def _():
        corr[...] += term

    @pl.when(step == pl.num_programs(0) - 1)
    def _():
        for p1 in range(SPAN):
            rows = slice(p1 * PR, (p1 + 1) * PR)
            picked[p1, 0:PR] = corr[rows]
            for s in range(3):
                picked[p1, (s + 1) * PR : (s + 2) * PR] = inner_ref[
                    s * 32 + p1 * PR : s * 32 + (p1 + 1) * PR
                ]
        extra = extra_ref[...].astype(F32).astype(jnp.int32)
        for c in range(2):
            for s in range(4):
                offs[c, s * PR : (s + 1) * PR, :] = offs_ref[s, c]
            offs[c, 2:4, :] = extra[c * 2 : c * 2 + 2, :32]
        row_off, col_off = offs[0], offs[1]
        wide = jnp.concatenate([row_off] * 8, axis=1)
        layers = [picked[p1] * (1.0 / PATCH) for p1 in range(SPAN)]
        low, mid, high = [pick(layers[d : d + 5], wide) for d in range(3)]

        def cut(layer, d):
            return pick([layer[:, (d + i) * 32 : (d + i + 1) * 32] for i in range(5)], col_off)

        center = cut(mid, 1)
        flows = (
            row_off.astype(F32) + peak_step(cut(low, 1), center, cut(high, 1)),
            col_off.astype(F32) + peak_step(cut(mid, 0), center, cut(mid, 2)),
        )
        load_ref[...] = jnp.zeros_like(load_ref)
        for s in range(4):
            lanes = slice(s * 32, (s + 1) * 32)
            for c in range(2):
                piece = flows[c][s * PR : (s + 1) * PR]
                flow_ref[c * PR : (c + 1) * PR, lanes] = piece
                load_ref[c * PR : (c + 1) * PR, lanes] = piece
            load_ref[2 * PR : 3 * PR, lanes] = valid_ref[s].astype(F32)


def relax_kernel(got_ref, own_ref, flow_out, mesh_out, raw, flow, coef, state, speed):
    gx, gy, sa = [lax.axis_index(a) for a in AXES]
    nx, ny, ns = [lax.axis_size(a) for a in AXES]
    lane = lax.broadcasted_iota(jnp.int32, (24, 128), 1)
    row = lax.broadcasted_iota(jnp.int32, (24, 128), 0)
    col = lane % 32
    raw[...] = jnp.zeros_like(raw)
    near = lax.broadcasted_iota(jnp.int32, (16, 128), 1) % 32 < 16
    left, right = jnp.maximum(gx - 1, 0), jnp.minimum(gx + 1, nx - 1)
    for g in range(5):
        gyc = jnp.clip(gy + g - 2, 0, ny - 1)
        for k in range(ns):
            mid = got_ref[(gx * ny + gyc) * ns + k].astype(F32)
            low = got_ref[(left * ny + gyc) * ns + k].astype(F32)
            high = got_ref[(right * ny + gyc) * ns + k].astype(F32)
            side = jnp.where(near, high, low)
            for c in range(3):
                raw[c, 0, k, g * PR : (g + 1) * PR, :] = mid[c * PR : (c + 1) * PR]
                raw[c, 1, k, g * PR : (g + 1) * PR, :] = side[c * PR : (c + 1) * PR]

    place = gy * PR - 2 * PR + row
    rows_ok = (place >= 0) & (place < ny * PR) & (row < 5 * PR)
    inside, degree = [], []
    for h in range(2):
        if h == 0:
            column = gx * 32 + col
        else:
            column = jnp.where(col < 16, (gx + 1) * 32 + col, (gx - 1) * 32 + col)
        ok = rows_ok & (column >= 0) & (column < nx * 32)
        inside.append(jnp.where(ok, 1.0, 0.0))
        edges = jnp.where(place == 0, 1.0, 0.0) + jnp.where(place == ny * PR - 1, 1.0, 0.0)
        edges += jnp.where(column == 0, 1.0, 0.0) + jnp.where(column == nx * 32 - 1, 1.0, 0.0)
        degree.append(4.0 - edges)

    swapped = (row % PR >= 2) & (lane < 32)
    for c in range(2):
        for h in range(2):
            carry = jnp.zeros((24, 128), F32)
            for k in range(ns):
                f = jnp.where(swapped, raw[c, h, (k + ns - 1) % ns], raw[c, h, k]) * inside[h]
                flow[c, h, k] = f
                x = f + jnp.where(lane >= 32, pltpu.roll(f, 32, 1), 0.0)
                x = x + jnp.where(lane >= 64, pltpu.roll(x, 64, 1), 0.0)
                state[0, c, h, k] = x + carry
                last = jnp.where(lane >= 96, x, 0.0)
                last = last + pltpu.roll(last, 64, 1)
                carry = carry + last + pltpu.roll(last, 32, 1)
                speed[c, h, k] = jnp.zeros((24, 128), F32)

    def above(get, k):
        up = get(k + 1) if k + 1 < ns else jnp.zeros((24, 128), F32)
        return pltpu.roll(jnp.where(lane < 32, up, get(k)), 96, 1)

    def below(get, k):
        down = get(k - 1) if k > 0 else jnp.zeros((24, 128), F32)
        return pltpu.roll(jnp.where(lane >= 96, down, get(k)), 32, 1)

    for h in range(2):
        for k in range(ns):
            w = raw[2, h, k] * inside[h] * (step_size * spring_stack)
            w_next = above(lambda i: raw[2, h, i], k) * inside[h] * (step_size * spring_stack)
            coef[0, h, k] = w
            coef[1, h, k] = w_next
            coef[2, h, k] = degree[h] * inside[h] * (step_size * spring_plane) + w + w_next
            for c in range(2):
                coef[3 + c, h, k] = w * flow[c, h, k] - w_next * above(lambda i: flow[c, h, i], k)

    plane = [inside[h] * (step_size * spring_plane) for h in range(2)]

    def advance(src, dst):
        for c in range(2):
            for h in range(2):
                for k in range(ns):
                    m, o = state[src, c, h, k], state[src, c, 1 - h, k]
                    get = lambda i: state[src, c, h, i]
                    around = jnp.where(col == 0, pltpu.roll(o, 97, 1), pltpu.roll(m, 1, 1))
                    around += jnp.where(col == 31, pltpu.roll(o, 31, 1), pltpu.roll(m, 127, 1))
                    around += pltpu.roll(m, 1, 0) + pltpu.roll(m, 23, 0)
                    v = damping * speed[c, h, k] - coef[2, h, k] * m + plane[h] * around
                    v += coef[0, h, k] * below(get, k) + coef[1, h, k] * above(get, k)
                    v += coef[3 + c, h, k]
                    speed[c, h, k] = v
                    state[dst, c, h, k] = m + v

    def two(i, unused):
        advance(0, 1)
        advance(1, 0)
        return unused

    lax.fori_loop(0, RELAX // 2, two, 0)
    mine = slice(2 * PR, 3 * PR)
    first = (lax.broadcasted_iota(jnp.int32, (PR, 128), 0) >= 2) & (
        lax.broadcasted_iota(jnp.int32, (PR, 128), 1) < 32
    )
    for c in range(2):
        m = state[0, c, 0, sa][mine]
        f = flow[c, 0, sa][mine]
        f = jnp.where(first, f, own_ref[c * PR : (c + 1) * PR])
        for s in range(4):
            lanes = slice(s * 32, (s + 1) * 32)
            mesh_out[s, c] = m[:, lanes]
            flow_out[s, c] = f[:, lanes]


def per_device(pixels, peak_offsets, validity):
    count, height, breadth = pixels.shape
    blocks = breadth // LANES
    size = lax.axis_size("sa")
    half = height // 2
    extra = peak_offsets[0, :, 2:, :].reshape(4, 32).astype(BF)
    extra = jnp.pad(extra, ((0, 12), (0, breadth - 32)))
    down = jnp.concatenate([pixels[0, half:], extra], axis=0)
    up = pixels[count - 1, :half]
    up = lax.ppermute(up, "sa", [(i, (i + 1) % size) for i in range(size)])
    down = lax.ppermute(down, "sa", [(i, (i - 1) % size) for i in range(size)])

    rows = jnp.asarray(row_matrix())
    cols = jnp.asarray(col_matrix())
    second = jnp.asarray(second_matrix(blocks))
    whole = lambda shape: pl.BlockSpec(shape, lambda j: (0,) * len(shape))
    table_specs = [
        whole((2 * KROWS, PR * PATCH)),
        whole((256, 256)),
        whole((64, 2 * KROWS)),
        pl.BlockSpec((1, 512, 8 * blocks * 4), lambda j: (j, 0, 0)),
    ]
    inner, mix = pl.pallas_call(
        inner_kernel,
        grid=(blocks,),
        in_specs=[pl.BlockSpec((count, height, LANES), lambda j: (0, 0, j))] + table_specs,
        out_specs=[
            whole((96, 256)),
            pl.BlockSpec((2 * KROWS, LANES), lambda j: (0, j)),
        ],
        out_shape=[
            jax.ShapeDtypeStruct((96, 256), F32),
            jax.ShapeDtypeStruct((2 * KROWS, breadth), BF),
        ],
        compiler_params=pltpu.CompilerParams(dimension_semantics=("arbitrary",)),
        cost_estimate=pl.CostEstimate(
            flops=8 * 10**9, bytes_accessed=8 * 2**20, transcendentals=10**6
        ),
        name="inner",
    )(pixels, rows, cols, jnp.asarray(first_matrix(False)), second)

    own, load = pl.pallas_call(
        edge_kernel,
        grid=(blocks,),
        in_specs=[
            pl.BlockSpec((half, LANES), lambda j: (0, j)),
            pl.BlockSpec((half, LANES), lambda j: (0, j)),
            pl.BlockSpec((16, 128), lambda j: (half // 16, 0)),
            pl.BlockSpec((2 * KROWS, LANES), lambda j: (0, j)),
        ]
        + table_specs
        + [whole((96, 256)), whole((count, 2, PR, 32)), whole((count, PR, 32))],
        out_specs=[whole((8, 128)), whole((16, 128))],
        out_shape=[
            jax.ShapeDtypeStruct((8, 128), F32),
            jax.ShapeDtypeStruct((16, 128), F32),
        ],
        scratch_shapes=[
            pltpu.VMEM((32, 256), F32),
            pltpu.VMEM((SPAN, 16, 256), F32),
            pltpu.VMEM((2, 16, 32), jnp.int32),
        ],
        compiler_params=pltpu.CompilerParams(dimension_semantics=("arbitrary",)),
        name="edge",
    )(
        up, down, down, mix, rows, cols, jnp.asarray(first_matrix(True)), second,
        inner, peak_offsets, validity,
    )

    devices = lax.axis_size(AXES)
    sent = jnp.broadcast_to(load.astype(BF)[None], (devices, 16, 128))
    got = lax.all_to_all(sent, AXES, 0, 0)

    field = (count, 2, PR, 32)
    vmem = lambda: pl.BlockSpec(memory_space=pltpu.VMEM)
    stack = (2, size, 24, 128)
    return pl.pallas_call(
        relax_kernel,
        in_specs=[vmem(), vmem()],
        out_specs=[vmem(), vmem()],
        out_shape=[jax.ShapeDtypeStruct(field, F32)] * 2,
        scratch_shapes=[
            pltpu.VMEM((3,) + stack, F32),
            pltpu.VMEM((2,) + stack, F32),
            pltpu.VMEM((5,) + stack, F32),
            pltpu.VMEM((2, 2) + stack, F32),
            pltpu.VMEM((2,) + stack, F32),
        ],
        name="relax",
    )(got, own)


def solution(mesh):
    return jax.shard_map(
        per_device,
        mesh=mesh,
        in_specs=(P("sa", "gy", "gx"), P("sa", None, "gy", "gx"), P("sa", "gy", "gx")),
        out_specs=(P("sa", None, "gy", "gx"), P("sa", None, "gy", "gx")),
        check_vma=False,
    )
```

time: 340 us -> 60.5 us (0.18); the launches traced: 335 us -> 60.1 us
  matrix products: 121 us -> 0 us
  local copies, waits for them, and re-layouts: 89 us -> 2.36 us
  other arithmetic: 55 us -> 1.44 us
  blocking collectives: 59.7 us -> 24.2 us
  Pallas kernels: 0 us -> 27.9 us
  starting transfers between devices: 8.3 us -> 3.45 us
    dot_general x40 -> x0, matrix products: 121 us -> none  [the longest x16 36.2 us: transform_rows(): jnp.einsum('kx,axc->akc', row_table, blocks, preferred_element_type=jnp.f...]
    all_gather x1 -> x0, blocking collectives: 59.7 us -> none  [gather_together(): lines, at, gathered = (lax.all_gather(ravelled, axis), 0, [])]
    convert_element_type x16 -> x0, local copies, waits for them, and re-layouts: 48.2 us -> none  [the longest x4 20.2 us: refine(): now_imag = current[1].astype(jnp.float32).reshape(layout)]
    convert_element_type x7 -> x1, other arithmetic: 38.4 us -> 0.7 us  [per_device(): sent = jnp.broadcast_to(load.astype(BF)[None], (devices, 16, 128))]
    pallas_call x0 -> x3, Pallas kernels: none -> 27.9 us  [the longest x1 14 us: per_device(): pl.pallas_call(inner_kernel, grid=(blocks,), in_specs=[pl.BlockSpec((coun...]
    all_to_all x0 -> x1, blocking collectives: none -> 24.2 us  [per_device(): got = lax.all_to_all(sent, AXES, 0, 0)]
    reshape x12 -> x0, local copies, waits for them, and re-layouts: 22.5 us -> none  [the longest x4 5.04 us: spectra(): col_imag = jnp.dot(flat, sine_cols, preferred_element_type=jnp.float32).a...]
    slice x4 -> x0, other arithmetic: 9.04 us -> none  [subpixel(): row_low = correlation[..., 0, 1]]
  transfers between devices with their start and end apart: 2 -> 2, of which waited for: 0 -> 0; matrix products, arithmetic and copies ran while one was open for 30% -> 1% of each run, Pallas kernels for 0% -> 23%
where the time goes in v1:
time: 60.5 us; the launch traced here: 60.1 us
  Pallas kernels  27.9 us (46%)
  blocking collectives  24.2 us (40%)
  starting transfers between devices  3.45 us (6%)
  local copies, waits for them, and re-layouts  2.36 us (4%)
  other arithmetic  1.44 us (2%)
  between operations  0.67 us (1%)
    all_to_all x1, blocking collectives, per_device(): got = lax.all_to_all(sent, AXES, 0, 0)  24.2 us
    pallas_call x1, Pallas kernels, per_device(): pl.pallas_call(inner_kernel, grid=(blocks,), in_specs=[pl.BlockSpec((coun...  14 us
    pallas_call x1, Pallas kernels, per_device(): pl.pallas_call(edge_kernel, grid=(blocks,), in_specs=[pl.BlockSpec((half,...  8.97 us
    pallas_call x1, Pallas kernels, per_device(): pl.pallas_call(relax_kernel, in_specs=[vmem(), vmem()], out_specs=[vmem()...  4.97 us
    ppermute x1, starting transfers between devices, per_device(): up = lax.ppermute(up, 'sa', [(i, (i + 1) % size) for i in range(size)])  2.1 us
    ppermute x1, starting transfers between devices, per_device(): down = lax.ppermute(down, 'sa', [(i, (i - 1) % size) for i in range(size)])  1.35 us
    squeeze x1, local copies, waits for them, and re-layouts, per_device(): down = jnp.concatenate([pixels[0, half:], extra], axis=0)  1.27 us
  transfers between devices with their start and end apart: 2, of which 0 were waited for; matrix products, arithmetic and copies ran while one was open for 1% of the time, Pallas kernels for 23%

profile of v1, /device:TPU:1, one launch (start us, length us, event | category | flops | bytes accessed | tf_op | source)
XLA Modules:
  0.0 60.1 jit_solution(14695506550913205111)
XLA Ops:
  0.6 1.3 %slice_bitcast_fusion = (bf16[128,2048]{1,0:T(8,128)(2,1)S(1)}, bf16[128,2048]{1,0:T(8,128)(2,1)S(1)}) fusion(bf16[4,256,2048]{2,1,0:T(8,128)(2,1)} %px_ref.1), kind=kLoop, calls=%fused_computation.3 | loop fusion | bytes 2097152 | tf_op jit(solution)/shard_map/squeeze | solution.py:336
  1.9 2.1 %collective-permute-start = (bf16[128,2048]{1,0:T(8,128)(2,1)S(1)}, bf16[128,2048]{1,0:T(8,128)(2,1)S(1)}, u32[]{:S(2)}, u32[]{:S(2)}) collective-permute-start(bf16[128,2048]{1,0:T(8,128)(2,1)S(1)} %get-tuple-element.11), channel_id=1, source_target_pairs={{0,1},{1,2},{2,3},{3,0},{4,5},{5,6},{6,7},{7,4},{8,9},{9,10},{10,1... | collective-permute-start | bytes 1572872 | tf_op jit(solution)/shard_map/ppermute | solution.py:338
  4.0 0.7 %slice_convert_fusion = bf16[1,2,2,32]{3,2,1,0:T(2,128)(2,1)S(1)} fusion(s32[4,2,4,32]{3,2,1,0:T(4,128)} %offs_ref.1), kind=kLoop, calls=%fused_computation.5 | loop fusion | flops 128 | bytes 768 | tf_op jit(solution)/shard_map/convert
  4.7 0.1 fusion.1
  4.8 1.4 %collective-permute-start.1 = (bf16[144,2048]{1,0:T(8,128)(2,1)S(1)}, bf16[144,2048]{1,0:T(8,128)(2,1)S(1)}, u32[]{:S(2)}, u32[]{:S(2)}) collective-permute-start(bf16[144,2048]{1,0:T(8,128)(2,1)S(1)} %fusion.1), channel_id=1, source_target_pairs={{0,3},{1,0},{2,1},{3,2},{4,7},{5,4},{6,5},{7,6},{8,11},{9,8},{10,9... | collective-permute-start | bytes 1769480 | tf_op jit(solution)/shard_map/ppermute | solution.py:339
  6.1 14.0 %inner.1 = (f32[96,256]{1,0:T(8,128)}, bf16[288,2048]{1,0:T(8,128)(2,1)}) custom-call(bf16[4,256,2048]{2,1,0:T(8,128)(2,1)} %px_ref.1, bf16[288,256]{1,0:T(8,128)(2,1)} %constant.13.clone.rows_ref, bf16[256,256]{1,0:T(8,128)(2,1)} %constant.14.clone.cols_ref, bf16[64,288]{1,0:T(8,128)(2,1)} %constant.16.clone.first_ref, ...), custom_call_target="tpu_custom_call" | custom-call | flops 8000000000 | bytes 8388608 | tf_op jit(solution)/shard_map/inner/pallas_call | solution.py:351
  20.1 0.0 collective-permute-done.up_ref
  20.1 0.0 copy-start.1
  20.1 0.0 collective-permute-done.1.down_ref.extra_ref
  20.1 0.0 copy-start
  20.1 0.8 %copy-done.1 = bf16[128,2048]{1,0:T(8,128)(2,1)} copy-done((bf16[128,2048]{1,0:T(8,128)(2,1)}, bf16[128,2048]{1,0:T(8,128)(2,1)S(1)}, u32[]{:S(2)}) %copy-start.1) | copy-done | bytes 524312
  20.9 0.2 copy-done
  21.1 9.0 %edge.1 = (f32[8,128]{1,0:T(8,128)}, f32[16,128]{1,0:T(8,128)}) custom-call(bf16[128,2048]{1,0:T(8,128)(2,1)} %copy-done.1, bf16[144,2048]{1,0:T(8,128)(2,1)} %copy-done, bf16[144,2048]{1,0:T(8,128)(2,1)} %copy-done, bf16[288,2048]{1,0:T(8,128)(2,1)} %get-tuple-element.6.mix_ref, bf16[288,256]{1,0:T(8,128)(2,1)} %constant.13.clone.rows_ref, ...), custom_call_target="tpu_custom_call" | custom-call | tf_op jit(solution)/shard_map/edge/pallas_call | solution.py:370
  30.1 0.7 %convert_element_type.10 = bf16[16,128]{1,0:T(8,128)(2,1)S(1)} convert(f32[16,128]{1,0:T(8,128)} %get-tuple-element.8) | non-fusion elementwise | flops 2048 | bytes 12288 | tf_op jit(solution)/shard_map/convert_element_type | solution.py:399
  30.8 0.1 broadcast_in_dim.2
  30.9 24.2 %all_to_all.5.got_ref = bf16[128,16,128]{2,1,0:T(8,128)(2,1)} all-to-all(bf16[128,16,128]{2,1,0:T(8,128)(2,1)S(1)} %broadcast_in_dim.2), channel_id=1, replica_groups=mesh['gx'=4,'gy'=8,'sa'=4] {'gx','gy','sa'}, dimensions={0} | all-to-all | bytes 1048576 | tf_op jit(solution)/shard_map/all_to_all | solution.py:400
  55.1 5.0 %relax.1 = (f32[4,2,4,32]{3,2,1,0:T(4,128)}, f32[4,2,4,32]{3,2,1,0:T(4,128)}) custom-call(bf16[128,16,128]{2,1,0:T(8,128)(2,1)} %all_to_all.5.got_ref, f32[8,128]{1,0:T(8,128)} %get-tuple-element.9.own_ref), custom_call_target="tpu_custom_call" | custom-call | tf_op jit(solution)/shard_map/relax/pallas_call | solution.py:405
Async XLA Ops:
  1.9 18.2 %collective-permute-start = (bf16[128,2048]{1,0:T(8,128)(2,1)S(1)}, bf16[128,2048]{1,0:T(8,128)(2,1)S(1)}, u32[]{:S(2)}, u32[]{:S(2)}) collective-permute-start(bf16[128,2048]{1,0:T(8,128)(2,1)S(1)} %get-tuple-element.11), channel_id=1, source_target_pairs={{0,1},{1,2},{2,3},{3,0},{4,5},{5,6},{6,7},{7,4},{8,9},{9,10},{10,1... | collective-permute-start | bytes 1572872 | tf_op jit(solution)/shard_map/ppermute | solution.py:338
  4.8 15.3 %collective-permute-start.1 = (bf16[144,2048]{1,0:T(8,128)(2,1)S(1)}, bf16[144,2048]{1,0:T(8,128)(2,1)S(1)}, u32[]{:S(2)}, u32[]{:S(2)}) collective-permute-start(bf16[144,2048]{1,0:T(8,128)(2,1)S(1)} %fusion.1), channel_id=1, source_target_pairs={{0,3},{1,0},{2,1},{3,2},{4,7},{5,4},{6,5},{7,6},{8,11},{9,8},{10,9... | collective-permute-start | bytes 1769480 | tf_op jit(solution)/shard_map/ppermute | solution.py:339
  20.1 0.8 %copy-start.1 = (bf16[128,2048]{1,0:T(8,128)(2,1)}, bf16[128,2048]{1,0:T(8,128)(2,1)S(1)}, u32[]{:S(2)}) copy-start(bf16[128,2048]{1,0:T(8,128)(2,1)S(1)} %collective-permute-done.up_ref) | copy-start | bytes 1572868
  20.1 1.0 %copy-start = (bf16[144,2048]{1,0:T(8,128)(2,1)}, bf16[144,2048]{1,0:T(8,128)(2,1)S(1)}, u32[]{:S(2)}) copy-start(bf16[144,2048]{1,0:T(8,128)(2,1)S(1)} %collective-permute-done.1.down_ref.extra_ref) | copy-start | bytes 1769476

commit v2 on v1

v2 whole, which is shorter than its diff:
```python
import math

import jax
import jax.numpy as jnp
import numpy as np
from jax import lax
from jax.experimental import pallas as pl
from jax.experimental.pallas import tpu as pltpu
from jax.sharding import PartitionSpec as P


PATCH = 64
RELAX = 8
HALF = PATCH // 2 + 1
PR = 4
KROWS = 144
LANES = 256
REACH = 3
SPAN = 2 * REACH + 1
GRANT = 20 * 2**20
AXES = ("gx", "gy", "sa")

spring_plane = 0.5
spring_stack = 1.0
step_size = 0.2
damping = 0.6
whiten_floor = 1024.0

BF = jnp.bfloat16
F32 = jnp.float32


def wave_tables():
    angles = np.arange(PATCH, dtype=np.float32) * np.float32(2.0 * math.pi / PATCH)
    cosine = np.cos(angles).astype(BF).astype(np.float32)
    sine = np.sin(angles).astype(BF).astype(np.float32)
    return cosine, sine


def row_matrix():
    cosine, sine = wave_tables()
    out = np.zeros((2, KROWS, PR * PATCH), np.float32)
    phase = np.arange(HALF)[:, None] * np.arange(PATCH)[None, :] % PATCH
    for pr in range(PR):
        rows = slice(pr * HALF, (pr + 1) * HALF)
        cols = slice(pr * PATCH, (pr + 1) * PATCH)
        out[0, rows, cols] = cosine[phase]
        out[1, rows, cols] = -sine[phase]
    return out.reshape(2 * KROWS, PR * PATCH).astype(BF)


def col_matrix():
    cosine, sine = wave_tables()
    phase = np.arange(PATCH)[:, None] * np.arange(PATCH)[None, :] % PATCH
    out = np.zeros((2, 2, PATCH, 2, 2, PATCH), np.float32)
    for p in range(2):
        out[0, p, :, 0, p] = cosine[phase]
        out[1, p, :, 0, p] = sine[phase]
        out[0, p, :, 1, p] = -sine[phase]
        out[1, p, :, 1, p] = cosine[phase]
    return out.reshape(256, 256).astype(BF)


def first_matrix(flip):
    cosine, sine = wave_tables()
    out = np.zeros((2, 32, 2, KROWS), np.float32)
    k1 = np.arange(HALF)
    weight = np.where((k1 == 0) | (k1 == PATCH // 2), 1.0, 2.0)
    for p1 in range(SPAN):
        phase = k1 * (p1 - REACH) % PATCH
        for pr in range(PR):
            sign = -1.0 if flip and pr >= PR // 2 else 1.0
            row, cols = p1 * PR + pr, slice(pr * HALF, (pr + 1) * HALF)
            out[0, row, 0, cols] = weight * cosine[phase]
            out[0, row, 1, cols] = -sign * weight * sine[phase]
            out[1, row, 0, cols] = weight * sine[phase]
            out[1, row, 1, cols] = sign * weight * cosine[phase]
    return out.reshape(64, 2 * KROWS).astype(BF)


def second_matrix(blocks):
    cosine, sine = wave_tables()
    out = np.zeros((blocks, 2, 4, PATCH, 8, blocks, 4), np.float32)
    k2 = np.arange(PATCH)
    for p2 in range(SPAN):
        phase = k2 * (p2 - REACH) % PATCH
        for j in range(blocks):
            for p in range(4):
                out[j, 0, p, :, p2, j, p] = cosine[phase]
                out[j, 1, p, :, p2, j, p] = -sine[phase]
    return out.reshape(blocks, 512, 8 * blocks * 4).astype(BF)


def whiten(now, old):
    real, imag = [], []
    for (now_real, now_imag), (old_real, old_imag) in zip(now, old):
        cross_real = now_real * old_real + now_imag * old_imag
        cross_imag = now_imag * old_real - now_real * old_imag
        power = cross_real * cross_real + cross_imag * cross_imag
        inverse = lax.rsqrt(power + whiten_floor * whiten_floor)
        real.append((cross_real * inverse).astype(BF))
        imag.append((cross_imag * inverse).astype(BF))
    return jnp.concatenate(
        [jnp.concatenate(real, axis=1), jnp.concatenate(imag, axis=1)], axis=0
    )


def first_sum(table_ref, prod):
    both = jnp.dot(table_ref[...], prod, preferred_element_type=F32)
    return jnp.concatenate([both[:32], both[32:]], axis=1)


def send_kernel(px_ref, offs_ref, up_ref, down_ref, offs, low, sems, offs_sem):
    count, height, breadth = px_ref.shape
    half = height // 2
    copies = []
    for b in range(breadth // 128):
        rows, lanes = pl.ds(b * half, half), pl.ds(b * 128, 128)
        copies += [
            pltpu.make_async_copy(
                px_ref.at[count - 1, pl.ds(0, half), lanes], up_ref.at[rows], sems.at[0, b]
            ),
            pltpu.make_async_copy(
                px_ref.at[0, pl.ds(half, half), lanes], down_ref.at[rows], sems.at[1, b]
            ),
        ]
    first = pltpu.make_async_copy(offs_ref.at[0], offs, offs_sem)
    first.start()
    for copy in copies:
        copy.start()
    low[...] = jnp.zeros_like(low)
    first.wait()
    for c in range(2):
        low[c * 2 : c * 2 + 2, :32] = offs[c, 2:4].astype(F32)
    down_ref[breadth * half // 128 :, :] = low[...].astype(BF)
    for copy in copies:
        copy.wait()


def row_sum(strips, rows_ref):
    return jnp.dot(rows_ref[...], strips, preferred_element_type=F32).astype(BF)


def col_sum(half, cols_ref):
    out = []
    for b in range(LANES // 128):
        lanes = slice(b * 128, (b + 1) * 128)
        both = jnp.concatenate([half[:KROWS, lanes], half[KROWS:, lanes]], axis=1)
        spec = jnp.dot(both, cols_ref[...], preferred_element_type=F32)
        out.append((spec[:, :128], spec[:, 128:]))
    return out


def inner_kernel(px_ref, rows_ref, cols_ref, first_ref, second_ref, corr_ref, mix_ref):
    count = px_ref.shape[0]
    sums, specs = [], []
    half = row_sum(px_ref[0], rows_ref)
    prod = None
    for s in range(count):
        specs.append(col_sum(half, cols_ref))
        if s + 1 < count:
            half = row_sum(px_ref[s + 1], rows_ref)
        if prod is not None:
            sums.append(first_sum(first_ref, prod).astype(BF))
        prod = whiten(specs[s], specs[s - 1]) if s else None
    sums.append(first_sum(first_ref, prod).astype(BF))
    edge, old = specs[0], specs[-1]
    low = lax.broadcasted_iota(jnp.int32, (KROWS, 128), 0) < 2 * HALF
    for b in range(LANES // 128):
        for part in range(2):
            mix_ref[part * KROWS : (part + 1) * KROWS, b * 128 : (b + 1) * 128] = jnp.where(
                low, edge[b][part], old[b][part]
            ).astype(BF)
    term = jnp.dot(jnp.concatenate(sums, axis=0), second_ref[0], preferred_element_type=F32)

    @pl.when(pl.program_id(0) == 0)
    def _():
        corr_ref[...] = term

    @pl.when(pl.program_id(0) > 0)
    def _():
        corr_ref[...] += term


def pick(pieces, offset):
    value = pieces[0]
    for i in range(1, 5):
        value = jnp.where(offset == i - 2, pieces[i], value)
    return value


def peak_step(low, center, high):
    bend = jnp.maximum(jnp.abs(low - 2.0 * center + high), 1.0)
    return (low - high) / (2.0 * bend)


def edge_kernel(
    up_ref, down_ref, mix_ref, rows_ref, cols_ref, first_ref, second_ref,
    inner_ref, offs_ref, valid_ref, flow_ref, load_ref, picked, offs, packed,
):
    sa = lax.axis_index("sa")
    breadth = mix_ref.shape[1]
    half = up_ref.shape[0] * 128 // breadth
    pr = lax.broadcasted_iota(jnp.int32, (32, 512), 0) % PR
    dropped = ((sa == 0) & (pr < 2)) | ((sa == lax.axis_size("sa") - 1) & (pr >= 2))

    def strips(j):
        parts = []
        for b in range(2 * j, 2 * j + 2):
            rows = slice(b * half, (b + 1) * half)
            parts.append(jnp.concatenate([up_ref[rows], down_ref[rows]], axis=0))
        return jnp.concatenate(parts, axis=1)

    blocks = breadth // LANES
    corr = jnp.zeros((32, 256), F32)
    row = row_sum(strips(0), rows_ref)
    prod = None
    for j in range(blocks + 1):
        if j < blocks:
            there = col_sum(row, cols_ref)
            if j + 1 < blocks:
                row = row_sum(strips(j + 1), rows_ref)
        if j:
            sums = first_sum(first_ref, prod)
            sums = jnp.where(dropped, 0.0, sums).astype(BF)
            corr += jnp.dot(sums, second_ref[j - 1], preferred_element_type=F32)
        if j < blocks:
            here = []
            for b in range(2 * j, 2 * j + 2):
                part = slice(b * 128, (b + 1) * 128)
                here.append((mix_ref[:KROWS, part].astype(F32), mix_ref[KROWS:, part].astype(F32)))
            prod = whiten(here, there)

    for p1 in range(SPAN):
        picked[p1, 0:PR] = corr[p1 * PR : (p1 + 1) * PR]
        for s in range(3):
            picked[p1, (s + 1) * PR : (s + 2) * PR] = inner_ref[
                s * 32 + p1 * PR : s * 32 + (p1 + 1) * PR
            ]
    extra = down_ref[breadth * half // 128 :, :].astype(F32).astype(jnp.int32)
    for c in range(2):
        for s in range(4):
            offs[c, s * PR : (s + 1) * PR, :] = offs_ref[s, c]
        offs[c, 2:4, :] = extra[c * 2 : c * 2 + 2, :32]
    row_off, col_off = offs[0], offs[1]
    wide = jnp.concatenate([row_off] * 8, axis=1)
    layers = [picked[p1] * (1.0 / PATCH) for p1 in range(SPAN)]
    low, mid, high = [pick(layers[d : d + 5], wide) for d in range(3)]

    def cut(layer, d):
        return pick([layer[:, (d + i) * 32 : (d + i + 1) * 32] for i in range(5)], col_off)

    center = cut(mid, 1)
    flows = (
        row_off.astype(F32) + peak_step(cut(low, 1), center, cut(high, 1)),
        col_off.astype(F32) + peak_step(cut(mid, 0), center, cut(mid, 2)),
    )
    weights = jnp.concatenate([valid_ref[s].astype(F32) for s in range(4)], axis=0)
    for c, field in enumerate(flows + (weights,)):
        ring = jnp.concatenate([field[:, 16:], field, field[:, :16]], axis=1)
        for s in range(4):
            rows = slice(s * PR, (s + 1) * PR)
            if c < 2:
                flow_ref[c * PR : (c + 1) * PR, s * 32 : (s + 1) * 32] = field[rows]
            at = (s % 2) * 12 + c * PR
            packed[at : at + PR, (s // 2) * 64 : (s // 2 + 1) * 64] = ring[rows]
    load_ref[...] = packed[...].astype(BF)


def relax_kernel(got_ref, own_ref, flow_out, mesh_out, raw, flow, coef, state, speed):
    gx, gy, sa = [lax.axis_index(a) for a in AXES]
    nx, ny, ns = [lax.axis_size(a) for a in AXES]
    shape = (24, 128)
    lane = lax.broadcasted_iota(jnp.int32, shape, 1)
    row = lax.broadcasted_iota(jnp.int32, shape, 0)
    low = lane < 64
    for c in range(3):
        for i in range(2):
            for k in range(ns):
                raw[c, i, k, 20:, :] = jnp.zeros((4, 128), F32)
    for g in range(5):
        at = jnp.clip(gy + g - 2, 0, ny - 1) * ns
        for k in range(ns):
            block = got_ref[at + k].astype(F32)
            for i in range(2):
                for c in range(3):
                    raw[c, i, k, g * PR : (g + 1) * PR, :] = block[
                        i * 12 + c * PR : i * 12 + (c + 1) * PR
                    ]

    place = gy * PR - 2 * PR + row
    column = gx * 32 - 16 + lane % 64
    ok = (place >= 0) & (place < ny * PR) & (row < 5 * PR) & (column >= 0) & (column < nx * 32)
    inside = jnp.where(ok, 1.0, 0.0)
    edges = jnp.where(place == 0, 1.0, 0.0) + jnp.where(place == ny * PR - 1, 1.0, 0.0)
    edges += jnp.where(column == 0, 1.0, 0.0) + jnp.where(column == nx * 32 - 1, 1.0, 0.0)
    degree = 4.0 - edges
    zero = jnp.zeros(shape, F32)

    swapped = (row % PR >= 2) & low
    for c in range(2):
        carry = zero
        for k in range(ns):
            even = jnp.where(swapped, raw[c, 0, (k + ns - 1) % ns], raw[c, 0, k]) * inside
            odd = raw[c, 1, k] * inside
            flow[c, 0, k] = even
            flow[c, 1, k] = odd
            pair = even + odd
            turned = pltpu.roll(pair, 64, 1)
            even = even + jnp.where(low, 0.0, turned) + carry
            state[0, c, 0, k] = even
            state[0, c, 1, k] = even + odd
            carry = carry + pair + turned
            speed[c, 0, k] = zero
            speed[c, 1, k] = zero

    def below(get, i, k):
        if i == 1:
            return get(0, k)
        return pltpu.roll(jnp.where(low, get(1, k), get(1, k - 1) if k else 0.0), 64, 1)

    def above(get, i, k):
        if i == 0:
            return get(1, k)
        return pltpu.roll(jnp.where(low, get(0, k + 1) if k + 1 < ns else 0.0, get(0, k)), 64, 1)

    plane = inside * (step_size * spring_plane)
    stack = inside * (step_size * spring_stack)
    for i in range(2):
        for k in range(ns):
            w = raw[2, i, k] * stack
            w_next = above(lambda i, k: raw[2, i, k], i, k) * stack
            coef[0, i, k] = w
            coef[1, i, k] = w_next
            coef[2, i, k] = degree * plane + w + w_next
            for c in range(2):
                get = lambda i, k: flow[c, i, k]
                coef[3 + c, i, k] = w * get(i, k) - w_next * above(get, i, k)

    def advance(src, dst):
        for c in range(2):
            get = lambda i, k: state[src, c, i, k]
            for k in range(ns):
                for i in range(2):
                    m = get(i, k)
                    around = pltpu.roll(m, 1, 1) + pltpu.roll(m, 127, 1)
                    around += pltpu.roll(m, 1, 0) + pltpu.roll(m, 23, 0)
                    v = damping * speed[c, i, k] - coef[2, i, k] * m + plane * around
                    v += coef[0, i, k] * below(get, i, k) + coef[1, i, k] * above(get, i, k)
                    v += coef[3 + c, i, k]
                    speed[c, i, k] = v
                    state[dst, c, i, k] = m + v

    def two(step, unused):
        advance(0, 1)
        advance(1, 0)
        return unused

    lax.fori_loop(0, RELAX // 2, two, 0)
    mine = slice(2 * PR, 3 * PR)
    late = lax.broadcasted_iota(jnp.int32, (PR, 32), 0) >= 2
    for c in range(2):
        for s in range(4):
            lanes = slice((s // 2) * 64 + 16, (s // 2) * 64 + 48)
            mesh_out[s, c] = state[0, c, s % 2, sa][mine, lanes]
            f = own_ref[c * PR : (c + 1) * PR, s * 32 : (s + 1) * 32]
            if s == 0:
                f = jnp.where(late, flow[c, 0, sa][mine, lanes], f)
            flow_out[s, c] = f


def per_device(pixels, peak_offsets, validity):
    count, height, breadth = pixels.shape
    blocks = breadth // LANES
    size = lax.axis_size("sa")
    half = height // 2
    vmem = lambda: pl.BlockSpec(memory_space=pltpu.VMEM)
    held = pltpu.with_memory_space_constraint(pixels, pltpu.HBM)
    packed = breadth * half // 128
    up, down = pl.pallas_call(
        send_kernel,
        in_specs=[pl.BlockSpec(memory_space=pltpu.HBM)] * 2,
        out_specs=[vmem(), vmem()],
        out_shape=[
            jax.ShapeDtypeStruct((packed, 128), BF),
            jax.ShapeDtypeStruct((packed + 8, 128), BF),
        ],
        scratch_shapes=[
            pltpu.VMEM((2, PR, 32), jnp.int32),
            pltpu.VMEM((8, 128), F32),
            pltpu.SemaphoreType.DMA((2, breadth // 128)),
            pltpu.SemaphoreType.DMA,
        ],
        compiler_params=pltpu.CompilerParams(vmem_limit_bytes=GRANT),
        name="send",
    )(held, pltpu.with_memory_space_constraint(peak_offsets, pltpu.HBM))
    up = lax.ppermute(up, "sa", [(i, (i + 1) % size) for i in range(size)])
    down = lax.ppermute(down, "sa", [(i, (i - 1) % size) for i in range(size)])

    rows = jnp.asarray(row_matrix())
    cols = jnp.asarray(col_matrix())
    second = jnp.asarray(second_matrix(blocks))
    whole = lambda shape: pl.BlockSpec(shape, lambda j: (0,) * len(shape))
    table_specs = [
        whole((2 * KROWS, PR * PATCH)),
        whole((256, 256)),
        whole((64, 2 * KROWS)),
        pl.BlockSpec((1, 512, 8 * blocks * 4), lambda j: (j, 0, 0)),
    ]
    inner, mix = pl.pallas_call(
        inner_kernel,
        grid=(blocks,),
        in_specs=[pl.BlockSpec((count, height, LANES), lambda j: (0, 0, j))] + table_specs,
        out_specs=[
            whole((96, 256)),
            pl.BlockSpec((2 * KROWS, LANES), lambda j: (0, j)),
        ],
        out_shape=[
            jax.ShapeDtypeStruct((96, 256), F32),
            jax.ShapeDtypeStruct((2 * KROWS, breadth), BF),
        ],
        compiler_params=pltpu.CompilerParams(dimension_semantics=("arbitrary",), vmem_limit_bytes=GRANT),
        cost_estimate=pl.CostEstimate(
            flops=8 * 10**9, bytes_accessed=8 * 2**20, transcendentals=10**6
        ),
        name="inner",
    )(
        held, rows, cols, jnp.asarray(first_matrix(False)), second,
    )

    own, load = pl.pallas_call(
        edge_kernel,
        in_specs=[vmem()] * 10,
        out_specs=[vmem(), vmem()],
        out_shape=[
            jax.ShapeDtypeStruct((8, 128), F32),
            jax.ShapeDtypeStruct((24, 128), BF),
        ],
        scratch_shapes=[
            pltpu.VMEM((SPAN, 16, 256), F32),
            pltpu.VMEM((2, 16, 32), jnp.int32),
            pltpu.VMEM((24, 128), F32),
        ],
        compiler_params=pltpu.CompilerParams(vmem_limit_bytes=GRANT),
        name="edge",
    )(
        up, down, mix, rows, cols, jnp.asarray(first_matrix(True)), second,
        inner, peak_offsets, validity,
    )

    breadths = lax.axis_size("gx")
    near = lax.ppermute(load, "gx", [(i, i ^ 1) for i in range(breadths)])
    far = [(i, ((i + 1) ^ 1) - 1) for i in range(1, breadths - 1)]
    far = lax.ppermute(load, "gx", far)
    odd = lax.axis_index("gx") % 2 == 1
    place = lax.broadcasted_iota(jnp.int32, load.shape, 1) % 64
    side = jnp.where((place < 16) == odd, near, far)
    load = jnp.where((place >= 16) & (place < 48), load, side)
    devices = lax.axis_size(("gy", "sa"))
    sent = jnp.broadcast_to(load[None], (devices,) + load.shape)
    got = lax.all_to_all(sent, ("gy", "sa"), 0, 0)

    field = (count, 2, PR, 32)
    stack = (2, size, 24, 128)
    return pl.pallas_call(
        relax_kernel,
        in_specs=[vmem(), vmem()],
        out_specs=[vmem(), vmem()],
        out_shape=[jax.ShapeDtypeStruct(field, F32)] * 2,
        scratch_shapes=[
            pltpu.VMEM((3,) + stack, F32),
            pltpu.VMEM((2,) + stack, F32),
            pltpu.VMEM((5,) + stack, F32),
            pltpu.VMEM((2, 2) + stack, F32),
            pltpu.VMEM((2,) + stack, F32),
        ],
        compiler_params=pltpu.CompilerParams(vmem_limit_bytes=GRANT),
        name="relax",
    )(got, own)


def solution(mesh):
    return jax.shard_map(
        per_device,
        mesh=mesh,
        in_specs=(P("sa", "gy", "gx"), P("sa", None, "gy", "gx"), P("sa", "gy", "gx")),
        out_specs=(P("sa", None, "gy", "gx"), P("sa", None, "gy", "gx")),
        check_vma=False,
    )
```

time: 60.5 us -> 46.1 us (0.76)
  the two profiles are of different devices: /device:TPU:1 before, /device:TPU:17 now
where the time goes in v2:
time: 46.1 us; the launch traced here: 45.7 us
  blocking collectives  18.9 us (41%)
  Pallas kernels  16 us (35%)
  starting transfers between devices  5.74 us (12%)
  waiting for transfers between devices  4.11 us (9%)
  between operations  0.79 us (2%)
    all_to_all x1, blocking collectives, per_device(): got = lax.all_to_all(sent, ('gy', 'sa'), 0, 0)  18.9 us
    pallas_call x1, Pallas kernels, per_device(): pl.pallas_call(inner_kernel, grid=(blocks,), in_specs=[pl.BlockSpec((coun...  9.57 us
    pallas_call x1, Pallas kernels, per_device(): pl.pallas_call(relax_kernel, in_specs=[vmem(), vmem()], out_specs=[vmem()...  2.47 us
    ppermute x1, waiting for transfers between devices, per_device(): far = lax.ppermute(load, 'gx', far)  2.41 us
    pallas_call x1, Pallas kernels, per_device(): pl.pallas_call(edge_kernel, in_specs=[vmem()] * 10, out_specs=[vmem(), vm...  2.37 us
    ppermute x1, starting transfers between devices, per_device(): far = lax.ppermute(load, 'gx', far)  1.91 us
    ppermute x1, waiting for transfers between devices, per_device(): up = lax.ppermute(up, 'sa', [(i, (i + 1) % size) for i in range(size)])  1.69 us
    pallas_call x1, Pallas kernels, per_device(): pl.pallas_call(send_kernel, in_specs=[pl.BlockSpec(memory_space=pltpu.HBM...  1.63 us
  transfers between devices with their start and end apart: 4, of which 2 were waited for; matrix products, arithmetic and copies ran while one was open for 0% of the time, Pallas kernels for 21%

profile of v2, /device:TPU:17, one launch (start us, length us, event | category | flops | bytes accessed | tf_op | source)
XLA Modules:
  0.0 45.7 jit_solution(10591271135965348397)
XLA Ops:
  0.6 0.0 copy-start
  0.6 0.0 copy-start.1
  0.7 0.0 copy-start.2
  0.7 0.0 copy-start.6
  0.7 1.6 %send.1 = (bf16[2048,128]{1,0:T(8,128)(2,1)S(1)}, bf16[2056,128]{1,0:T(8,128)(2,1)S(1)}) custom-call(bf16[4,256,2048]{2,1,0:T(8,128)(2,1)} %px_ref.3, s32[4,2,4,32]{3,2,1,0:T(4,128)} %offs_ref.3), custom_call_target="tpu_custom_call" | custom-call | tf_op jit(solution)/shard_map/send/pallas_call | solution.py:380
  2.3 1.3 %collective-permute-start = (bf16[2048,128]{1,0:T(8,128)(2,1)S(1)}, bf16[2048,128]{1,0:T(8,128)(2,1)S(1)}, u32[]{:S(2)}, u32[]{:S(2)}) collective-permute-start(bf16[2048,128]{1,0:T(8,128)(2,1)S(1)} %get-tuple-element.8), channel_id=1, source_target_pairs={{0,1},{1,2},{2,3},{3,0},{4,5},{5,6},{6,7},{7,4},{8,9},{9,10},{10,1... | collective-permute-start | bytes 1572872 | tf_op jit(solution)/shard_map/ppermute | solution.py:397
  3.6 1.5 %collective-permute-start.1 = (bf16[2056,128]{1,0:T(8,128)(2,1)S(1)}, bf16[2056,128]{1,0:T(8,128)(2,1)S(1)}, u32[]{:S(2)}, u32[]{:S(2)}) collective-permute-start(bf16[2056,128]{1,0:T(8,128)(2,1)S(1)} %get-tuple-element.9), channel_id=1, source_target_pairs={{0,3},{1,0},{2,1},{3,2},{4,7},{5,4},{6,5},{7,6},{8,11},{9,8},{10,9... | collective-permute-start | bytes 1579016 | tf_op jit(solution)/shard_map/ppermute | solution.py:398
  5.1 0.0 copy-done
  5.1 0.0 copy-done.1
  5.1 0.0 copy-done.2
  5.1 0.0 copy-done.6
  5.1 0.0 copy-start.3
  5.1 0.0 copy-start.4
  5.1 0.0 copy-start.5
  5.1 9.6 %inner.1 = (f32[96,256]{1,0:T(8,128)S(1)}, bf16[288,2048]{1,0:T(8,128)(2,1)S(1)}) custom-call(bf16[4,256,2048]{2,1,0:T(8,128)(2,1)} %px_ref.3, bf16[288,256]{1,0:T(8,128)(2,1)S(1)} %copy-done.1, bf16[256,256]{1,0:T(8,128)(2,1)S(1)} %copy-done.2, bf16[64,288]{1,0:T(8,128)(2,1)S(1)} %copy-done.6, bf16[8,512,256]{2,1,0:T(8,128)(2,1)S(1)} %copy-done), custom_call_target="tpu_custom_call" | custom-call | flops 8000000000 | bytes 8388608 | tf_op jit(solution)/shard_map/inner/pallas_call | solution.py:410
  14.7 1.7 %collective-permute-done.up_ref = bf16[2048,128]{1,0:T(8,128)(2,1)S(1)} collective-permute-done((bf16[2048,128]{1,0:T(8,128)(2,1)S(1)}, bf16[2048,128]{1,0:T(8,128)(2,1)S(1)}, u32[]{:S(2)}, u32[]{:S(2)}) %collective-permute-start) | collective-permute-done | bytes 524320 | tf_op jit(solution)/shard_map/ppermute | solution.py:397
  16.4 0.0 collective-permute-done.1.down_ref
  16.4 0.0 copy-done.3
  16.4 0.0 copy-done.4
  16.4 0.0 copy-done.5
  16.4 2.4 %edge.1 = (f32[8,128]{1,0:T(8,128)S(1)}, bf16[24,128]{1,0:T(8,128)(2,1)S(1)}) custom-call(bf16[2048,128]{1,0:T(8,128)(2,1)S(1)} %collective-permute-done.up_ref, bf16[2056,128]{1,0:T(8,128)(2,1)S(1)} %collective-permute-done.1.down_ref, bf16[288,2048]{1,0:T(8,128)(2,1)S(1)} %get-tuple-element.10.mix_ref, bf16[288,256]{1,0:T(8,128)(2,1)S(1)} %copy-done.1, ...), custom_call_target="tpu_custom_call" | custom-call | tf_op jit(solution)/shard_map/edge/pallas_call | solution.py:431
  18.8 1.1 %collective-permute-start.2 = (bf16[24,128]{1,0:T(8,128)(2,1)S(1)}, bf16[24,128]{1,0:T(8,128)(2,1)S(1)}, u32[]{:S(2)}, u32[]{:S(2)}) collective-permute-start(bf16[24,128]{1,0:T(8,128)(2,1)S(1)} %get-tuple-element.12), channel_id=1, source_target_pairs={{0,32},{32,0},{64,96},{96,64},{1,33},{33,1},{65,97},{97,65},{2,34}... | collective-permute-start | bytes 18440 | tf_op jit(solution)/shard_map/ppermute | solution.py:452
  19.9 1.9 %collective-permute-start.3 = (bf16[24,128]{1,0:T(8,128)(2,1)S(1)}, bf16[24,128]{1,0:T(8,128)(2,1)S(1)}, u32[]{:S(2)}, u32[]{:S(2)}) collective-permute-start(bf16[24,128]{1,0:T(8,128)(2,1)S(1)} %get-tuple-element.12), channel_id=1, source_target_pairs={{32,64},{64,32},{33,65},{65,33},{34,66},{66,34},{35,67},{67,35},{3... | collective-permute-start | bytes 18440 | tf_op jit(solution)/shard_map/ppermute | solution.py:454
  21.8 0.0 collective-permute-done.2
  21.8 2.4 %collective-permute-done.3 = bf16[24,128]{1,0:T(8,128)(2,1)S(1)} collective-permute-done((bf16[24,128]{1,0:T(8,128)(2,1)S(1)}, bf16[24,128]{1,0:T(8,128)(2,1)S(1)}, u32[]{:S(2)}, u32[]{:S(2)}) %collective-permute-start.3) | collective-permute-done | bytes 6176 | tf_op jit(solution)/shard_map/ppermute | solution.py:454
  24.3 18.9 %all_to_all.5.got_ref = bf16[32,24,128]{2,1,0:T(8,128)(2,1)S(1)} all-to-all(bf16[32,24,128]{2,1,0:T(8,128)(2,1)S(1)} %broadcast_in_dim.2), channel_id=1, replica_groups=mesh['gx'=4,'gy'=8,'sa'=4] {'gy','sa'}, dimensions={0} | all-to-all | bytes 393216 | tf_op jit(solution)/shard_map/all_to_all | solution.py:461
  43.2 2.5 %relax.1 = (f32[4,2,4,32]{3,2,1,0:T(4,128)}, f32[4,2,4,32]{3,2,1,0:T(4,128)}) custom-call(bf16[32,24,128]{2,1,0:T(8,128)(2,1)S(1)} %all_to_all.5.got_ref, f32[8,128]{1,0:T(8,128)S(1)} %get-tuple-element.13.own_ref), custom_call_target="tpu_custom_call" | custom-call | tf_op jit(solution)/shard_map/relax/pallas_call | solution.py:465
  (4 shorter events, 0.0 us)
Async XLA Ops:
  0.6 4.4 %copy-start = (bf16[8,512,256]{2,1,0:T(8,128)(2,1)S(1)}, bf16[8,512,256]{2,1,0:T(8,128)(2,1)}, u32[]{:S(2)}) copy-start(bf16[8,512,256]{2,1,0:T(8,128)(2,1)} %constant.51.clone.second_ref) | copy-start | bytes 6291460
  0.6 4.4 %copy-start.1 = (bf16[288,256]{1,0:T(8,128)(2,1)S(1)}, bf16[288,256]{1,0:T(8,128)(2,1)}, u32[]{:S(2)}) copy-start(bf16[288,256]{1,0:T(8,128)(2,1)} %constant.49.clone.rows_ref) | copy-start | bytes 442372
  0.7 4.4 %copy-start.2 = (bf16[256,256]{1,0:T(8,128)(2,1)S(1)}, bf16[256,256]{1,0:T(8,128)(2,1)}, u32[]{:S(2)}) copy-start(bf16[256,256]{1,0:T(8,128)(2,1)} %constant.50.clone.cols_ref) | copy-start | bytes 393220
  0.7 4.4 %copy-start.6 = (bf16[64,288]{1,0:T(8,128)(2,1)S(1)}, bf16[64,288]{1,0:T(8,128)(2,1)}, u32[]{:S(2)}) copy-start(bf16[64,288]{1,0:T(8,128)(2,1)} %constant.52.clone.first_ref) | copy-start | bytes 110596
  2.3 14.1 %collective-permute-start = (bf16[2048,128]{1,0:T(8,128)(2,1)S(1)}, bf16[2048,128]{1,0:T(8,128)(2,1)S(1)}, u32[]{:S(2)}, u32[]{:S(2)}) collective-permute-start(bf16[2048,128]{1,0:T(8,128)(2,1)S(1)} %get-tuple-element.8), channel_id=1, source_target_pairs={{0,1},{1,2},{2,3},{3,0},{4,5},{5,6},{6,7},{7,4},{8,9},{9,10},{10,1... | collective-permute-start | bytes 1572872 | tf_op jit(solution)/shard_map/ppermute | solution.py:397
  3.6 12.8 %collective-permute-start.1 = (bf16[2056,128]{1,0:T(8,128)(2,1)S(1)}, bf16[2056,128]{1,0:T(8,128)(2,1)S(1)}, u32[]{:S(2)}, u32[]{:S(2)}) collective-permute-start(bf16[2056,128]{1,0:T(8,128)(2,1)S(1)} %get-tuple-element.9), channel_id=1, source_target_pairs={{0,3},{1,0},{2,1},{3,2},{4,7},{5,4},{6,5},{7,6},{8,11},{9,8},{10,9... | collective-permute-start | bytes 1579016 | tf_op jit(solution)/shard_map/ppermute | solution.py:398
  5.1 11.3 %copy-start.3 = (s32[4,2,4,32]{3,2,1,0:T(4,128)S(1)}, s32[4,2,4,32]{3,2,1,0:T(4,128)}, u32[]{:S(2)}) copy-start(s32[4,2,4,32]{3,2,1,0:T(4,128)} %offs_ref.3) | copy-start | bytes 12292
  5.1 11.3 %copy-start.4 = (bf16[64,288]{1,0:T(8,128)(2,1)S(1)}, bf16[64,288]{1,0:T(8,128)(2,1)}, u32[]{:S(2)}) copy-start(bf16[64,288]{1,0:T(8,128)(2,1)} %constant.53.clone.first_ref) | copy-start | bytes 110596
  5.1 11.3 %copy-start.5 = (s32[4,4,32]{2,1,0:T(4,128)S(1)}, s32[4,4,32]{2,1,0:T(4,128)}, u32[]{:S(2)}) copy-start(s32[4,4,32]{2,1,0:T(4,128)} %valid_ref.1) | copy-start | bytes 6148
  18.8 3.0 %collective-permute-start.2 = (bf16[24,128]{1,0:T(8,128)(2,1)S(1)}, bf16[24,128]{1,0:T(8,128)(2,1)S(1)}, u32[]{:S(2)}, u32[]{:S(2)}) collective-permute-start(bf16[24,128]{1,0:T(8,128)(2,1)S(1)} %get-tuple-element.12), channel_id=1, source_target_pairs={{0,32},{32,0},{64,96},{96,64},{1,33},{33,1},{65,97},{97,65},{2,34}... | collective-permute-start | bytes 18440 | tf_op jit(solution)/shard_map/ppermute | solution.py:452
  19.9 4.4 %collective-permute-start.3 = (bf16[24,128]{1,0:T(8,128)(2,1)S(1)}, bf16[24,128]{1,0:T(8,128)(2,1)S(1)}, u32[]{:S(2)}, u32[]{:S(2)}) collective-permute-start(bf16[24,128]{1,0:T(8,128)(2,1)S(1)} %get-tuple-element.12), channel_id=1, source_target_pairs={{32,64},{64,32},{33,65},{65,33},{34,66},{66,34},{35,67},{67,35},{3... | collective-permute-start | bytes 18440 | tf_op jit(solution)/shard_map/ppermute | solution.py:454

commit v3 on v2

--- a/solution.py
+++ b/solution.py
@@ -14,7 +14,9 @@
 HALF = PATCH // 2 + 1
 PR = 4
 KROWS = 144
-LANES = 256
+LANES = 512
+SUB = LANES // 128
+HELD = LANES // PATCH
 REACH = 3
 SPAN = 2 * REACH + 1
 GRANT = 20 * 2**20
@@ -80,15 +82,15 @@
 
 def second_matrix(blocks):
     cosine, sine = wave_tables()
-    out = np.zeros((blocks, 2, 4, PATCH, 8, blocks, 4), np.float32)
+    out = np.zeros((blocks, 2, HELD, PATCH, 8, blocks, HELD), np.float32)
     k2 = np.arange(PATCH)
     for p2 in range(SPAN):
         phase = k2 * (p2 - REACH) % PATCH
         for j in range(blocks):
-            for p in range(4):
+            for p in range(HELD):
                 out[j, 0, p, :, p2, j, p] = cosine[phase]
                 out[j, 1, p, :, p2, j, p] = -sine[phase]
-    return out.reshape(blocks, 512, 8 * blocks * 4).astype(BF)
+    return out.reshape(blocks, 2 * LANES, 8 * blocks * HELD).astype(BF)
 
 
 def whiten(now, old):
@@ -110,30 +112,22 @@
     return jnp.concatenate([both[:32], both[32:]], axis=1)
 
 
-def send_kernel(px_ref, offs_ref, up_ref, down_ref, offs, low, sems, offs_sem):
-    count, height, breadth = px_ref.shape
-    half = height // 2
-    copies = []
-    for b in range(breadth // 128):
-        rows, lanes = pl.ds(b * half, half), pl.ds(b * 128, 128)
-        copies += [
-            pltpu.make_async_copy(
-                px_ref.at[count - 1, pl.ds(0, half), lanes], up_ref.at[rows], sems.at[0, b]
-            ),
-            pltpu.make_async_copy(
-                px_ref.at[0, pl.ds(half, half), lanes], down_ref.at[rows], sems.at[1, b]
-            ),
-        ]
-    first = pltpu.make_async_copy(offs_ref.at[0], offs, offs_sem)
-    first.start()
+def send_kernel(px_ref, offs_ref, up_ref, down_ref, extra_ref, offs, low, sems):
+    half = up_ref.shape[0]
+    last = px_ref.shape[0] - 1
+    copies = [
+        pltpu.make_async_copy(offs_ref.at[0], offs, sems.at[0]),
+        pltpu.make_async_copy(px_ref.at[last, pl.ds(0, half)], up_ref, sems.at[1]),
+        pltpu.make_async_copy(px_ref.at[0, pl.ds(half, half)], down_ref, sems.at[2]),
+    ]
     for copy in copies:
         copy.start()
     low[...] = jnp.zeros_like(low)
-    first.wait()
+    copies[0].wait()
     for c in range(2):
         low[c * 2 : c * 2 + 2, :32] = offs[c, 2:4].astype(F32)
-    down_ref[breadth * half // 128 :, :] = low[...].astype(BF)
-    for copy in copies:
+    extra_ref[...] = low[...].astype(BF)
+    for copy in copies[1:]:
         copy.wait()
 
 
@@ -142,12 +136,15 @@
 
 
 def col_sum(half, cols_ref):
+    both = []
+    for b in range(SUB):
+        lanes = slice(b * 128, (b + 1) * 128)
+        both.append(jnp.concatenate([half[:KROWS, lanes], half[KROWS:, lanes]], axis=1))
+    spec = jnp.dot(jnp.concatenate(both, axis=0), cols_ref[...], preferred_element_type=F32)
     out = []
-    for b in range(LANES // 128):
-        lanes = slice(b * 128, (b + 1) * 128)
-        both = jnp.concatenate([half[:KROWS, lanes], half[KROWS:, lanes]], axis=1)
-        spec = jnp.dot(both, cols_ref[...], preferred_element_type=F32)
-        out.append((spec[:, :128], spec[:, 128:]))
+    for b in range(SUB):
+        rows = slice(b * KROWS, (b + 1) * KROWS)
+        out.append((spec[rows, :128], spec[rows, 128:]))
     return out
 
 
@@ -166,7 +163,7 @@
     sums.append(first_sum(first_ref, prod).astype(BF))
     edge, old = specs[0], specs[-1]
     low = lax.broadcasted_iota(jnp.int32, (KROWS, 128), 0) < 2 * HALF
-    for b in range(LANES // 128):
+    for b in range(SUB):
         for part in range(2):
             mix_ref[part * KROWS : (part + 1) * KROWS, b * 128 : (b + 1) * 128] = jnp.where(
                 low, edge[b][part], old[b][part]
@@ -195,21 +192,17 @@
 
 
 def edge_kernel(
-    up_ref, down_ref, mix_ref, rows_ref, cols_ref, first_ref, second_ref,
+    up_ref, down_ref, extra_ref, mix_ref, rows_ref, cols_ref, first_ref, second_ref,
     inner_ref, offs_ref, valid_ref, flow_ref, load_ref, picked, offs, packed,
 ):
     sa = lax.axis_index("sa")
     breadth = mix_ref.shape[1]
-    half = up_ref.shape[0] * 128 // breadth
-    pr = lax.broadcasted_iota(jnp.int32, (32, 512), 0) % PR
+    pr = lax.broadcasted_iota(jnp.int32, (32, 2 * LANES), 0) % PR
     dropped = ((sa == 0) & (pr < 2)) | ((sa == lax.axis_size("sa") - 1) & (pr >= 2))
 
     def strips(j):
-        parts = []
-        for b in range(2 * j, 2 * j + 2):
-            rows = slice(b * half, (b + 1) * half)
-            parts.append(jnp.concatenate([up_ref[rows], down_ref[rows]], axis=0))
-        return jnp.concatenate(parts, axis=1)
+        lanes = slice(j * LANES, (j + 1) * LANES)
+        return jnp.concatenate([up_ref[:, lanes], down_ref[:, lanes]], axis=0)
 
     blocks = breadth // LANES
     corr = jnp.zeros((32, 256), F32)
@@ -226,7 +219,7 @@
             corr += jnp.dot(sums, second_ref[j - 1], preferred_element_type=F32)
         if j < blocks:
             here = []
-            for b in range(2 * j, 2 * j + 2):
+            for b in range(SUB * j, SUB * (j + 1)):
                 part = slice(b * 128, (b + 1) * 128)
                 here.append((mix_ref[:KROWS, part].astype(F32), mix_ref[KROWS:, part].astype(F32)))
             prod = whiten(here, there)
@@ -237,7 +230,7 @@
             picked[p1, (s + 1) * PR : (s + 2) * PR] = inner_ref[
                 s * 32 + p1 * PR : s * 32 + (p1 + 1) * PR
             ]
-    extra = down_ref[breadth * half // 128 :, :].astype(F32).astype(jnp.int32)
+    extra = extra_ref[...].astype(F32).astype(jnp.int32)
     for c in range(2):
         for s in range(4):
             offs[c, s * PR : (s + 1) * PR, :] = offs_ref[s, c]
@@ -279,9 +272,13 @@
             for k in range(ns):
                 raw[c, i, k, 20:, :] = jnp.zeros((4, 128), F32)
     for g in range(5):
-        at = jnp.clip(gy + g - 2, 0, ny - 1) * ns
+        chip = (gy + g) // 2 - gy // 2 - 1
+        pair = (chip < 0) == (gy // 2 % 2 == 1)
+        chip = jnp.where(chip == 0, 0, jnp.where(pair, 1, 2))
+        core = g % 2
         for k in range(ns):
-            block = got_ref[at + k].astype(F32)
+            hop = sa ^ k
+            block = got_ref[hop ^ (hop // 2), chip, core].astype(F32)
             for i in range(2):
                 for c in range(3):
                     raw[c, i, k, g * PR : (g + 1) * PR, :] = block[
@@ -369,6 +366,45 @@
             flow_out[s, c] = f
 
 
+PAIR = {0: 1, 1: 0, 2: 3, 3: 2}
+CROSS = {1: 2, 2: 1}
+RING = {1: 2, 2: 1, 0: 3, 3: 0}
+SKIP = {0: 2, 2: 0, 1: 3, 3: 1}
+
+
+def trade(array, axis, partner):
+    sizes = [lax.axis_size(a) for a in AXES]
+    route = []
+    for x, y, k in np.ndindex(*sizes):
+        place = {"gx": x, "chip": y // 2, "sa": k}
+        target = (x, y ^ 1, k)
+        if place[axis] in partner:
+            place[axis] = partner[place[axis]]
+            target = (place["gx"], place["chip"] * 2 + y % 2, place["sa"])
+        route.append((
+            int(np.ravel_multi_index((x, y, k), sizes)),
+            int(np.ravel_multi_index(target, sizes)),
+        ))
+    return lax.ppermute(array, AXES, route)
+
+
+def spread(load):
+    near = trade(load, "gx", PAIR)
+    far = trade(load, "gx", CROSS)
+    odd = lax.axis_index("gx") % 2 == 1
+    place = lax.broadcasted_iota(jnp.int32, load.shape, 1) % 64
+    side = jnp.where((place < 16) == odd, near, far)
+    load = jnp.where((place >= 16) & (place < 48), load, side)
+    load = jnp.stack([load, trade(load, "gx", {})])
+    near = trade(load, "chip", PAIR)
+    far = trade(load, "chip", CROSS)
+    load = jnp.stack([load, near, far])
+    one = trade(load, "sa", PAIR)
+    two = trade(load, "sa", RING)
+    three = trade(load, "sa", SKIP)
+    return jnp.stack([load, one, two, three])
+
+
 def per_device(pixels, peak_offsets, validity):
     count, height, breadth = pixels.shape
     blocks = breadth // LANES
@@ -376,26 +412,28 @@
     half = height // 2
     vmem = lambda: pl.BlockSpec(memory_space=pltpu.VMEM)
     held = pltpu.with_memory_space_constraint(pixels, pltpu.HBM)
-    packed = breadth * half // 128
-    up, down = pl.pallas_call(
+    up, down, extra = pl.pallas_call(
         send_kernel,
         in_specs=[pl.BlockSpec(memory_space=pltpu.HBM)] * 2,
-        out_specs=[vmem(), vmem()],
+        out_specs=[vmem()] * 3,
         out_shape=[
-            jax.ShapeDtypeStruct((packed, 128), BF),
-            jax.ShapeDtypeStruct((packed + 8, 128), BF),
+            jax.ShapeDtypeStruct((half, breadth), BF),
+            jax.ShapeDtypeStruct((half, breadth), BF),
+            jax.ShapeDtypeStruct((8, 128), BF),
         ],
         scratch_shapes=[
             pltpu.VMEM((2, PR, 32), jnp.int32),
             pltpu.VMEM((8, 128), F32),
-            pltpu.SemaphoreType.DMA((2, breadth // 128)),
-            pltpu.SemaphoreType.DMA,
+            pltpu.SemaphoreType.DMA((3,)),
         ],
         compiler_params=pltpu.CompilerParams(vmem_limit_bytes=GRANT),
         name="send",
     )(held, pltpu.with_memory_space_constraint(peak_offsets, pltpu.HBM))
-    up = lax.ppermute(up, "sa", [(i, (i + 1) % size) for i in range(size)])
-    down = lax.ppermute(down, "sa", [(i, (i - 1) % size) for i in range(size)])
+    rise = [(i, (i + 1) % size) for i in range(size)]
+    sink = [(i, (i - 1) % size) for i in range(size)]
+    up = lax.ppermute(up, "sa", rise)
+    down = lax.ppermute(down, "sa", sink)
+    extra = lax.ppermute(extra, "sa", sink)
 
     rows = jnp.asarray(row_matrix())
     cols = jnp.asarray(col_matrix())
@@ -405,7 +443,7 @@
         whole((2 * KROWS, PR * PATCH)),
         whole((256, 256)),
         whole((64, 2 * KROWS)),
-        pl.BlockSpec((1, 512, 8 * blocks * 4), lambda j: (j, 0, 0)),
+        pl.BlockSpec((1, 2 * LANES, 8 * blocks * HELD), lambda j: (j, 0, 0)),
     ]
     inner, mix = pl.pallas_call(
         inner_kernel,
@@ -430,7 +468,7 @@
 
     own, load = pl.pallas_call(
         edge_kernel,
-        in_specs=[vmem()] * 10,
+        in_specs=[vmem()] * 11,
         out_specs=[vmem(), vmem()],
         out_shape=[
             jax.ShapeDtypeStruct((8, 128), F32),
@@ -444,21 +482,11 @@
         compiler_params=pltpu.CompilerParams(vmem_limit_bytes=GRANT),
         name="edge",
     )(
-        up, down, mix, rows, cols, jnp.asarray(first_matrix(True)), second,
+        up, down, extra, mix, rows, cols, jnp.asarray(first_matrix(True)), second,
         inner, peak_offsets, validity,
     )
 
-    breadths = lax.axis_size("gx")
-    near = lax.ppermute(load, "gx", [(i, i ^ 1) for i in range(breadths)])
-    far = [(i, ((i + 1) ^ 1) - 1) for i in range(1, breadths - 1)]
-    far = lax.ppermute(load, "gx", far)
-    odd = lax.axis_index("gx") % 2 == 1
-    place = lax.broadcasted_iota(jnp.int32, load.shape, 1) % 64
-    side = jnp.where((place < 16) == odd, near, far)
-    load = jnp.where((place >= 16) & (place < 48), load, side)
-    devices = lax.axis_size(("gy", "sa"))
-    sent = jnp.broadcast_to(load[None], (devices,) + load.shape)
-    got = lax.all_to_all(sent, ("gy", "sa"), 0, 0)
+    got = spread(load)
 
     field = (count, 2, PR, 32)
     stack = (2, size, 24, 128)

time: 46.1 us -> 41.9 us (0.909)
  the two profiles are of different devices: /device:TPU:17 before, /device:TPU:48 now
where the time goes in v3:
time: 41.9 us; the launch traced here: 41.8 us
  waiting for transfers between devices  15.7 us (37%)
  Pallas kernels  12.8 us (31%)
  starting transfers between devices  12.5 us (30%)
  between operations  0.75 us (2%)
    ppermute x8, waiting for transfers between devices, trade(): return lax.ppermute(array, AXES, route)  12.4 us
    ppermute x8, starting transfers between devices, trade(): return lax.ppermute(array, AXES, route)  7.62 us
    pallas_call x1, Pallas kernels, per_device(): pl.pallas_call(inner_kernel, grid=(blocks,), in_specs=[pl.BlockSpec((coun...  6.87 us
    ppermute x1, waiting for transfers between devices, per_device(): extra = lax.ppermute(extra, 'sa', sink)  3.23 us
    pallas_call x1, Pallas kernels, per_device(): pl.pallas_call(relax_kernel, in_specs=[vmem(), vmem()], out_specs=[vmem()...  2.52 us
    pallas_call x1, Pallas kernels, per_device(): pl.pallas_call(edge_kernel, in_specs=[vmem()] * 11, out_specs=[vmem(), vm...  2.02 us
    ppermute x1, starting transfers between devices, per_device(): down = lax.ppermute(down, 'sa', sink)  1.75 us
    ppermute x1, starting transfers between devices, per_device(): up = lax.ppermute(up, 'sa', rise)  1.56 us
  transfers between devices with their start and end apart: 11, of which 9 were waited for; matrix products, arithmetic and copies ran while one was open for 0% of the time, Pallas kernels for 16%

profile of v3, /device:TPU:48, one launch (start us, length us, event | category | flops | bytes accessed | tf_op | source)
XLA Modules:
  0.0 41.8 jit_solution(16832956874210134944)
XLA Ops:
  0.6 0.0 copy-start
  0.6 0.0 copy-start.1
  0.7 0.0 copy-start.2
  0.7 0.0 copy-start.6
  0.7 1.4 %send.1 = (bf16[128,2048]{1,0:T(8,128)(2,1)S(1)}, bf16[128,2048]{1,0:T(8,128)(2,1)S(1)}, bf16[8,128]{1,0:T(8,128)(2,1)S(1)}) custom-call(bf16[4,256,2048]{2,1,0:T(8,128)(2,1)} %px_ref.3, s32[4,2,4,32]{3,2,1,0:T(4,128)} %offs_ref.3), custom_call_target="tpu_custom_call" | custom-call | tf_op jit(solution)/shard_map/send/pallas_call | solution.py:415
  2.1 1.6 %collective-permute-start = (bf16[128,2048]{1,0:T(8,128)(2,1)S(1)}, bf16[128,2048]{1,0:T(8,128)(2,1)S(1)}, u32[]{:S(2)}, u32[]{:S(2)}) collective-permute-start(bf16[128,2048]{1,0:T(8,128)(2,1)S(1)} %get-tuple-element.9), channel_id=1, source_target_pairs={{0,1},{1,2},{2,3},{3,0},{4,5},{5,6},{6,7},{7,4},{8,9},{9,10},{10,1... | collective-permute-start | bytes 1572872 | tf_op jit(solution)/shard_map/ppermute | solution.py:434
  3.6 1.7 %collective-permute-start.1 = (bf16[128,2048]{1,0:T(8,128)(2,1)S(1)}, bf16[128,2048]{1,0:T(8,128)(2,1)S(1)}, u32[]{:S(2)}, u32[]{:S(2)}) collective-permute-start(bf16[128,2048]{1,0:T(8,128)(2,1)S(1)} %get-tuple-element.10), channel_id=1, source_target_pairs={{0,3},{1,0},{2,1},{3,2},{4,7},{5,4},{6,5},{7,6},{8,11},{9,8},{10,9... | collective-permute-start | bytes 1572872 | tf_op jit(solution)/shard_map/ppermute | solution.py:435
  5.4 1.5 %collective-permute-start.2 = (bf16[8,128]{1,0:T(8,128)(2,1)S(1)}, bf16[8,128]{1,0:T(8,128)(2,1)S(1)}, u32[]{:S(2)}, u32[]{:S(2)}) collective-permute-start(bf16[8,128]{1,0:T(8,128)(2,1)S(1)} %get-tuple-element.11), channel_id=1, source_target_pairs={{0,3},{1,0},{2,1},{3,2},{4,7},{5,4},{6,5},{7,6},{8,11},{9,8},{10,9... | collective-permute-start | bytes 6152 | tf_op jit(solution)/shard_map/ppermute | solution.py:436
  6.9 0.0 copy-done
  6.9 0.0 copy-done.1
  7.0 6.9 %inner.1 = (f32[96,256]{1,0:T(8,128)S(1)}, bf16[288,2048]{1,0:T(8,128)(2,1)S(1)}) custom-call(bf16[4,256,2048]{2,1,0:T(8,128)(2,1)} %px_ref.3, bf16[288,256]{1,0:T(8,128)(2,1)S(1)} %copy-done.1, bf16[256,256]{1,0:T(8,128)(2,1)S(1)} %copy-done.2, bf16[64,288]{1,0:T(8,128)(2,1)S(1)} %copy-done.6, bf16[4,1024,256]{2,1,0:T(8,128)(2,1)S(1)} %copy-done), custom_call_target="tpu_custom_call" | custom-call | flops 8000000000 | bytes 8388608 | tf_op jit(solution)/shard_map/inner/pallas_call | solution.py:448
  13.8 3.2 %collective-permute-done.2.extra_ref = bf16[8,128]{1,0:T(8,128)(2,1)S(1)} collective-permute-done((bf16[8,128]{1,0:T(8,128)(2,1)S(1)}, bf16[8,128]{1,0:T(8,128)(2,1)S(1)}, u32[]{:S(2)}, u32[]{:S(2)}) %collective-permute-start.2) | collective-permute-done | bytes 2080 | tf_op jit(solution)/shard_map/ppermute | solution.py:436
  17.1 0.0 collective-permute-done.up_ref
  17.1 0.0 collective-permute-done.1.down_ref
  17.1 2.0 %edge.1 = (f32[8,128]{1,0:T(8,128)S(1)}, bf16[24,128]{1,0:T(8,128)(2,1)S(1)}) custom-call(bf16[128,2048]{1,0:T(8,128)(2,1)S(1)} %collective-permute-done.up_ref, bf16[128,2048]{1,0:T(8,128)(2,1)S(1)} %collective-permute-done.1.down_ref, bf16[8,128]{1,0:T(8,128)(2,1)S(1)} %collective-permute-done.2.extra_ref, ...), custom_call_target="tpu_custom_call" | custom-call | tf_op jit(solution)/shard_map/edge/pallas_call | solution.py:469
  19.1 1.4 %collective-permute-start.3 = (bf16[24,128]{1,0:T(8,128)(2,1)S(1)}, bf16[24,128]{1,0:T(8,128)(2,1)S(1)}, u32[]{:S(2)}, u32[]{:S(2)}) collective-permute-start(bf16[24,128]{1,0:T(8,128)(2,1)S(1)} %get-tuple-element.14), channel_id=1, source_target_pairs={{0,32},{1,33},{2,34},{3,35},{4,36},{5,37},{6,38},{7,39},{8,40},{9,... | collective-permute-start | bytes 18440 | tf_op jit(solution)/shard_map/ppermute | solution.py:388
  20.5 0.0 collective-permute-start.4
  20.5 2.3 %collective-permute-done.3 = bf16[24,128]{1,0:T(8,128)(2,1)S(1)} collective-permute-done((bf16[24,128]{1,0:T(8,128)(2,1)S(1)}, bf16[24,128]{1,0:T(8,128)(2,1)S(1)}, u32[]{:S(2)}, u32[]{:S(2)}) %collective-permute-start.3) | collective-permute-done | bytes 6176 | tf_op jit(solution)/shard_map/ppermute | solution.py:388
  22.8 1.3 %collective-permute-done.4 = bf16[24,128]{1,0:T(8,128)(2,1)S(1)} collective-permute-done((bf16[24,128]{1,0:T(8,128)(2,1)S(1)}, bf16[24,128]{1,0:T(8,128)(2,1)S(1)}, u32[]{:S(2)}, u32[]{:S(2)}) %collective-permute-start.4) | collective-permute-done | bytes 6176 | tf_op jit(solution)/shard_map/ppermute | solution.py:388
  24.1 0.1 collective-permute-start.5
  24.2 1.2 %collective-permute-done.5 = bf16[24,128]{1,0:T(8,128)(2,1)S(1)} collective-permute-done((bf16[24,128]{1,0:T(8,128)(2,1)S(1)}, bf16[24,128]{1,0:T(8,128)(2,1)S(1)}, u32[]{:S(2)}, u32[]{:S(2)}) %collective-permute-start.5) | collective-permute-done | bytes 6176 | tf_op jit(solution)/shard_map/ppermute | solution.py:388
  25.4 1.9 %collective-permute-start.7 = (bf16[2,24,128]{2,1,0:T(8,128)(2,1)S(1)}, bf16[2,24,128]{2,1,0:T(8,128)(2,1)S(1)}, u32[]{:S(2)}, u32[]{:S(2)}) collective-permute-start(bf16[2,24,128]{2,1,0:T(8,128)(2,1)S(1)} %get-tuple-element.19), channel_id=1, source_target_pairs={{0,4},{1,5},{2,6},{3,7},{4,0},{5,1},{6,2},{7,3},{8,16},{9,17},{10,... | collective-permute-start | bytes 36872 | tf_op jit(solution)/shard_map/ppermute | solution.py:388
  27.3 0.0 collective-permute-start.6
  27.3 1.8 %collective-permute-done.7 = bf16[2,24,128]{2,1,0:T(8,128)(2,1)S(1)} collective-permute-done((bf16[2,24,128]{2,1,0:T(8,128)(2,1)S(1)}, bf16[2,24,128]{2,1,0:T(8,128)(2,1)S(1)}, u32[]{:S(2)}, u32[]{:S(2)}) %collective-permute-start.7) | collective-permute-done | bytes 12320 | tf_op jit(solution)/shard_map/ppermute | solution.py:388
  29.1 1.9 %collective-permute-done.6 = bf16[2,24,128]{2,1,0:T(8,128)(2,1)S(1)} collective-permute-done((bf16[2,24,128]{2,1,0:T(8,128)(2,1)S(1)}, bf16[2,24,128]{2,1,0:T(8,128)(2,1)S(1)}, u32[]{:S(2)}, u32[]{:S(2)}) %collective-permute-start.6) | collective-permute-done | bytes 12320 | tf_op jit(solution)/shard_map/ppermute | solution.py:388
  31.0 2.8 %collective-permute-start.10 = (bf16[3,2,24,128]{3,2,1,0:T(8,128)(2,1)S(1)}, bf16[3,2,24,128]{3,2,1,0:T(8,128)(2,1)S(1)}, u32[]{:S(2)}, u32[]{:S(2)}) collective-permute-start(bf16[3,2,24,128]{3,2,1,0:T(8,128)(2,1)S(1)} %get-tuple-element.17), channel_id=1, source_target_pairs={{0,2},{1,3},{2,0},{3,1},{4,6},{5,7},{6,4},{7,5},{8,10},{9,11},{10,... | collective-permute-start | bytes 110600 | tf_op jit(solution)/shard_map/ppermute | solution.py:388
  33.8 1.4 %collective-permute-start.9 = (bf16[3,2,24,128]{3,2,1,0:T(8,128)(2,1)S(1)}, bf16[3,2,24,128]{3,2,1,0:T(8,128)(2,1)S(1)}, u32[]{:S(2)}, u32[]{:S(2)}) collective-permute-start(bf16[3,2,24,128]{3,2,1,0:T(8,128)(2,1)S(1)} %get-tuple-element.17), channel_id=1, source_target_pairs={{0,3},{1,2},{2,1},{3,0},{4,7},{5,6},{6,5},{7,4},{8,11},{9,10},{10,... | collective-permute-start | bytes 110600 | tf_op jit(solution)/shard_map/ppermute | solution.py:388
  35.3 0.0 collective-permute-start.8
  35.3 1.4 %collective-permute-done.10 = bf16[3,2,24,128]{3,2,1,0:T(8,128)(2,1)S(1)} collective-permute-done((bf16[3,2,24,128]{3,2,1,0:T(8,128)(2,1)S(1)}, bf16[3,2,24,128]{3,2,1,0:T(8,128)(2,1)S(1)}, u32[]{:S(2)}, u32[]{:S(2)}) %collective-permute-start.10) | collective-permute-done | bytes 36896 | tf_op jit(solution)/shard_map/ppermute | solution.py:388
  36.7 2.3 %collective-permute-done.9 = bf16[3,2,24,128]{3,2,1,0:T(8,128)(2,1)S(1)} collective-permute-done((bf16[3,2,24,128]{3,2,1,0:T(8,128)(2,1)S(1)}, bf16[3,2,24,128]{3,2,1,0:T(8,128)(2,1)S(1)}, u32[]{:S(2)}, u32[]{:S(2)}) %collective-permute-start.9) | collective-permute-done | bytes 36896 | tf_op jit(solution)/shard_map/ppermute | solution.py:388
  39.0 0.2 collective-permute-done.8
  39.2 2.5 %relax.1 = (f32[4,2,4,32]{3,2,1,0:T(4,128)}, f32[4,2,4,32]{3,2,1,0:T(4,128)}) custom-call(bf16[4,3,2,24,128]{4,3,2,1,0:T(8,128)(2,1)S(1)} %pad_maximum_fusion.got_ref, f32[8,128]{1,0:T(8,128)S(1)} %get-tuple-element.15.own_ref), custom_call_target="tpu_custom_call" | custom-call | tf_op jit(solution)/shard_map/relax/pallas_call | solution.py:493
  (14 shorter events, 0.1 us)
Async XLA Ops:
  0.6 6.3 %copy-start = (bf16[4,1024,256]{2,1,0:T(8,128)(2,1)S(1)}, bf16[4,1024,256]{2,1,0:T(8,128)(2,1)}, u32[]{:S(2)}) copy-start(bf16[4,1024,256]{2,1,0:T(8,128)(2,1)} %constant.51.clone.second_ref) | copy-start | bytes 6291460
  0.6 6.3 %copy-start.1 = (bf16[288,256]{1,0:T(8,128)(2,1)S(1)}, bf16[288,256]{1,0:T(8,128)(2,1)}, u32[]{:S(2)}) copy-start(bf16[288,256]{1,0:T(8,128)(2,1)} %constant.49.clone.rows_ref) | copy-start | bytes 442372
  0.7 6.3 %copy-start.2 = (bf16[256,256]{1,0:T(8,128)(2,1)S(1)}, bf16[256,256]{1,0:T(8,128)(2,1)}, u32[]{:S(2)}) copy-start(bf16[256,256]{1,0:T(8,128)(2,1)} %constant.50.clone.cols_ref) | copy-start | bytes 393220
  0.7 6.3 %copy-start.6 = (bf16[64,288]{1,0:T(8,128)(2,1)S(1)}, bf16[64,288]{1,0:T(8,128)(2,1)}, u32[]{:S(2)}) copy-start(bf16[64,288]{1,0:T(8,128)(2,1)} %constant.52.clone.first_ref) | copy-start | bytes 110596
  2.1 15.0 %collective-permute-start = (bf16[128,2048]{1,0:T(8,128)(2,1)S(1)}, bf16[128,2048]{1,0:T(8,128)(2,1)S(1)}, u32[]{:S(2)}, u32[]{:S(2)}) collective-permute-start(bf16[128,2048]{1,0:T(8,128)(2,1)S(1)} %get-tuple-element.9), channel_id=1, source_target_pairs={{0,1},{1,2},{2,3},{3,0},{4,5},{5,6},{6,7},{7,4},{8,9},{9,10},{10,1... | collective-permute-start | bytes 1572872 | tf_op jit(solution)/shard_map/ppermute | solution.py:434
  3.6 13.4 %collective-permute-start.1 = (bf16[128,2048]{1,0:T(8,128)(2,1)S(1)}, bf16[128,2048]{1,0:T(8,128)(2,1)S(1)}, u32[]{:S(2)}, u32[]{:S(2)}) collective-permute-start(bf16[128,2048]{1,0:T(8,128)(2,1)S(1)} %get-tuple-element.10), channel_id=1, source_target_pairs={{0,3},{1,0},{2,1},{3,2},{4,7},{5,4},{6,5},{7,6},{8,11},{9,8},{10,9... | collective-permute-start | bytes 1572872 | tf_op jit(solution)/shard_map/ppermute | solution.py:435
  5.4 11.7 %copy-start.3 = (s32[4,2,4,32]{3,2,1,0:T(4,128)S(1)}, s32[4,2,4,32]{3,2,1,0:T(4,128)}, u32[]{:S(2)}) copy-start(s32[4,2,4,32]{3,2,1,0:T(4,128)} %offs_ref.3) | copy-start | bytes 12292
  5.4 11.7 %copy-start.4 = (bf16[64,288]{1,0:T(8,128)(2,1)S(1)}, bf16[64,288]{1,0:T(8,128)(2,1)}, u32[]{:S(2)}) copy-start(bf16[64,288]{1,0:T(8,128)(2,1)} %constant.53.clone.first_ref) | copy-start | bytes 110596
  5.4 11.7 %copy-start.5 = (s32[4,4,32]{2,1,0:T(4,128)S(1)}, s32[4,4,32]{2,1,0:T(4,128)}, u32[]{:S(2)}) copy-start(s32[4,4,32]{2,1,0:T(4,128)} %valid_ref.1) | copy-start | bytes 6148
  5.4 11.7 %collective-permute-start.2 = (bf16[8,128]{1,0:T(8,128)(2,1)S(1)}, bf16[8,128]{1,0:T(8,128)(2,1)S(1)}, u32[]{:S(2)}, u32[]{:S(2)}) collective-permute-start(bf16[8,128]{1,0:T(8,128)(2,1)S(1)} %get-tuple-element.11), channel_id=1, source_target_pairs={{0,3},{1,0},{2,1},{3,2},{4,7},{5,4},{6,5},{7,6},{8,11},{9,8},{10,9... | collective-permute-start | bytes 6152 | tf_op jit(solution)/shard_map/ppermute | solution.py:436
  19.1 3.7 %collective-permute-start.3 = (bf16[24,128]{1,0:T(8,128)(2,1)S(1)}, bf16[24,128]{1,0:T(8,128)(2,1)S(1)}, u32[]{:S(2)}, u32[]{:S(2)}) collective-permute-start(bf16[24,128]{1,0:T(8,128)(2,1)S(1)} %get-tuple-element.14), channel_id=1, source_target_pairs={{0,32},{1,33},{2,34},{3,35},{4,36},{5,37},{6,38},{7,39},{8,40},{9,... | collective-permute-start | bytes 18440 | tf_op jit(solution)/shard_map/ppermute | solution.py:388
  20.5 3.6 %collective-permute-start.4 = (bf16[24,128]{1,0:T(8,128)(2,1)S(1)}, bf16[24,128]{1,0:T(8,128)(2,1)S(1)}, u32[]{:S(2)}, u32[]{:S(2)}) collective-permute-start(bf16[24,128]{1,0:T(8,128)(2,1)S(1)} %get-tuple-element.14), channel_id=1, source_target_pairs={{0,4},{1,5},{2,6},{3,7},{4,0},{5,1},{6,2},{7,3},{8,12},{9,13},{10,... | collective-permute-start | bytes 18440 | tf_op jit(solution)/shard_map/ppermute | solution.py:388
  24.1 1.2 %collective-permute-start.5 = (bf16[24,128]{1,0:T(8,128)(2,1)S(1)}, bf16[24,128]{1,0:T(8,128)(2,1)S(1)}, u32[]{:S(2)}, u32[]{:S(2)}) collective-permute-start(bf16[24,128]{1,0:T(8,128)(2,1)S(1)} %fusion.1), channel_id=1, source_target_pairs={{0,4},{1,5},{2,6},{3,7},{4,0},{5,1},{6,2},{7,3},{8,12},{9,13},{10,... | collective-permute-start | bytes 18440 | tf_op jit(solution)/shard_map/ppermute | solution.py:388
  25.4 3.7 %collective-permute-start.7 = (bf16[2,24,128]{2,1,0:T(8,128)(2,1)S(1)}, bf16[2,24,128]{2,1,0:T(8,128)(2,1)S(1)}, u32[]{:S(2)}, u32[]{:S(2)}) collective-permute-start(bf16[2,24,128]{2,1,0:T(8,128)(2,1)S(1)} %get-tuple-element.19), channel_id=1, source_target_pairs={{0,4},{1,5},{2,6},{3,7},{4,0},{5,1},{6,2},{7,3},{8,16},{9,17},{10,... | collective-permute-start | bytes 36872 | tf_op jit(solution)/shard_map/ppermute | solution.py:388
  27.3 3.7 %collective-permute-start.6 = (bf16[2,24,128]{2,1,0:T(8,128)(2,1)S(1)}, bf16[2,24,128]{2,1,0:T(8,128)(2,1)S(1)}, u32[]{:S(2)}, u32[]{:S(2)}) collective-permute-start(bf16[2,24,128]{2,1,0:T(8,128)(2,1)S(1)} %get-tuple-element.19), channel_id=1, source_target_pairs={{0,8},{1,9},{2,10},{3,11},{4,12},{5,13},{6,14},{7,15},{8,0},{9,1},... | collective-permute-start | bytes 36872 | tf_op jit(solution)/shard_map/ppermute | solution.py:388
  31.0 5.6 %collective-permute-start.10 = (bf16[3,2,24,128]{3,2,1,0:T(8,128)(2,1)S(1)}, bf16[3,2,24,128]{3,2,1,0:T(8,128)(2,1)S(1)}, u32[]{:S(2)}, u32[]{:S(2)}) collective-permute-start(bf16[3,2,24,128]{3,2,1,0:T(8,128)(2,1)S(1)} %get-tuple-element.17), channel_id=1, source_target_pairs={{0,2},{1,3},{2,0},{3,1},{4,6},{5,7},{6,4},{7,5},{8,10},{9,11},{10,... | collective-permute-start | bytes 110600 | tf_op jit(solution)/shard_map/ppermute | solution.py:388
  33.8 5.2 %collective-permute-start.9 = (bf16[3,2,24,128]{3,2,1,0:T(8,128)(2,1)S(1)}, bf16[3,2,24,128]{3,2,1,0:T(8,128)(2,1)S(1)}, u32[]{:S(2)}, u32[]{:S(2)}) collective-permute-start(bf16[3,2,24,128]{3,2,1,0:T(8,128)(2,1)S(1)} %get-tuple-element.17), channel_id=1, source_target_pairs={{0,3},{1,2},{2,1},{3,0},{4,7},{5,6},{6,5},{7,4},{8,11},{9,10},{10,... | collective-permute-start | bytes 110600 | tf_op jit(solution)/shard_map/ppermute | solution.py:388
  35.3 4.0 %collective-permute-start.8 = (bf16[3,2,24,128]{3,2,1,0:T(8,128)(2,1)S(1)}, bf16[3,2,24,128]{3,2,1,0:T(8,128)(2,1)S(1)}, u32[]{:S(2)}, u32[]{:S(2)}) collective-permute-start(bf16[3,2,24,128]{3,2,1,0:T(8,128)(2,1)S(1)} %get-tuple-element.17), channel_id=1, source_target_pairs={{0,1},{1,0},{2,3},{3,2},{4,5},{5,4},{6,7},{7,6},{8,9},{9,8},{10,11... | collective-permute-start | bytes 110600 | tf_op jit(solution)/shard_map/ppermute | solution.py:388

commit v4 on v3

--- a/solution.py
+++ b/solution.py
@@ -260,7 +260,7 @@
     load_ref[...] = packed[...].astype(BF)
 
 
-def relax_kernel(got_ref, own_ref, flow_out, mesh_out, raw, flow, coef, state, speed):
+def relax_kernel(got_ref, own_ref, flow_out, mesh_out, raw, flow, coef, state):
     gx, gy, sa = [lax.axis_index(a) for a in AXES]
     nx, ny, ns = [lax.axis_size(a) for a in AXES]
     shape = (24, 128)
@@ -294,6 +294,16 @@
     degree = 4.0 - edges
     zero = jnp.zeros(shape, F32)
 
+    blank = (0, 1, ns + 2, ns + 3)
+    for k in blank:
+        for i in range(2):
+            for c in range(2):
+                state[0, c, i, k] = zero
+                state[1, c, i, k] = zero
+            if k in (1, ns + 2):
+                for c in range(5):
+                    coef[c, i, k] = zero
+
     swapped = (row % PR >= 2) & low
     for c in range(2):
         carry = zero
@@ -305,61 +315,78 @@
             pair = even + odd
             turned = pltpu.roll(pair, 64, 1)
             even = even + jnp.where(low, 0.0, turned) + carry
-            state[0, c, 0, k] = even
-            state[0, c, 1, k] = even + odd
+            odd = even + odd
+            for old in range(2):
+                state[old, c, 0, k + 2] = even
+                state[old, c, 1, k + 2] = odd
             carry = carry + pair + turned
-            speed[c, 0, k] = zero
-            speed[c, 1, k] = zero
-
-    def below(get, i, k):
-        if i == 1:
-            return get(0, k)
-        return pltpu.roll(jnp.where(low, get(1, k), get(1, k - 1) if k else 0.0), 64, 1)
-
-    def above(get, i, k):
-        if i == 0:
-            return get(1, k)
-        return pltpu.roll(jnp.where(low, get(0, k + 1) if k + 1 < ns else 0.0, get(0, k)), 64, 1)
+
+    def turn(array):
+        return pltpu.roll(array, 64, 1)
 
     plane = inside * (step_size * spring_plane)
     stack = inside * (step_size * spring_stack)
-    for i in range(2):
-        for k in range(ns):
-            w = raw[2, i, k] * stack
-            w_next = above(lambda i, k: raw[2, i, k], i, k) * stack
-            coef[0, i, k] = w
-            coef[1, i, k] = w_next
-            coef[2, i, k] = degree * plane + w + w_next
-            for c in range(2):
-                get = lambda i, k: flow[c, i, k]
-                coef[3 + c, i, k] = w * get(i, k) - w_next * above(get, i, k)
-
-    def advance(src, dst):
+    for k in range(ns):
+        weights = [raw[2, i, k] * stack for i in range(2)]
+        later = raw[2, 0, k + 1] * stack if k + 1 < ns else 0.0
+        nexts = [weights[1], turn(jnp.where(low, later, weights[0]))]
+        for i in range(2):
+            coef[0, i, k + 2] = weights[i]
+            coef[1, i, k + 2] = nexts[i]
+            coef[2, i, k + 2] = 1.0 + damping - degree * plane - weights[i] - nexts[i]
         for c in range(2):
-            get = lambda i, k: state[src, c, i, k]
+            later = flow[c, 0, k + 1] if k + 1 < ns else 0.0
+            ahead = [flow[c, 1, k], turn(jnp.where(low, later, flow[c, 0, k]))]
+            for i in range(2):
+                coef[3 + c, i, k + 2] = weights[i] * flow[c, i, k] - nexts[i] * ahead[i]
+
+    def advance(step, c, k):
+        src, dst = (step + 1) % 2, step % 2
+        top = 8 if step == RELAX else 0
+        end = 24 if step < 4 else 16
+        rows, read = slice(top, end), slice(0, end)
+        now = [state[src, c, i, k, read] for i in range(2)]
+        here = [m[rows] for m in now]
+        edge = low[rows]
+        behind = [
+            turn(jnp.where(edge, here[1], state[src, c, 1, k - 1, rows])),
+            here[0],
+        ]
+        ahead = [
+            here[1],
+            turn(jnp.where(edge, state[src, c, 0, k + 1, rows], here[0])),
+        ]
+        done = []
+        for i in range(2):
+            around = pltpu.roll(here[i], 1, 1) + pltpu.roll(here[i], 127, 1)
+            around += pltpu.roll(now[i], 1, 0)[rows]
+            if step == 4:
+                around += pltpu.roll(state[src, c, i, k], 23, 0)[rows]
+            else:
+                around += pltpu.roll(now[i], end - 1, 0)[rows]
+            m = coef[2, i, k, rows] * here[i] - damping * state[dst, c, i, k, rows]
+            m += plane[rows] * around + coef[3 + c, i, k, rows]
+            m += coef[0, i, k, rows] * behind[i] + coef[1, i, k, rows] * ahead[i]
+            if step < RELAX:
+                state[dst, c, i, k, rows] = m
+            done.append(m)
+        return done
+
+    for step in range(1, 4):
+        for c in range(2):
             for k in range(ns):
-                for i in range(2):
-                    m = get(i, k)
-                    around = pltpu.roll(m, 1, 1) + pltpu.roll(m, 127, 1)
-                    around += pltpu.roll(m, 1, 0) + pltpu.roll(m, 23, 0)
-                    v = damping * speed[c, i, k] - coef[2, i, k] * m + plane * around
-                    v += coef[0, i, k] * below(get, i, k) + coef[1, i, k] * above(get, i, k)
-                    v += coef[3 + c, i, k]
-                    speed[c, i, k] = v
-                    state[dst, c, i, k] = m + v
-
-    def two(step, unused):
-        advance(0, 1)
-        advance(1, 0)
-        return unused
-
-    lax.fori_loop(0, RELAX // 2, two, 0)
+                advance(step, c, k + 2)
+    for step in range(4, RELAX):
+        for c in range(2):
+            for d in range(3):
+                advance(step, c, sa + d + 1)
     mine = slice(2 * PR, 3 * PR)
     late = lax.broadcasted_iota(jnp.int32, (PR, 32), 0) >= 2
     for c in range(2):
+        final = advance(RELAX, c, sa + 2)
         for s in range(4):
             lanes = slice((s // 2) * 64 + 16, (s // 2) * 64 + 48)
-            mesh_out[s, c] = state[0, c, s % 2, sa][mine, lanes]
+            mesh_out[s, c] = final[s % 2][:PR, lanes]
             f = own_ref[c * PR : (c + 1) * PR, s * 32 : (s + 1) * 32]
             if s == 0:
                 f = jnp.where(late, flow[c, 0, sa][mine, lanes], f)
@@ -498,9 +525,8 @@
         scratch_shapes=[
             pltpu.VMEM((3,) + stack, F32),
             pltpu.VMEM((2,) + stack, F32),
-            pltpu.VMEM((5,) + stack, F32),
-            pltpu.VMEM((2, 2) + stack, F32),
-            pltpu.VMEM((2,) + stack, F32),
+            pltpu.VMEM((5, 2, size + 4, 24, 128), F32),
+            pltpu.VMEM((2, 2, 2, size + 4, 24, 128), F32),
         ],
         compiler_params=pltpu.CompilerParams(vmem_limit_bytes=GRANT),
         name="relax",

time: 41.9 us -> 41.4 us (0.988)
  Pallas kernels: 12.8 us -> 12.2 us
    pallas_call x1, Pallas kernels: 2.52 us -> 1.96 us  [per_device(): pl.pallas_call(relax_kernel, in_specs=[vmem(), vmem()], out_specs=[vmem()...]
  transfers between devices with their start and end apart: 11 -> 11, of which waited for: 9 -> 9; matrix products, arithmetic and copies ran while one was open for 0% -> 0% of each run, Pallas kernels for 16% -> 17%
where the time goes in v4:
time: 41.4 us; the launch traced here: 41.2 us
  waiting for transfers between devices  15.7 us (38%)
  starting transfers between devices  12.5 us (30%)
  Pallas kernels  12.2 us (29%)
  between operations  0.75 us (2%)
    ppermute x8, waiting for transfers between devices, trade(): return lax.ppermute(array, AXES, route)  12.4 us
    ppermute x8, starting transfers between devices, trade(): return lax.ppermute(array, AXES, route)  7.62 us
    pallas_call x1, Pallas kernels, per_device(): pl.pallas_call(inner_kernel, grid=(blocks,), in_specs=[pl.BlockSpec((coun...  6.87 us
    ppermute x1, waiting for transfers between devices, per_device(): extra = lax.ppermute(extra, 'sa', sink)  3.23 us
    pallas_call x1, Pallas kernels, per_device(): pl.pallas_call(edge_kernel, in_specs=[vmem()] * 11, out_specs=[vmem(), vm...  2.02 us
    pallas_call x1, Pallas kernels, per_device(): pl.pallas_call(relax_kernel, in_specs=[vmem(), vmem()], out_specs=[vmem()...  1.96 us
    ppermute x1, starting transfers between devices, per_device(): down = lax.ppermute(down, 'sa', sink)  1.75 us
    ppermute x1, starting transfers between devices, per_device(): up = lax.ppermute(up, 'sa', rise)  1.56 us
  transfers between devices with their start and end apart: 11, of which 9 were waited for; matrix products, arithmetic and copies ran while one was open for 0% of the time, Pallas kernels for 17%

profile of v4, /device:TPU:48, one launch (start us, length us, event | category | flops | bytes accessed | tf_op | source)
XLA Modules:
  0.0 41.2 jit_solution(15660824581223985140)
XLA Ops:
  0.6 0.0 copy-start
  0.6 0.0 copy-start.1
  0.7 0.0 copy-start.2
  0.7 0.0 copy-start.6
  0.7 1.4 %send.1 = (bf16[128,2048]{1,0:T(8,128)(2,1)S(1)}, bf16[128,2048]{1,0:T(8,128)(2,1)S(1)}, bf16[8,128]{1,0:T(8,128)(2,1)S(1)}) custom-call(bf16[4,256,2048]{2,1,0:T(8,128)(2,1)} %px_ref.3, s32[4,2,4,32]{3,2,1,0:T(4,128)} %offs_ref.3), custom_call_target="tpu_custom_call" | custom-call | tf_op jit(solution)/shard_map/send/pallas_call | solution.py:442
  2.1 1.6 %collective-permute-start = (bf16[128,2048]{1,0:T(8,128)(2,1)S(1)}, bf16[128,2048]{1,0:T(8,128)(2,1)S(1)}, u32[]{:S(2)}, u32[]{:S(2)}) collective-permute-start(bf16[128,2048]{1,0:T(8,128)(2,1)S(1)} %get-tuple-element.9), channel_id=1, source_target_pairs={{0,1},{1,2},{2,3},{3,0},{4,5},{5,6},{6,7},{7,4},{8,9},{9,10},{10,1... | collective-permute-start | bytes 1572872 | tf_op jit(solution)/shard_map/ppermute | solution.py:461
  3.6 1.7 %collective-permute-start.1 = (bf16[128,2048]{1,0:T(8,128)(2,1)S(1)}, bf16[128,2048]{1,0:T(8,128)(2,1)S(1)}, u32[]{:S(2)}, u32[]{:S(2)}) collective-permute-start(bf16[128,2048]{1,0:T(8,128)(2,1)S(1)} %get-tuple-element.10), channel_id=1, source_target_pairs={{0,3},{1,0},{2,1},{3,2},{4,7},{5,4},{6,5},{7,6},{8,11},{9,8},{10,9... | collective-permute-start | bytes 1572872 | tf_op jit(solution)/shard_map/ppermute | solution.py:462
  5.4 1.5 %collective-permute-start.2 = (bf16[8,128]{1,0:T(8,128)(2,1)S(1)}, bf16[8,128]{1,0:T(8,128)(2,1)S(1)}, u32[]{:S(2)}, u32[]{:S(2)}) collective-permute-start(bf16[8,128]{1,0:T(8,128)(2,1)S(1)} %get-tuple-element.11), channel_id=1, source_target_pairs={{0,3},{1,0},{2,1},{3,2},{4,7},{5,4},{6,5},{7,6},{8,11},{9,8},{10,9... | collective-permute-start | bytes 6152 | tf_op jit(solution)/shard_map/ppermute | solution.py:463
  6.9 0.0 copy-done
  6.9 0.0 copy-done.1
  7.0 6.9 %inner.1 = (f32[96,256]{1,0:T(8,128)S(1)}, bf16[288,2048]{1,0:T(8,128)(2,1)S(1)}) custom-call(bf16[4,256,2048]{2,1,0:T(8,128)(2,1)} %px_ref.3, bf16[288,256]{1,0:T(8,128)(2,1)S(1)} %copy-done.1, bf16[256,256]{1,0:T(8,128)(2,1)S(1)} %copy-done.2, bf16[64,288]{1,0:T(8,128)(2,1)S(1)} %copy-done.6, bf16[4,1024,256]{2,1,0:T(8,128)(2,1)S(1)} %copy-done), custom_call_target="tpu_custom_call" | custom-call | flops 8000000000 | bytes 8388608 | tf_op jit(solution)/shard_map/inner/pallas_call | solution.py:475
  13.8 3.2 %collective-permute-done.2.extra_ref = bf16[8,128]{1,0:T(8,128)(2,1)S(1)} collective-permute-done((bf16[8,128]{1,0:T(8,128)(2,1)S(1)}, bf16[8,128]{1,0:T(8,128)(2,1)S(1)}, u32[]{:S(2)}, u32[]{:S(2)}) %collective-permute-start.2) | collective-permute-done | bytes 2080 | tf_op jit(solution)/shard_map/ppermute | solution.py:463
  17.1 0.0 collective-permute-done.up_ref
  17.1 0.0 collective-permute-done.1.down_ref
  17.1 2.0 %edge.1 = (f32[8,128]{1,0:T(8,128)S(1)}, bf16[24,128]{1,0:T(8,128)(2,1)S(1)}) custom-call(bf16[128,2048]{1,0:T(8,128)(2,1)S(1)} %collective-permute-done.up_ref, bf16[128,2048]{1,0:T(8,128)(2,1)S(1)} %collective-permute-done.1.down_ref, bf16[8,128]{1,0:T(8,128)(2,1)S(1)} %collective-permute-done.2.extra_ref, ...), custom_call_target="tpu_custom_call" | custom-call | tf_op jit(solution)/shard_map/edge/pallas_call | solution.py:496
  19.1 1.4 %collective-permute-start.3 = (bf16[24,128]{1,0:T(8,128)(2,1)S(1)}, bf16[24,128]{1,0:T(8,128)(2,1)S(1)}, u32[]{:S(2)}, u32[]{:S(2)}) collective-permute-start(bf16[24,128]{1,0:T(8,128)(2,1)S(1)} %get-tuple-element.14), channel_id=1, source_target_pairs={{0,32},{1,33},{2,34},{3,35},{4,36},{5,37},{6,38},{7,39},{8,40},{9,... | collective-permute-start | bytes 18440 | tf_op jit(solution)/shard_map/ppermute | solution.py:415
  20.5 0.0 collective-permute-start.4
  20.5 2.3 %collective-permute-done.3 = bf16[24,128]{1,0:T(8,128)(2,1)S(1)} collective-permute-done((bf16[24,128]{1,0:T(8,128)(2,1)S(1)}, bf16[24,128]{1,0:T(8,128)(2,1)S(1)}, u32[]{:S(2)}, u32[]{:S(2)}) %collective-permute-start.3) | collective-permute-done | bytes 6176 | tf_op jit(solution)/shard_map/ppermute | solution.py:415
  22.8 1.3 %collective-permute-done.4 = bf16[24,128]{1,0:T(8,128)(2,1)S(1)} collective-permute-done((bf16[24,128]{1,0:T(8,128)(2,1)S(1)}, bf16[24,128]{1,0:T(8,128)(2,1)S(1)}, u32[]{:S(2)}, u32[]{:S(2)}) %collective-permute-start.4) | collective-permute-done | bytes 6176 | tf_op jit(solution)/shard_map/ppermute | solution.py:415
  24.1 0.1 collective-permute-start.5
  24.2 1.2 %collective-permute-done.5 = bf16[24,128]{1,0:T(8,128)(2,1)S(1)} collective-permute-done((bf16[24,128]{1,0:T(8,128)(2,1)S(1)}, bf16[24,128]{1,0:T(8,128)(2,1)S(1)}, u32[]{:S(2)}, u32[]{:S(2)}) %collective-permute-start.5) | collective-permute-done | bytes 6176 | tf_op jit(solution)/shard_map/ppermute | solution.py:415
  25.4 1.9 %collective-permute-start.7 = (bf16[2,24,128]{2,1,0:T(8,128)(2,1)S(1)}, bf16[2,24,128]{2,1,0:T(8,128)(2,1)S(1)}, u32[]{:S(2)}, u32[]{:S(2)}) collective-permute-start(bf16[2,24,128]{2,1,0:T(8,128)(2,1)S(1)} %get-tuple-element.19), channel_id=1, source_target_pairs={{0,4},{1,5},{2,6},{3,7},{4,0},{5,1},{6,2},{7,3},{8,16},{9,17},{10,... | collective-permute-start | bytes 36872 | tf_op jit(solution)/shard_map/ppermute | solution.py:415
  27.3 0.0 collective-permute-start.6
  27.3 1.8 %collective-permute-done.7 = bf16[2,24,128]{2,1,0:T(8,128)(2,1)S(1)} collective-permute-done((bf16[2,24,128]{2,1,0:T(8,128)(2,1)S(1)}, bf16[2,24,128]{2,1,0:T(8,128)(2,1)S(1)}, u32[]{:S(2)}, u32[]{:S(2)}) %collective-permute-start.7) | collective-permute-done | bytes 12320 | tf_op jit(solution)/shard_map/ppermute | solution.py:415
  29.1 1.9 %collective-permute-done.6 = bf16[2,24,128]{2,1,0:T(8,128)(2,1)S(1)} collective-permute-done((bf16[2,24,128]{2,1,0:T(8,128)(2,1)S(1)}, bf16[2,24,128]{2,1,0:T(8,128)(2,1)S(1)}, u32[]{:S(2)}, u32[]{:S(2)}) %collective-permute-start.6) | collective-permute-done | bytes 12320 | tf_op jit(solution)/shard_map/ppermute | solution.py:415
  31.0 2.8 %collective-permute-start.10 = (bf16[3,2,24,128]{3,2,1,0:T(8,128)(2,1)S(1)}, bf16[3,2,24,128]{3,2,1,0:T(8,128)(2,1)S(1)}, u32[]{:S(2)}, u32[]{:S(2)}) collective-permute-start(bf16[3,2,24,128]{3,2,1,0:T(8,128)(2,1)S(1)} %get-tuple-element.17), channel_id=1, source_target_pairs={{0,2},{1,3},{2,0},{3,1},{4,6},{5,7},{6,4},{7,5},{8,10},{9,11},{10,... | collective-permute-start | bytes 110600 | tf_op jit(solution)/shard_map/ppermute | solution.py:415
  33.8 1.4 %collective-permute-start.9 = (bf16[3,2,24,128]{3,2,1,0:T(8,128)(2,1)S(1)}, bf16[3,2,24,128]{3,2,1,0:T(8,128)(2,1)S(1)}, u32[]{:S(2)}, u32[]{:S(2)}) collective-permute-start(bf16[3,2,24,128]{3,2,1,0:T(8,128)(2,1)S(1)} %get-tuple-element.17), channel_id=1, source_target_pairs={{0,3},{1,2},{2,1},{3,0},{4,7},{5,6},{6,5},{7,4},{8,11},{9,10},{10,... | collective-permute-start | bytes 110600 | tf_op jit(solution)/shard_map/ppermute | solution.py:415
  35.3 0.0 collective-permute-start.8
  35.3 1.4 %collective-permute-done.10 = bf16[3,2,24,128]{3,2,1,0:T(8,128)(2,1)S(1)} collective-permute-done((bf16[3,2,24,128]{3,2,1,0:T(8,128)(2,1)S(1)}, bf16[3,2,24,128]{3,2,1,0:T(8,128)(2,1)S(1)}, u32[]{:S(2)}, u32[]{:S(2)}) %collective-permute-start.10) | collective-permute-done | bytes 36896 | tf_op jit(solution)/shard_map/ppermute | solution.py:415
  36.7 2.3 %collective-permute-done.9 = bf16[3,2,24,128]{3,2,1,0:T(8,128)(2,1)S(1)} collective-permute-done((bf16[3,2,24,128]{3,2,1,0:T(8,128)(2,1)S(1)}, bf16[3,2,24,128]{3,2,1,0:T(8,128)(2,1)S(1)}, u32[]{:S(2)}, u32[]{:S(2)}) %collective-permute-start.9) | collective-permute-done | bytes 36896 | tf_op jit(solution)/shard_map/ppermute | solution.py:415
  39.0 0.2 collective-permute-done.8
  39.2 2.0 %relax.1 = (f32[4,2,4,32]{3,2,1,0:T(4,128)}, f32[4,2,4,32]{3,2,1,0:T(4,128)}) custom-call(bf16[4,3,2,24,128]{4,3,2,1,0:T(8,128)(2,1)S(1)} %pad_maximum_fusion.got_ref, f32[8,128]{1,0:T(8,128)S(1)} %get-tuple-element.15.own_ref), custom_call_target="tpu_custom_call" | custom-call | tf_op jit(solution)/shard_map/relax/pallas_call | solution.py:520
  (14 shorter events, 0.1 us)
Async XLA Ops:
  0.6 6.3 %copy-start = (bf16[4,1024,256]{2,1,0:T(8,128)(2,1)S(1)}, bf16[4,1024,256]{2,1,0:T(8,128)(2,1)}, u32[]{:S(2)}) copy-start(bf16[4,1024,256]{2,1,0:T(8,128)(2,1)} %constant.51.clone.second_ref) | copy-start | bytes 6291460
  0.6 6.3 %copy-start.1 = (bf16[288,256]{1,0:T(8,128)(2,1)S(1)}, bf16[288,256]{1,0:T(8,128)(2,1)}, u32[]{:S(2)}) copy-start(bf16[288,256]{1,0:T(8,128)(2,1)} %constant.49.clone.rows_ref) | copy-start | bytes 442372
  0.7 6.3 %copy-start.2 = (bf16[256,256]{1,0:T(8,128)(2,1)S(1)}, bf16[256,256]{1,0:T(8,128)(2,1)}, u32[]{:S(2)}) copy-start(bf16[256,256]{1,0:T(8,128)(2,1)} %constant.50.clone.cols_ref) | copy-start | bytes 393220
  0.7 6.3 %copy-start.6 = (bf16[64,288]{1,0:T(8,128)(2,1)S(1)}, bf16[64,288]{1,0:T(8,128)(2,1)}, u32[]{:S(2)}) copy-start(bf16[64,288]{1,0:T(8,128)(2,1)} %constant.52.clone.first_ref) | copy-start | bytes 110596
  2.1 15.0 %collective-permute-start = (bf16[128,2048]{1,0:T(8,128)(2,1)S(1)}, bf16[128,2048]{1,0:T(8,128)(2,1)S(1)}, u32[]{:S(2)}, u32[]{:S(2)}) collective-permute-start(bf16[128,2048]{1,0:T(8,128)(2,1)S(1)} %get-tuple-element.9), channel_id=1, source_target_pairs={{0,1},{1,2},{2,3},{3,0},{4,5},{5,6},{6,7},{7,4},{8,9},{9,10},{10,1... | collective-permute-start | bytes 1572872 | tf_op jit(solution)/shard_map/ppermute | solution.py:461
  3.6 13.4 %collective-permute-start.1 = (bf16[128,2048]{1,0:T(8,128)(2,1)S(1)}, bf16[128,2048]{1,0:T(8,128)(2,1)S(1)}, u32[]{:S(2)}, u32[]{:S(2)}) collective-permute-start(bf16[128,2048]{1,0:T(8,128)(2,1)S(1)} %get-tuple-element.10), channel_id=1, source_target_pairs={{0,3},{1,0},{2,1},{3,2},{4,7},{5,4},{6,5},{7,6},{8,11},{9,8},{10,9... | collective-permute-start | bytes 1572872 | tf_op jit(solution)/shard_map/ppermute | solution.py:462
  5.4 11.7 %copy-start.3 = (s32[4,2,4,32]{3,2,1,0:T(4,128)S(1)}, s32[4,2,4,32]{3,2,1,0:T(4,128)}, u32[]{:S(2)}) copy-start(s32[4,2,4,32]{3,2,1,0:T(4,128)} %offs_ref.3) | copy-start | bytes 12292
  5.4 11.7 %copy-start.4 = (bf16[64,288]{1,0:T(8,128)(2,1)S(1)}, bf16[64,288]{1,0:T(8,128)(2,1)}, u32[]{:S(2)}) copy-start(bf16[64,288]{1,0:T(8,128)(2,1)} %constant.53.clone.first_ref) | copy-start | bytes 110596
  5.4 11.7 %copy-start.5 = (s32[4,4,32]{2,1,0:T(4,128)S(1)}, s32[4,4,32]{2,1,0:T(4,128)}, u32[]{:S(2)}) copy-start(s32[4,4,32]{2,1,0:T(4,128)} %valid_ref.1) | copy-start | bytes 6148
  5.4 11.7 %collective-permute-start.2 = (bf16[8,128]{1,0:T(8,128)(2,1)S(1)}, bf16[8,128]{1,0:T(8,128)(2,1)S(1)}, u32[]{:S(2)}, u32[]{:S(2)}) collective-permute-start(bf16[8,128]{1,0:T(8,128)(2,1)S(1)} %get-tuple-element.11), channel_id=1, source_target_pairs={{0,3},{1,0},{2,1},{3,2},{4,7},{5,4},{6,5},{7,6},{8,11},{9,8},{10,9... | collective-permute-start | bytes 6152 | tf_op jit(solution)/shard_map/ppermute | solution.py:463
  19.1 3.7 %collective-permute-start.3 = (bf16[24,128]{1,0:T(8,128)(2,1)S(1)}, bf16[24,128]{1,0:T(8,128)(2,1)S(1)}, u32[]{:S(2)}, u32[]{:S(2)}) collective-permute-start(bf16[24,128]{1,0:T(8,128)(2,1)S(1)} %get-tuple-element.14), channel_id=1, source_target_pairs={{0,32},{1,33},{2,34},{3,35},{4,36},{5,37},{6,38},{7,39},{8,40},{9,... | collective-permute-start | bytes 18440 | tf_op jit(solution)/shard_map/ppermute | solution.py:415
  20.5 3.6 %collective-permute-start.4 = (bf16[24,128]{1,0:T(8,128)(2,1)S(1)}, bf16[24,128]{1,0:T(8,128)(2,1)S(1)}, u32[]{:S(2)}, u32[]{:S(2)}) collective-permute-start(bf16[24,128]{1,0:T(8,128)(2,1)S(1)} %get-tuple-element.14), channel_id=1, source_target_pairs={{0,4},{1,5},{2,6},{3,7},{4,0},{5,1},{6,2},{7,3},{8,12},{9,13},{10,... | collective-permute-start | bytes 18440 | tf_op jit(solution)/shard_map/ppermute | solution.py:415
  24.1 1.2 %collective-permute-start.5 = (bf16[24,128]{1,0:T(8,128)(2,1)S(1)}, bf16[24,128]{1,0:T(8,128)(2,1)S(1)}, u32[]{:S(2)}, u32[]{:S(2)}) collective-permute-start(bf16[24,128]{1,0:T(8,128)(2,1)S(1)} %fusion.1), channel_id=1, source_target_pairs={{0,4},{1,5},{2,6},{3,7},{4,0},{5,1},{6,2},{7,3},{8,12},{9,13},{10,... | collective-permute-start | bytes 18440 | tf_op jit(solution)/shard_map/ppermute | solution.py:415
  25.4 3.7 %collective-permute-start.7 = (bf16[2,24,128]{2,1,0:T(8,128)(2,1)S(1)}, bf16[2,24,128]{2,1,0:T(8,128)(2,1)S(1)}, u32[]{:S(2)}, u32[]{:S(2)}) collective-permute-start(bf16[2,24,128]{2,1,0:T(8,128)(2,1)S(1)} %get-tuple-element.19), channel_id=1, source_target_pairs={{0,4},{1,5},{2,6},{3,7},{4,0},{5,1},{6,2},{7,3},{8,16},{9,17},{10,... | collective-permute-start | bytes 36872 | tf_op jit(solution)/shard_map/ppermute | solution.py:415
  27.3 3.7 %collective-permute-start.6 = (bf16[2,24,128]{2,1,0:T(8,128)(2,1)S(1)}, bf16[2,24,128]{2,1,0:T(8,128)(2,1)S(1)}, u32[]{:S(2)}, u32[]{:S(2)}) collective-permute-start(bf16[2,24,128]{2,1,0:T(8,128)(2,1)S(1)} %get-tuple-element.19), channel_id=1, source_target_pairs={{0,8},{1,9},{2,10},{3,11},{4,12},{5,13},{6,14},{7,15},{8,0},{9,1},... | collective-permute-start | bytes 36872 | tf_op jit(solution)/shard_map/ppermute | solution.py:415
  31.0 5.6 %collective-permute-start.10 = (bf16[3,2,24,128]{3,2,1,0:T(8,128)(2,1)S(1)}, bf16[3,2,24,128]{3,2,1,0:T(8,128)(2,1)S(1)}, u32[]{:S(2)}, u32[]{:S(2)}) collective-permute-start(bf16[3,2,24,128]{3,2,1,0:T(8,128)(2,1)S(1)} %get-tuple-element.17), channel_id=1, source_target_pairs={{0,2},{1,3},{2,0},{3,1},{4,6},{5,7},{6,4},{7,5},{8,10},{9,11},{10,... | collective-permute-start | bytes 110600 | tf_op jit(solution)/shard_map/ppermute | solution.py:415
  33.8 5.2 %collective-permute-start.9 = (bf16[3,2,24,128]{3,2,1,0:T(8,128)(2,1)S(1)}, bf16[3,2,24,128]{3,2,1,0:T(8,128)(2,1)S(1)}, u32[]{:S(2)}, u32[]{:S(2)}) collective-permute-start(bf16[3,2,24,128]{3,2,1,0:T(8,128)(2,1)S(1)} %get-tuple-element.17), channel_id=1, source_target_pairs={{0,3},{1,2},{2,1},{3,0},{4,7},{5,6},{6,5},{7,4},{8,11},{9,10},{10,... | collective-permute-start | bytes 110600 | tf_op jit(solution)/shard_map/ppermute | solution.py:415
  35.3 4.0 %collective-permute-start.8 = (bf16[3,2,24,128]{3,2,1,0:T(8,128)(2,1)S(1)}, bf16[3,2,24,128]{3,2,1,0:T(8,128)(2,1)S(1)}, u32[]{:S(2)}, u32[]{:S(2)}) collective-permute-start(bf16[3,2,24,128]{3,2,1,0:T(8,128)(2,1)S(1)} %get-tuple-element.17), channel_id=1, source_target_pairs={{0,1},{1,0},{2,3},{3,2},{4,5},{5,4},{6,7},{7,6},{8,9},{9,8},{10,11... | collective-permute-start | bytes 110600 | tf_op jit(solution)/shard_map/ppermute | solution.py:415

commit v5 on v4

--- a/solution.py
+++ b/solution.py
@@ -148,7 +148,42 @@
     return out
 
 
-def inner_kernel(px_ref, rows_ref, cols_ref, first_ref, second_ref, corr_ref, mix_ref):
+def pick(pieces, offset):
+    value = pieces[0]
+    for i in range(1, 5):
+        value = jnp.where(offset == i - 2, pieces[i], value)
+    return value
+
+
+def peak_step(low, center, high):
+    bend = jnp.maximum(jnp.abs(low - 2.0 * center + high), 1.0)
+    return (low - high) / (2.0 * bend)
+
+
+def refine(layers, row_off, col_off):
+    wide = jnp.concatenate([row_off] * 8, axis=1)
+    low, mid, high = [pick(layers[d : d + 5], wide) for d in range(3)]
+
+    def cut(layer, d):
+        return pick([layer[:, (d + i) * 32 : (d + i + 1) * 32] for i in range(5)], col_off)
+
+    center = cut(mid, 1)
+    return (
+        row_off.astype(F32) + peak_step(cut(low, 1), center, cut(high, 1)),
+        col_off.astype(F32) + peak_step(cut(mid, 0), center, cut(mid, 2)),
+    )
+
+
+def lay(ref, c, s, field):
+    ring = jnp.concatenate([field[:, 16:], field, field[:, :16]], axis=1)
+    at = (s % 2) * 12 + c * PR
+    ref[at : at + PR, (s // 2) * 64 : (s // 2 + 1) * 64] = ring
+
+
+def inner_kernel(
+    px_ref, rows_ref, cols_ref, first_ref, second_ref, offs_ref, valid_ref,
+    flow_ref, load_ref, mix_ref, corr_ref, picked, offs,
+):
     count = px_ref.shape[0]
     sums, specs = [], []
     half = row_sum(px_ref[0], rows_ref)
@@ -178,22 +213,29 @@
     def _():
         corr_ref[...] += term
 
-
-def pick(pieces, offset):
-    value = pieces[0]
-    for i in range(1, 5):
-        value = jnp.where(offset == i - 2, pieces[i], value)
-    return value
-
-
-def peak_step(low, center, high):
-    bend = jnp.maximum(jnp.abs(low - 2.0 * center + high), 1.0)
-    return (low - high) / (2.0 * bend)
+    @pl.when(pl.program_id(0) == pl.num_programs(0) - 1)
+    def _():
+        flow_ref[...] = jnp.zeros_like(flow_ref)
+        load_ref[...] = jnp.zeros_like(load_ref)
+        for s in range(1, count):
+            rows = slice((s - 1) * PR, s * PR)
+            for p1 in range(SPAN):
+                at = (s - 1) * 32 + p1 * PR
+                picked[p1, rows] = corr_ref[at : at + PR] * (1.0 / PATCH)
+            for c in range(2):
+                offs[c, rows] = offs_ref[s, c]
+        flows = refine([picked[p1] for p1 in range(SPAN)], offs[0], offs[1])
+        for s in range(count):
+            lay(load_ref, 2, s, valid_ref[s].astype(F32))
+            for c in range(2 if s else 0):
+                piece = flows[c][(s - 1) * PR : s * PR]
+                lay(load_ref, c, s, piece)
+                flow_ref[c * PR : (c + 1) * PR, s * 32 : (s + 1) * 32] = piece
 
 
 def edge_kernel(
     up_ref, down_ref, extra_ref, mix_ref, rows_ref, cols_ref, first_ref, second_ref,
-    inner_ref, offs_ref, valid_ref, flow_ref, load_ref, picked, offs, packed,
+    inner_ref, ready_ref, offs_ref, flow_ref, load_ref, offs, packed,
 ):
     sa = lax.axis_index("sa")
     breadth = mix_ref.shape[1]
@@ -224,39 +266,17 @@
                 here.append((mix_ref[:KROWS, part].astype(F32), mix_ref[KROWS:, part].astype(F32)))
             prod = whiten(here, there)
 
-    for p1 in range(SPAN):
-        picked[p1, 0:PR] = corr[p1 * PR : (p1 + 1) * PR]
-        for s in range(3):
-            picked[p1, (s + 1) * PR : (s + 2) * PR] = inner_ref[
-                s * 32 + p1 * PR : s * 32 + (p1 + 1) * PR
-            ]
     extra = extra_ref[...].astype(F32).astype(jnp.int32)
     for c in range(2):
-        for s in range(4):
-            offs[c, s * PR : (s + 1) * PR, :] = offs_ref[s, c]
+        offs[c] = offs_ref[0, c]
         offs[c, 2:4, :] = extra[c * 2 : c * 2 + 2, :32]
-    row_off, col_off = offs[0], offs[1]
-    wide = jnp.concatenate([row_off] * 8, axis=1)
-    layers = [picked[p1] * (1.0 / PATCH) for p1 in range(SPAN)]
-    low, mid, high = [pick(layers[d : d + 5], wide) for d in range(3)]
-
-    def cut(layer, d):
-        return pick([layer[:, (d + i) * 32 : (d + i + 1) * 32] for i in range(5)], col_off)
-
-    center = cut(mid, 1)
-    flows = (
-        row_off.astype(F32) + peak_step(cut(low, 1), center, cut(high, 1)),
-        col_off.astype(F32) + peak_step(cut(mid, 0), center, cut(mid, 2)),
-    )
-    weights = jnp.concatenate([valid_ref[s].astype(F32) for s in range(4)], axis=0)
-    for c, field in enumerate(flows + (weights,)):
-        ring = jnp.concatenate([field[:, 16:], field, field[:, :16]], axis=1)
-        for s in range(4):
-            rows = slice(s * PR, (s + 1) * PR)
-            if c < 2:
-                flow_ref[c * PR : (c + 1) * PR, s * 32 : (s + 1) * 32] = field[rows]
-            at = (s % 2) * 12 + c * PR
-            packed[at : at + PR, (s // 2) * 64 : (s // 2 + 1) * 64] = ring[rows]
+    layers = [corr[p1 * PR : (p1 + 1) * PR] * (1.0 / PATCH) for p1 in range(SPAN)]
+    flows = refine(layers, offs[0], offs[1])
+    flow_ref[...] = inner_ref[...]
+    packed[...] = ready_ref[...]
+    for c in range(2):
+        flow_ref[c * PR : (c + 1) * PR, :32] = flows[c]
+        lay(packed, c, 0, flows[c])
     load_ref[...] = packed[...].astype(BF)
 
 
@@ -372,25 +392,31 @@
             done.append(m)
         return done
 
-    for step in range(1, 4):
-        for c in range(2):
-            for k in range(ns):
-                advance(step, c, k + 2)
-    for step in range(4, RELAX):
-        for c in range(2):
-            for d in range(3):
-                advance(step, c, sa + d + 1)
     mine = slice(2 * PR, 3 * PR)
     late = lax.broadcasted_iota(jnp.int32, (PR, 32), 0) >= 2
-    for c in range(2):
-        final = advance(RELAX, c, sa + 2)
-        for s in range(4):
-            lanes = slice((s // 2) * 64 + 16, (s // 2) * 64 + 48)
-            mesh_out[s, c] = final[s % 2][:PR, lanes]
-            f = own_ref[c * PR : (c + 1) * PR, s * 32 : (s + 1) * 32]
-            if s == 0:
-                f = jnp.where(late, flow[c, 0, sa][mine, lanes], f)
-            flow_out[s, c] = f
+
+    def run(at, wide, narrow):
+        for step in range(1, RELAX):
+            for c in range(2):
+                for k in wide if step < 4 else narrow:
+                    advance(step, c, k)
+        for c in range(2):
+            final = advance(RELAX, c, at + 2)
+            for s in range(4):
+                lanes = slice((s // 2) * 64 + 16, (s // 2) * 64 + 48)
+                mesh_out[s, c] = final[s % 2][:PR, lanes]
+                f = own_ref[c * PR : (c + 1) * PR, s * 32 : (s + 1) * 32]
+                if s == 0:
+                    f = jnp.where(late, flow[c, 0, at][mine, lanes], f)
+                flow_out[s, c] = f
+
+    @pl.when(sa == 0)
+    def _():
+        run(0, range(2, ns + 1), range(2, 4))
+
+    @pl.when(sa != 0)
+    def _():
+        run(sa, range(2, ns + 2), [sa + 1, sa + 2, sa + 3])
 
 
 PAIR = {0: 1, 1: 0, 2: 3, 3: 2}
@@ -472,17 +498,26 @@
         whole((64, 2 * KROWS)),
         pl.BlockSpec((1, 2 * LANES, 8 * blocks * HELD), lambda j: (j, 0, 0)),
     ]
-    inner, mix = pl.pallas_call(
+    inner, ready, mix = pl.pallas_call(
         inner_kernel,
         grid=(blocks,),
-        in_specs=[pl.BlockSpec((count, height, LANES), lambda j: (0, 0, j))] + table_specs,
+        in_specs=[pl.BlockSpec((count, height, LANES), lambda j: (0, 0, j))]
+        + table_specs
+        + [whole((count, 2, PR, 32)), whole((count, PR, 32))],
         out_specs=[
-            whole((96, 256)),
+            whole((8, 128)),
+            whole((24, 128)),
             pl.BlockSpec((2 * KROWS, LANES), lambda j: (0, j)),
         ],
         out_shape=[
-            jax.ShapeDtypeStruct((96, 256), F32),
+            jax.ShapeDtypeStruct((8, 128), F32),
+            jax.ShapeDtypeStruct((24, 128), F32),
             jax.ShapeDtypeStruct((2 * KROWS, breadth), BF),
+        ],
+        scratch_shapes=[
+            pltpu.VMEM((96, 256), F32),
+            pltpu.VMEM((SPAN, 12, 256), F32),
+            pltpu.VMEM((2, 12, 32), jnp.int32),
         ],
         compiler_params=pltpu.CompilerParams(dimension_semantics=("arbitrary",), vmem_limit_bytes=GRANT),
         cost_estimate=pl.CostEstimate(
@@ -490,7 +525,7 @@
         ),
         name="inner",
     )(
-        held, rows, cols, jnp.asarray(first_matrix(False)), second,
+        held, rows, cols, jnp.asarray(first_matrix(False)), second, peak_offsets, validity,
     )
 
     own, load = pl.pallas_call(
@@ -502,15 +537,14 @@
             jax.ShapeDtypeStruct((24, 128), BF),
         ],
         scratch_shapes=[
-            pltpu.VMEM((SPAN, 16, 256), F32),
-            pltpu.VMEM((2, 16, 32), jnp.int32),
+            pltpu.VMEM((2, PR, 32), jnp.int32),
             pltpu.VMEM((24, 128), F32),
         ],
         compiler_params=pltpu.CompilerParams(vmem_limit_bytes=GRANT),
         name="edge",
     )(
         up, down, extra, mix, rows, cols, jnp.asarray(first_matrix(True)), second,
-        inner, peak_offsets, validity,
+        inner, ready, peak_offsets,
     )
 
     got = spread(load)

time: 41.4 us -> 41.1 us (level)
  transfers between devices with their start and end apart: 11 -> 11, of which waited for: 9 -> 9; matrix products, arithmetic and copies ran while one was open for 0% -> 0% of each run, Pallas kernels for 17% -> 18%
where the time goes in v5:
time: 41.1 us; the launch traced here: 40.9 us
  waiting for transfers between devices  15.3 us (37%)
  starting transfers between devices  12.4 us (30%)
  Pallas kernels  12.3 us (30%)
  between operations  0.76 us (2%)
    ppermute x8, waiting for transfers between devices, trade(): return lax.ppermute(array, AXES, route)  12.4 us
    ppermute x8, starting transfers between devices, trade(): return lax.ppermute(array, AXES, route)  7.56 us
    pallas_call x1, Pallas kernels, per_device(): pl.pallas_call(inner_kernel, grid=(blocks,), in_specs=[pl.BlockSpec((coun...  7.19 us
    ppermute x1, waiting for transfers between devices, per_device(): extra = lax.ppermute(extra, 'sa', sink)  2.89 us
    pallas_call x1, Pallas kernels, per_device(): pl.pallas_call(edge_kernel, in_specs=[vmem()] * 11, out_specs=[vmem(), vm...  1.99 us
    pallas_call x1, Pallas kernels, per_device(): pl.pallas_call(relax_kernel, in_specs=[vmem(), vmem()], out_specs=[vmem()...  1.77 us
    ppermute x1, starting transfers between devices, per_device(): down = lax.ppermute(down, 'sa', sink)  1.75 us
    ppermute x1, starting transfers between devices, per_device(): up = lax.ppermute(up, 'sa', rise)  1.56 us
  transfers between devices with their start and end apart: 11, of which 9 were waited for; matrix products, arithmetic and copies ran while one was open for 0% of the time, Pallas kernels for 18%

profile of v5, /device:TPU:48, one launch (start us, length us, event | category | flops | bytes accessed | tf_op | source)
XLA Modules:
  0.0 40.9 jit_solution(13106251489611176782)
XLA Ops:
  0.6 0.0 copy-start
  0.6 0.0 copy-start.1
  0.7 0.0 copy-start.2
  0.7 0.0 copy-start.6
  0.7 0.0 copy-start.3
  0.7 1.4 %send.1 = (bf16[128,2048]{1,0:T(8,128)(2,1)S(1)}, bf16[128,2048]{1,0:T(8,128)(2,1)S(1)}, bf16[8,128]{1,0:T(8,128)(2,1)S(1)}) custom-call(bf16[4,256,2048]{2,1,0:T(8,128)(2,1)} %px_ref.3, s32[4,2,4,32]{3,2,1,0:T(4,128)} %offs_ref.5), custom_call_target="tpu_custom_call" | custom-call | tf_op jit(solution)/shard_map/send/pallas_call | solution.py:468
  2.1 1.6 %collective-permute-start = (bf16[128,2048]{1,0:T(8,128)(2,1)S(1)}, bf16[128,2048]{1,0:T(8,128)(2,1)S(1)}, u32[]{:S(2)}, u32[]{:S(2)}) collective-permute-start(bf16[128,2048]{1,0:T(8,128)(2,1)S(1)} %get-tuple-element.10), channel_id=1, source_target_pairs={{0,1},{1,2},{2,3},{3,0},{4,5},{5,6},{6,7},{7,4},{8,9},{9,10},{10,1... | collective-permute-start | bytes 1572872 | tf_op jit(solution)/shard_map/ppermute | solution.py:487
  3.7 1.7 %collective-permute-start.1 = (bf16[128,2048]{1,0:T(8,128)(2,1)S(1)}, bf16[128,2048]{1,0:T(8,128)(2,1)S(1)}, u32[]{:S(2)}, u32[]{:S(2)}) collective-permute-start(bf16[128,2048]{1,0:T(8,128)(2,1)S(1)} %get-tuple-element.11), channel_id=1, source_target_pairs={{0,3},{1,0},{2,1},{3,2},{4,7},{5,4},{6,5},{7,6},{8,11},{9,8},{10,9... | collective-permute-start | bytes 1572872 | tf_op jit(solution)/shard_map/ppermute | solution.py:488
  5.4 1.5 %collective-permute-start.2 = (bf16[8,128]{1,0:T(8,128)(2,1)S(1)}, bf16[8,128]{1,0:T(8,128)(2,1)S(1)}, u32[]{:S(2)}, u32[]{:S(2)}) collective-permute-start(bf16[8,128]{1,0:T(8,128)(2,1)S(1)} %get-tuple-element.12), channel_id=1, source_target_pairs={{0,3},{1,0},{2,1},{3,2},{4,7},{5,4},{6,5},{7,6},{8,11},{9,8},{10,9... | collective-permute-start | bytes 6152 | tf_op jit(solution)/shard_map/ppermute | solution.py:489
  7.0 0.0 copy-done.1
  7.0 7.2 %inner.1 = (f32[8,128]{1,0:T(8,128)S(1)}, f32[24,128]{1,0:T(8,128)S(1)}, bf16[288,2048]{1,0:T(8,128)(2,1)S(1)}) custom-call(bf16[4,256,2048]{2,1,0:T(8,128)(2,1)} %px_ref.3, bf16[288,256]{1,0:T(8,128)(2,1)S(1)} %copy-done.1, bf16[256,256]{1,0:T(8,128)(2,1)S(1)} %copy-done.2, bf16[64,288]{1,0:T(8,128)(2,1)S(1)} %copy-done.6, ...), custom_call_target="tpu_custom_call" | custom-call | flops 8000000000 | bytes 8388608 | tf_op jit(solution)/shard_map/inner/pallas_call | solution.py:501
  14.2 2.9 %collective-permute-done.2.extra_ref = bf16[8,128]{1,0:T(8,128)(2,1)S(1)} collective-permute-done((bf16[8,128]{1,0:T(8,128)(2,1)S(1)}, bf16[8,128]{1,0:T(8,128)(2,1)S(1)}, u32[]{:S(2)}, u32[]{:S(2)}) %collective-permute-start.2) | collective-permute-done | bytes 2080 | tf_op jit(solution)/shard_map/ppermute | solution.py:489
  17.1 0.0 collective-permute-done.up_ref
  17.1 0.0 collective-permute-done.1.down_ref
  17.1 2.0 %edge.1 = (f32[8,128]{1,0:T(8,128)S(1)}, bf16[24,128]{1,0:T(8,128)(2,1)S(1)}) custom-call(bf16[128,2048]{1,0:T(8,128)(2,1)S(1)} %collective-permute-done.up_ref, bf16[128,2048]{1,0:T(8,128)(2,1)S(1)} %collective-permute-done.1.down_ref, bf16[8,128]{1,0:T(8,128)(2,1)S(1)} %collective-permute-done.2.extra_ref, ...), custom_call_target="tpu_custom_call" | custom-call | tf_op jit(solution)/shard_map/edge/pallas_call | solution.py:531
  19.1 1.3 %collective-permute-start.3 = (bf16[24,128]{1,0:T(8,128)(2,1)S(1)}, bf16[24,128]{1,0:T(8,128)(2,1)S(1)}, u32[]{:S(2)}, u32[]{:S(2)}) collective-permute-start(bf16[24,128]{1,0:T(8,128)(2,1)S(1)} %get-tuple-element.16), channel_id=1, source_target_pairs={{0,32},{1,33},{2,34},{3,35},{4,36},{5,37},{6,38},{7,39},{8,40},{9,... | collective-permute-start | bytes 18440 | tf_op jit(solution)/shard_map/ppermute | solution.py:441
  20.4 0.0 collective-permute-start.4
  20.4 2.3 %collective-permute-done.3 = bf16[24,128]{1,0:T(8,128)(2,1)S(1)} collective-permute-done((bf16[24,128]{1,0:T(8,128)(2,1)S(1)}, bf16[24,128]{1,0:T(8,128)(2,1)S(1)}, u32[]{:S(2)}, u32[]{:S(2)}) %collective-permute-start.3) | collective-permute-done | bytes 6176 | tf_op jit(solution)/shard_map/ppermute | solution.py:441
  22.7 1.3 %collective-permute-done.4 = bf16[24,128]{1,0:T(8,128)(2,1)S(1)} collective-permute-done((bf16[24,128]{1,0:T(8,128)(2,1)S(1)}, bf16[24,128]{1,0:T(8,128)(2,1)S(1)}, u32[]{:S(2)}, u32[]{:S(2)}) %collective-permute-start.4) | collective-permute-done | bytes 6176 | tf_op jit(solution)/shard_map/ppermute | solution.py:441
  24.0 0.1 collective-permute-start.5
  24.1 1.2 %collective-permute-done.5 = bf16[24,128]{1,0:T(8,128)(2,1)S(1)} collective-permute-done((bf16[24,128]{1,0:T(8,128)(2,1)S(1)}, bf16[24,128]{1,0:T(8,128)(2,1)S(1)}, u32[]{:S(2)}, u32[]{:S(2)}) %collective-permute-start.5) | collective-permute-done | bytes 6176 | tf_op jit(solution)/shard_map/ppermute | solution.py:441
  25.3 1.9 %collective-permute-start.7 = (bf16[2,24,128]{2,1,0:T(8,128)(2,1)S(1)}, bf16[2,24,128]{2,1,0:T(8,128)(2,1)S(1)}, u32[]{:S(2)}, u32[]{:S(2)}) collective-permute-start(bf16[2,24,128]{2,1,0:T(8,128)(2,1)S(1)} %get-tuple-element.21), channel_id=1, source_target_pairs={{0,4},{1,5},{2,6},{3,7},{4,0},{5,1},{6,2},{7,3},{8,16},{9,17},{10,... | collective-permute-start | bytes 36872 | tf_op jit(solution)/shard_map/ppermute | solution.py:441
  27.2 0.0 collective-permute-start.6
  27.2 1.8 %collective-permute-done.7 = bf16[2,24,128]{2,1,0:T(8,128)(2,1)S(1)} collective-permute-done((bf16[2,24,128]{2,1,0:T(8,128)(2,1)S(1)}, bf16[2,24,128]{2,1,0:T(8,128)(2,1)S(1)}, u32[]{:S(2)}, u32[]{:S(2)}) %collective-permute-start.7) | collective-permute-done | bytes 12320 | tf_op jit(solution)/shard_map/ppermute | solution.py:441
  29.0 1.9 %collective-permute-done.6 = bf16[2,24,128]{2,1,0:T(8,128)(2,1)S(1)} collective-permute-done((bf16[2,24,128]{2,1,0:T(8,128)(2,1)S(1)}, bf16[2,24,128]{2,1,0:T(8,128)(2,1)S(1)}, u32[]{:S(2)}, u32[]{:S(2)}) %collective-permute-start.6) | collective-permute-done | bytes 12320 | tf_op jit(solution)/shard_map/ppermute | solution.py:441
  30.9 2.8 %collective-permute-start.10 = (bf16[3,2,24,128]{3,2,1,0:T(8,128)(2,1)S(1)}, bf16[3,2,24,128]{3,2,1,0:T(8,128)(2,1)S(1)}, u32[]{:S(2)}, u32[]{:S(2)}) collective-permute-start(bf16[3,2,24,128]{3,2,1,0:T(8,128)(2,1)S(1)} %get-tuple-element.19), channel_id=1, source_target_pairs={{0,2},{1,3},{2,0},{3,1},{4,6},{5,7},{6,4},{7,5},{8,10},{9,11},{10,... | collective-permute-start | bytes 110600 | tf_op jit(solution)/shard_map/ppermute | solution.py:441
  33.7 1.4 %collective-permute-start.9 = (bf16[3,2,24,128]{3,2,1,0:T(8,128)(2,1)S(1)}, bf16[3,2,24,128]{3,2,1,0:T(8,128)(2,1)S(1)}, u32[]{:S(2)}, u32[]{:S(2)}) collective-permute-start(bf16[3,2,24,128]{3,2,1,0:T(8,128)(2,1)S(1)} %get-tuple-element.19), channel_id=1, source_target_pairs={{0,3},{1,2},{2,1},{3,0},{4,7},{5,6},{6,5},{7,4},{8,11},{9,10},{10,... | collective-permute-start | bytes 110600 | tf_op jit(solution)/shard_map/ppermute | solution.py:441
  35.2 0.0 collective-permute-start.8
  35.2 1.4 %collective-permute-done.10 = bf16[3,2,24,128]{3,2,1,0:T(8,128)(2,1)S(1)} collective-permute-done((bf16[3,2,24,128]{3,2,1,0:T(8,128)(2,1)S(1)}, bf16[3,2,24,128]{3,2,1,0:T(8,128)(2,1)S(1)}, u32[]{:S(2)}, u32[]{:S(2)}) %collective-permute-start.10) | collective-permute-done | bytes 36896 | tf_op jit(solution)/shard_map/ppermute | solution.py:441
  36.6 2.3 %collective-permute-done.9 = bf16[3,2,24,128]{3,2,1,0:T(8,128)(2,1)S(1)} collective-permute-done((bf16[3,2,24,128]{3,2,1,0:T(8,128)(2,1)S(1)}, bf16[3,2,24,128]{3,2,1,0:T(8,128)(2,1)S(1)}, u32[]{:S(2)}, u32[]{:S(2)}) %collective-permute-start.9) | collective-permute-done | bytes 36896 | tf_op jit(solution)/shard_map/ppermute | solution.py:441
  38.9 0.2 collective-permute-done.8
  39.2 1.8 %relax.1 = (f32[4,2,4,32]{3,2,1,0:T(4,128)}, f32[4,2,4,32]{3,2,1,0:T(4,128)}) custom-call(bf16[4,3,2,24,128]{4,3,2,1,0:T(8,128)(2,1)S(1)} %pad_maximum_fusion.got_ref, f32[8,128]{1,0:T(8,128)S(1)} %get-tuple-element.17.own_ref), custom_call_target="tpu_custom_call" | custom-call | tf_op jit(solution)/shard_map/relax/pallas_call | solution.py:554
  (14 shorter events, 0.1 us)
Async XLA Ops:
  0.6 6.3 %copy-start = (bf16[4,1024,256]{2,1,0:T(8,128)(2,1)S(1)}, bf16[4,1024,256]{2,1,0:T(8,128)(2,1)}, u32[]{:S(2)}) copy-start(bf16[4,1024,256]{2,1,0:T(8,128)(2,1)} %constant.51.clone.second_ref) | copy-start | bytes 6291460
  0.6 6.3 %copy-start.1 = (bf16[288,256]{1,0:T(8,128)(2,1)S(1)}, bf16[288,256]{1,0:T(8,128)(2,1)}, u32[]{:S(2)}) copy-start(bf16[288,256]{1,0:T(8,128)(2,1)} %constant.49.clone.rows_ref) | copy-start | bytes 442372
  0.7 6.3 %copy-start.2 = (bf16[256,256]{1,0:T(8,128)(2,1)S(1)}, bf16[256,256]{1,0:T(8,128)(2,1)}, u32[]{:S(2)}) copy-start(bf16[256,256]{1,0:T(8,128)(2,1)} %constant.50.clone.cols_ref) | copy-start | bytes 393220
  0.7 6.3 %copy-start.6 = (bf16[64,288]{1,0:T(8,128)(2,1)S(1)}, bf16[64,288]{1,0:T(8,128)(2,1)}, u32[]{:S(2)}) copy-start(bf16[64,288]{1,0:T(8,128)(2,1)} %constant.52.clone.first_ref) | copy-start | bytes 110596
  0.7 6.3 %copy-start.3 = (s32[4,2,4,32]{3,2,1,0:T(4,128)S(1)}, s32[4,2,4,32]{3,2,1,0:T(4,128)}, u32[]{:S(2)}) copy-start(s32[4,2,4,32]{3,2,1,0:T(4,128)} %offs_ref.5) | copy-start | bytes 12292
  0.7 6.3 %copy-start.5 = (s32[4,4,32]{2,1,0:T(4,128)S(1)}, s32[4,4,32]{2,1,0:T(4,128)}, u32[]{:S(2)}) copy-start(s32[4,4,32]{2,1,0:T(4,128)} %valid_ref.1) | copy-start | bytes 6148
  2.1 15.0 %collective-permute-start = (bf16[128,2048]{1,0:T(8,128)(2,1)S(1)}, bf16[128,2048]{1,0:T(8,128)(2,1)S(1)}, u32[]{:S(2)}, u32[]{:S(2)}) collective-permute-start(bf16[128,2048]{1,0:T(8,128)(2,1)S(1)} %get-tuple-element.10), channel_id=1, source_target_pairs={{0,1},{1,2},{2,3},{3,0},{4,5},{5,6},{6,7},{7,4},{8,9},{9,10},{10,1... | collective-permute-start | bytes 1572872 | tf_op jit(solution)/shard_map/ppermute | solution.py:487
  3.7 13.4 %collective-permute-start.1 = (bf16[128,2048]{1,0:T(8,128)(2,1)S(1)}, bf16[128,2048]{1,0:T(8,128)(2,1)S(1)}, u32[]{:S(2)}, u32[]{:S(2)}) collective-permute-start(bf16[128,2048]{1,0:T(8,128)(2,1)S(1)} %get-tuple-element.11), channel_id=1, source_target_pairs={{0,3},{1,0},{2,1},{3,2},{4,7},{5,4},{6,5},{7,6},{8,11},{9,8},{10,9... | collective-permute-start | bytes 1572872 | tf_op jit(solution)/shard_map/ppermute | solution.py:488
  5.4 11.7 %copy-start.4 = (bf16[64,288]{1,0:T(8,128)(2,1)S(1)}, bf16[64,288]{1,0:T(8,128)(2,1)}, u32[]{:S(2)}) copy-start(bf16[64,288]{1,0:T(8,128)(2,1)} %constant.53.clone.first_ref) | copy-start | bytes 110596
  5.4 11.7 %collective-permute-start.2 = (bf16[8,128]{1,0:T(8,128)(2,1)S(1)}, bf16[8,128]{1,0:T(8,128)(2,1)S(1)}, u32[]{:S(2)}, u32[]{:S(2)}) collective-permute-start(bf16[8,128]{1,0:T(8,128)(2,1)S(1)} %get-tuple-element.12), channel_id=1, source_target_pairs={{0,3},{1,0},{2,1},{3,2},{4,7},{5,4},{6,5},{7,6},{8,11},{9,8},{10,9... | collective-permute-start | bytes 6152 | tf_op jit(solution)/shard_map/ppermute | solution.py:489
  19.1 3.6 %collective-permute-start.3 = (bf16[24,128]{1,0:T(8,128)(2,1)S(1)}, bf16[24,128]{1,0:T(8,128)(2,1)S(1)}, u32[]{:S(2)}, u32[]{:S(2)}) collective-permute-start(bf16[24,128]{1,0:T(8,128)(2,1)S(1)} %get-tuple-element.16), channel_id=1, source_target_pairs={{0,32},{1,33},{2,34},{3,35},{4,36},{5,37},{6,38},{7,39},{8,40},{9,... | collective-permute-start | bytes 18440 | tf_op jit(solution)/shard_map/ppermute | solution.py:441
  20.4 3.6 %collective-permute-start.4 = (bf16[24,128]{1,0:T(8,128)(2,1)S(1)}, bf16[24,128]{1,0:T(8,128)(2,1)S(1)}, u32[]{:S(2)}, u32[]{:S(2)}) collective-permute-start(bf16[24,128]{1,0:T(8,128)(2,1)S(1)} %get-tuple-element.16), channel_id=1, source_target_pairs={{0,4},{1,5},{2,6},{3,7},{4,0},{5,1},{6,2},{7,3},{8,12},{9,13},{10,... | collective-permute-start | bytes 18440 | tf_op jit(solution)/shard_map/ppermute | solution.py:441
  24.0 1.2 %collective-permute-start.5 = (bf16[24,128]{1,0:T(8,128)(2,1)S(1)}, bf16[24,128]{1,0:T(8,128)(2,1)S(1)}, u32[]{:S(2)}, u32[]{:S(2)}) collective-permute-start(bf16[24,128]{1,0:T(8,128)(2,1)S(1)} %fusion.1), channel_id=1, source_target_pairs={{0,4},{1,5},{2,6},{3,7},{4,0},{5,1},{6,2},{7,3},{8,12},{9,13},{10,... | collective-permute-start | bytes 18440 | tf_op jit(solution)/shard_map/ppermute | solution.py:441
  25.3 3.7 %collective-permute-start.7 = (bf16[2,24,128]{2,1,0:T(8,128)(2,1)S(1)}, bf16[2,24,128]{2,1,0:T(8,128)(2,1)S(1)}, u32[]{:S(2)}, u32[]{:S(2)}) collective-permute-start(bf16[2,24,128]{2,1,0:T(8,128)(2,1)S(1)} %get-tuple-element.21), channel_id=1, source_target_pairs={{0,4},{1,5},{2,6},{3,7},{4,0},{5,1},{6,2},{7,3},{8,16},{9,17},{10,... | collective-permute-start | bytes 36872 | tf_op jit(solution)/shard_map/ppermute | solution.py:441
  27.2 3.7 %collective-permute-start.6 = (bf16[2,24,128]{2,1,0:T(8,128)(2,1)S(1)}, bf16[2,24,128]{2,1,0:T(8,128)(2,1)S(1)}, u32[]{:S(2)}, u32[]{:S(2)}) collective-permute-start(bf16[2,24,128]{2,1,0:T(8,128)(2,1)S(1)} %get-tuple-element.21), channel_id=1, source_target_pairs={{0,8},{1,9},{2,10},{3,11},{4,12},{5,13},{6,14},{7,15},{8,0},{9,1},... | collective-permute-start | bytes 36872 | tf_op jit(solution)/shard_map/ppermute | solution.py:441
  30.9 5.6 %collective-permute-start.10 = (bf16[3,2,24,128]{3,2,1,0:T(8,128)(2,1)S(1)}, bf16[3,2,24,128]{3,2,1,0:T(8,128)(2,1)S(1)}, u32[]{:S(2)}, u32[]{:S(2)}) collective-permute-start(bf16[3,2,24,128]{3,2,1,0:T(8,128)(2,1)S(1)} %get-tuple-element.19), channel_id=1, source_target_pairs={{0,2},{1,3},{2,0},{3,1},{4,6},{5,7},{6,4},{7,5},{8,10},{9,11},{10,... | collective-permute-start | bytes 110600 | tf_op jit(solution)/shard_map/ppermute | solution.py:441
  33.7 5.2 %collective-permute-start.9 = (bf16[3,2,24,128]{3,2,1,0:T(8,128)(2,1)S(1)}, bf16[3,2,24,128]{3,2,1,0:T(8,128)(2,1)S(1)}, u32[]{:S(2)}, u32[]{:S(2)}) collective-permute-start(bf16[3,2,24,128]{3,2,1,0:T(8,128)(2,1)S(1)} %get-tuple-element.19), channel_id=1, source_target_pairs={{0,3},{1,2},{2,1},{3,0},{4,7},{5,6},{6,5},{7,4},{8,11},{9,10},{10,... | collective-permute-start | bytes 110600 | tf_op jit(solution)/shard_map/ppermute | solution.py:441
  35.2 4.0 %collective-permute-start.8 = (bf16[3,2,24,128]{3,2,1,0:T(8,128)(2,1)S(1)}, bf16[3,2,24,128]{3,2,1,0:T(8,128)(2,1)S(1)}, u32[]{:S(2)}, u32[]{:S(2)}) collective-permute-start(bf16[3,2,24,128]{3,2,1,0:T(8,128)(2,1)S(1)} %get-tuple-element.19), channel_id=1, source_target_pairs={{0,1},{1,0},{2,3},{3,2},{4,5},{5,4},{6,7},{7,6},{8,9},{9,8},{10,11... | collective-permute-start | bytes 110600 | tf_op jit(solution)/shard_map/ppermute | solution.py:441

commit v6 on v5

--- a/solution.py
+++ b/solution.py
@@ -298,7 +298,7 @@
         core = g % 2
         for k in range(ns):
             hop = sa ^ k
-            block = got_ref[hop ^ (hop // 2), chip, core].astype(F32)
+            block = got_ref[hop ^ (hop // 2), core, chip].astype(F32)
             for i in range(2):
                 for c in range(3):
                     raw[c, i, k, g * PR : (g + 1) * PR, :] = block[
@@ -448,10 +448,10 @@
     place = lax.broadcasted_iota(jnp.int32, load.shape, 1) % 64
     side = jnp.where((place < 16) == odd, near, far)
     load = jnp.where((place >= 16) & (place < 48), load, side)
-    load = jnp.stack([load, trade(load, "gx", {})])
     near = trade(load, "chip", PAIR)
     far = trade(load, "chip", CROSS)
     load = jnp.stack([load, near, far])
+    load = jnp.stack([load, trade(load, "gx", {})])
     one = trade(load, "sa", PAIR)
     two = trade(load, "sa", RING)
     three = trade(load, "sa", SKIP)
@@ -525,7 +525,13 @@
         ),
         name="inner",
     )(
-        held, rows, cols, jnp.asarray(first_matrix(False)), second, peak_offsets, validity,
+        held,
+        *[
+            pltpu.with_memory_space_constraint(table, pltpu.HBM)
+            for table in (
+                rows, cols, jnp.asarray(first_matrix(False)), second, peak_offsets, validity,
+            )
+        ],
     )
 
     own, load = pl.pallas_call(

time: 41.1 us -> 40.8 us (level)
  no operation moved by 1% of the time
where the time goes in v6:
time: 40.8 us; the launch traced here: 40.7 us
  waiting for transfers between devices  14.9 us (37%)
  Pallas kernels  12.5 us (31%)
  starting transfers between devices  12.5 us (31%)
  between operations  0.73 us (2%)
    ppermute x8, waiting for transfers between devices, trade(): return lax.ppermute(array, AXES, route)  12.4 us
    ppermute x8, starting transfers between devices, trade(): return lax.ppermute(array, AXES, route)  7.55 us
    pallas_call x1, Pallas kernels, per_device(): pl.pallas_call(inner_kernel, grid=(blocks,), in_specs=[pl.BlockSpec((coun...  7.5 us
    ppermute x1, waiting for transfers between devices, per_device(): extra = lax.ppermute(extra, 'sa', sink)  2.53 us
    pallas_call x1, Pallas kernels, per_device(): pl.pallas_call(edge_kernel, in_specs=[vmem()] * 11, out_specs=[vmem(), vm...  1.97 us
    pallas_call x1, Pallas kernels, per_device(): pl.pallas_call(relax_kernel, in_specs=[vmem(), vmem()], out_specs=[vmem()...  1.77 us
    ppermute x1, starting transfers between devices, per_device(): down = lax.ppermute(down, 'sa', sink)  1.75 us
    ppermute x1, starting transfers between devices, per_device(): extra = lax.ppermute(extra, 'sa', sink)  1.62 us
  transfers between devices with their start and end apart: 11, of which 9 were waited for; matrix products, arithmetic and copies ran while one was open for 0% of the time, Pallas kernels for 18%

profile of v6, /device:TPU:48, one launch (start us, length us, event | category | flops | bytes accessed | tf_op | source)
XLA Modules:
  0.0 40.7 jit_solution(1709826768983528357)
XLA Ops:
  0.6 1.2 %send.1 = (bf16[128,2048]{1,0:T(8,128)(2,1)S(1)}, bf16[128,2048]{1,0:T(8,128)(2,1)S(1)}, bf16[8,128]{1,0:T(8,128)(2,1)S(1)}) custom-call(bf16[4,256,2048]{2,1,0:T(8,128)(2,1)} %px_ref.3, s32[4,2,4,32]{3,2,1,0:T(4,128)} %offs_ref.5), custom_call_target="tpu_custom_call" | custom-call | tf_op jit(solution)/shard_map/send/pallas_call | solution.py:468
  1.9 1.6 %collective-permute-start = (bf16[128,2048]{1,0:T(8,128)(2,1)S(1)}, bf16[128,2048]{1,0:T(8,128)(2,1)S(1)}, u32[]{:S(2)}, u32[]{:S(2)}) collective-permute-start(bf16[128,2048]{1,0:T(8,128)(2,1)S(1)} %get-tuple-element.10), channel_id=1, source_target_pairs={{0,1},{1,2},{2,3},{3,0},{4,5},{5,6},{6,7},{7,4},{8,9},{9,10},{10,1... | collective-permute-start | bytes 1572872 | tf_op jit(solution)/shard_map/ppermute | solution.py:487
  3.4 1.7 %collective-permute-start.1 = (bf16[128,2048]{1,0:T(8,128)(2,1)S(1)}, bf16[128,2048]{1,0:T(8,128)(2,1)S(1)}, u32[]{:S(2)}, u32[]{:S(2)}) collective-permute-start(bf16[128,2048]{1,0:T(8,128)(2,1)S(1)} %get-tuple-element.11), channel_id=1, source_target_pairs={{0,3},{1,0},{2,1},{3,2},{4,7},{5,4},{6,5},{7,6},{8,11},{9,8},{10,9... | collective-permute-start | bytes 1572872 | tf_op jit(solution)/shard_map/ppermute | solution.py:488
  5.2 0.0 copy-start.4
  5.2 1.6 %collective-permute-start.2 = (bf16[8,128]{1,0:T(8,128)(2,1)S(1)}, bf16[8,128]{1,0:T(8,128)(2,1)S(1)}, u32[]{:S(2)}, u32[]{:S(2)}) collective-permute-start(bf16[8,128]{1,0:T(8,128)(2,1)S(1)} %get-tuple-element.12), channel_id=1, source_target_pairs={{0,3},{1,0},{2,1},{3,2},{4,7},{5,4},{6,5},{7,6},{8,11},{9,8},{10,9... | collective-permute-start | bytes 6152 | tf_op jit(solution)/shard_map/ppermute | solution.py:489
  6.8 7.5 %inner.1 = (f32[8,128]{1,0:T(8,128)S(1)}, f32[24,128]{1,0:T(8,128)S(1)}, bf16[288,2048]{1,0:T(8,128)(2,1)S(1)}) custom-call(bf16[4,256,2048]{2,1,0:T(8,128)(2,1)} %px_ref.3, bf16[288,256]{1,0:T(8,128)(2,1)} %constant.49.clone.rows_ref, bf16[256,256]{1,0:T(8,128)(2,1)} %constant.50.clone.cols_ref, bf16[64,288]{1,0:T(8,128)(2,1)} %constant.52.clone.first_ref, ...), custom_call_target="tpu_custom_call" | custom-call | flops 8000000000 | bytes 8388608 | tf_op jit(solution)/shard_map/inner/pallas_call | solution.py:501
  14.3 2.5 %collective-permute-done.2.extra_ref = bf16[8,128]{1,0:T(8,128)(2,1)S(1)} collective-permute-done((bf16[8,128]{1,0:T(8,128)(2,1)S(1)}, bf16[8,128]{1,0:T(8,128)(2,1)S(1)}, u32[]{:S(2)}, u32[]{:S(2)}) %collective-permute-start.2) | collective-permute-done | bytes 2080 | tf_op jit(solution)/shard_map/ppermute | solution.py:489
  16.9 0.0 collective-permute-done.up_ref
  16.9 0.0 collective-permute-done.1.down_ref
  16.9 0.0 copy-done
  16.9 0.0 copy-done.1
  16.9 0.0 copy-done.2
  16.9 0.0 copy-done.3
  16.9 0.0 copy-done.4
  16.9 2.0 %edge.1 = (f32[8,128]{1,0:T(8,128)S(1)}, bf16[24,128]{1,0:T(8,128)(2,1)S(1)}) custom-call(bf16[128,2048]{1,0:T(8,128)(2,1)S(1)} %collective-permute-done.up_ref, bf16[128,2048]{1,0:T(8,128)(2,1)S(1)} %collective-permute-done.1.down_ref, bf16[8,128]{1,0:T(8,128)(2,1)S(1)} %collective-permute-done.2.extra_ref, ...), custom_call_target="tpu_custom_call" | custom-call | tf_op jit(solution)/shard_map/edge/pallas_call | solution.py:537
  18.9 1.3 %collective-permute-start.3 = (bf16[24,128]{1,0:T(8,128)(2,1)S(1)}, bf16[24,128]{1,0:T(8,128)(2,1)S(1)}, u32[]{:S(2)}, u32[]{:S(2)}) collective-permute-start(bf16[24,128]{1,0:T(8,128)(2,1)S(1)} %get-tuple-element.16), channel_id=1, source_target_pairs={{0,32},{1,33},{2,34},{3,35},{4,36},{5,37},{6,38},{7,39},{8,40},{9,... | collective-permute-start | bytes 18440 | tf_op jit(solution)/shard_map/ppermute | solution.py:441
  20.2 0.0 collective-permute-start.4
  20.2 2.3 %collective-permute-done.3 = bf16[24,128]{1,0:T(8,128)(2,1)S(1)} collective-permute-done((bf16[24,128]{1,0:T(8,128)(2,1)S(1)}, bf16[24,128]{1,0:T(8,128)(2,1)S(1)}, u32[]{:S(2)}, u32[]{:S(2)}) %collective-permute-start.3) | collective-permute-done | bytes 6176 | tf_op jit(solution)/shard_map/ppermute | solution.py:441
  22.5 1.3 %collective-permute-done.4 = bf16[24,128]{1,0:T(8,128)(2,1)S(1)} collective-permute-done((bf16[24,128]{1,0:T(8,128)(2,1)S(1)}, bf16[24,128]{1,0:T(8,128)(2,1)S(1)}, u32[]{:S(2)}, u32[]{:S(2)}) %collective-permute-start.4) | collective-permute-done | bytes 6176 | tf_op jit(solution)/shard_map/ppermute | solution.py:441
  23.8 2.0 %collective-permute-start.6 = (bf16[24,128]{1,0:T(8,128)(2,1)S(1)}, bf16[24,128]{1,0:T(8,128)(2,1)S(1)}, u32[]{:S(2)}, u32[]{:S(2)}) collective-permute-start(bf16[24,128]{1,0:T(8,128)(2,1)S(1)} %fusion.1), channel_id=1, source_target_pairs={{0,4},{1,5},{2,6},{3,7},{4,0},{5,1},{6,2},{7,3},{8,16},{9,17},{10,... | collective-permute-start | bytes 18440 | tf_op jit(solution)/shard_map/ppermute | solution.py:441
  25.8 0.0 collective-permute-start.5
  25.8 1.7 %collective-permute-done.6 = bf16[24,128]{1,0:T(8,128)(2,1)S(1)} collective-permute-done((bf16[24,128]{1,0:T(8,128)(2,1)S(1)}, bf16[24,128]{1,0:T(8,128)(2,1)S(1)}, u32[]{:S(2)}, u32[]{:S(2)}) %collective-permute-start.6) | collective-permute-done | bytes 6176 | tf_op jit(solution)/shard_map/ppermute | solution.py:441
  27.5 1.9 %collective-permute-done.5 = bf16[24,128]{1,0:T(8,128)(2,1)S(1)} collective-permute-done((bf16[24,128]{1,0:T(8,128)(2,1)S(1)}, bf16[24,128]{1,0:T(8,128)(2,1)S(1)}, u32[]{:S(2)}, u32[]{:S(2)}) %collective-permute-start.5) | collective-permute-done | bytes 6176 | tf_op jit(solution)/shard_map/ppermute | solution.py:441
  29.5 0.0 collective-permute-start.7
  29.5 1.2 %collective-permute-done.7 = bf16[3,24,128]{2,1,0:T(8,128)(2,1)S(1)} collective-permute-done((bf16[3,24,128]{2,1,0:T(8,128)(2,1)S(1)}, bf16[3,24,128]{2,1,0:T(8,128)(2,1)S(1)}, u32[]{:S(2)}, u32[]{:S(2)}) %collective-permute-start.7) | collective-permute-done | bytes 18464 | tf_op jit(solution)/shard_map/ppermute | solution.py:441
  30.7 2.8 %collective-permute-start.10 = (bf16[2,3,24,128]{3,2,1,0:T(8,128)(2,1)S(1)}, bf16[2,3,24,128]{3,2,1,0:T(8,128)(2,1)S(1)}, u32[]{:S(2)}, u32[]{:S(2)}) collective-permute-start(bf16[2,3,24,128]{3,2,1,0:T(8,128)(2,1)S(1)} %get-tuple-element.19), channel_id=1, source_target_pairs={{0,2},{1,3},{2,0},{3,1},{4,6},{5,7},{6,4},{7,5},{8,10},{9,11},{10,... | collective-permute-start | bytes 110600 | tf_op jit(solution)/shard_map/ppermute | solution.py:441
  33.5 1.4 %collective-permute-start.9 = (bf16[2,3,24,128]{3,2,1,0:T(8,128)(2,1)S(1)}, bf16[2,3,24,128]{3,2,1,0:T(8,128)(2,1)S(1)}, u32[]{:S(2)}, u32[]{:S(2)}) collective-permute-start(bf16[2,3,24,128]{3,2,1,0:T(8,128)(2,1)S(1)} %get-tuple-element.19), channel_id=1, source_target_pairs={{0,3},{1,2},{2,1},{3,0},{4,7},{5,6},{6,5},{7,4},{8,11},{9,10},{10,... | collective-permute-start | bytes 110600 | tf_op jit(solution)/shard_map/ppermute | solution.py:441
  34.9 0.0 collective-permute-start.8
  34.9 1.3 %collective-permute-done.10 = bf16[2,3,24,128]{3,2,1,0:T(8,128)(2,1)S(1)} collective-permute-done((bf16[2,3,24,128]{3,2,1,0:T(8,128)(2,1)S(1)}, bf16[2,3,24,128]{3,2,1,0:T(8,128)(2,1)S(1)}, u32[]{:S(2)}, u32[]{:S(2)}) %collective-permute-start.10) | collective-permute-done | bytes 36896 | tf_op jit(solution)/shard_map/ppermute | solution.py:441
  36.2 2.4 %collective-permute-done.9 = bf16[2,3,24,128]{3,2,1,0:T(8,128)(2,1)S(1)} collective-permute-done((bf16[2,3,24,128]{3,2,1,0:T(8,128)(2,1)S(1)}, bf16[2,3,24,128]{3,2,1,0:T(8,128)(2,1)S(1)}, u32[]{:S(2)}, u32[]{:S(2)}) %collective-permute-start.9) | collective-permute-done | bytes 36896 | tf_op jit(solution)/shard_map/ppermute | solution.py:441
  38.6 0.2 collective-permute-done.8
  38.9 1.8 %relax.1 = (f32[4,2,4,32]{3,2,1,0:T(4,128)}, f32[4,2,4,32]{3,2,1,0:T(4,128)}) custom-call(bf16[4,2,3,24,128]{4,3,2,1,0:T(8,128)(2,1)S(1)} %pad_maximum_fusion.got_ref, f32[8,128]{1,0:T(8,128)S(1)} %get-tuple-element.17.own_ref), custom_call_target="tpu_custom_call" | custom-call | tf_op jit(solution)/shard_map/relax/pallas_call | solution.py:560
  (10 shorter events, 0.1 us)
Async XLA Ops:
  1.9 15.0 %collective-permute-start = (bf16[128,2048]{1,0:T(8,128)(2,1)S(1)}, bf16[128,2048]{1,0:T(8,128)(2,1)S(1)}, u32[]{:S(2)}, u32[]{:S(2)}) collective-permute-start(bf16[128,2048]{1,0:T(8,128)(2,1)S(1)} %get-tuple-element.10), channel_id=1, source_target_pairs={{0,1},{1,2},{2,3},{3,0},{4,5},{5,6},{6,7},{7,4},{8,9},{9,10},{10,1... | collective-permute-start | bytes 1572872 | tf_op jit(solution)/shard_map/ppermute | solution.py:487
  3.4 13.4 %collective-permute-start.1 = (bf16[128,2048]{1,0:T(8,128)(2,1)S(1)}, bf16[128,2048]{1,0:T(8,128)(2,1)S(1)}, u32[]{:S(2)}, u32[]{:S(2)}) collective-permute-start(bf16[128,2048]{1,0:T(8,128)(2,1)S(1)} %get-tuple-element.11), channel_id=1, source_target_pairs={{0,3},{1,0},{2,1},{3,2},{4,7},{5,4},{6,5},{7,6},{8,11},{9,8},{10,9... | collective-permute-start | bytes 1572872 | tf_op jit(solution)/shard_map/ppermute | solution.py:488
  5.2 11.7 %copy-start = (bf16[4,1024,256]{2,1,0:T(8,128)(2,1)S(1)}, bf16[4,1024,256]{2,1,0:T(8,128)(2,1)}, u32[]{:S(2)}) copy-start(bf16[4,1024,256]{2,1,0:T(8,128)(2,1)} %constant.51.clone.second_ref) | copy-start | bytes 6291460
  5.2 11.7 %copy-start.1 = (bf16[288,256]{1,0:T(8,128)(2,1)S(1)}, bf16[288,256]{1,0:T(8,128)(2,1)}, u32[]{:S(2)}) copy-start(bf16[288,256]{1,0:T(8,128)(2,1)} %constant.49.clone.rows_ref) | copy-start | bytes 442372
  5.2 11.7 %copy-start.2 = (bf16[256,256]{1,0:T(8,128)(2,1)S(1)}, bf16[256,256]{1,0:T(8,128)(2,1)}, u32[]{:S(2)}) copy-start(bf16[256,256]{1,0:T(8,128)(2,1)} %constant.50.clone.cols_ref) | copy-start | bytes 393220
  5.2 11.7 %copy-start.3 = (s32[4,2,4,32]{3,2,1,0:T(4,128)S(1)}, s32[4,2,4,32]{3,2,1,0:T(4,128)}, u32[]{:S(2)}) copy-start(s32[4,2,4,32]{3,2,1,0:T(4,128)} %offs_ref.5) | copy-start | bytes 12292
  5.2 11.7 %copy-start.4 = (bf16[64,288]{1,0:T(8,128)(2,1)S(1)}, bf16[64,288]{1,0:T(8,128)(2,1)}, u32[]{:S(2)}) copy-start(bf16[64,288]{1,0:T(8,128)(2,1)} %constant.53.clone.first_ref) | copy-start | bytes 110596
  5.2 11.7 %collective-permute-start.2 = (bf16[8,128]{1,0:T(8,128)(2,1)S(1)}, bf16[8,128]{1,0:T(8,128)(2,1)S(1)}, u32[]{:S(2)}, u32[]{:S(2)}) collective-permute-start(bf16[8,128]{1,0:T(8,128)(2,1)S(1)} %get-tuple-element.12), channel_id=1, source_target_pairs={{0,3},{1,0},{2,1},{3,2},{4,7},{5,4},{6,5},{7,6},{8,11},{9,8},{10,9... | collective-permute-start | bytes 6152 | tf_op jit(solution)/shard_map/ppermute | solution.py:489
  18.9 3.6 %collective-permute-start.3 = (bf16[24,128]{1,0:T(8,128)(2,1)S(1)}, bf16[24,128]{1,0:T(8,128)(2,1)S(1)}, u32[]{:S(2)}, u32[]{:S(2)}) collective-permute-start(bf16[24,128]{1,0:T(8,128)(2,1)S(1)} %get-tuple-element.16), channel_id=1, source_target_pairs={{0,32},{1,33},{2,34},{3,35},{4,36},{5,37},{6,38},{7,39},{8,40},{9,... | collective-permute-start | bytes 18440 | tf_op jit(solution)/shard_map/ppermute | solution.py:441
  20.2 3.6 %collective-permute-start.4 = (bf16[24,128]{1,0:T(8,128)(2,1)S(1)}, bf16[24,128]{1,0:T(8,128)(2,1)S(1)}, u32[]{:S(2)}, u32[]{:S(2)}) collective-permute-start(bf16[24,128]{1,0:T(8,128)(2,1)S(1)} %get-tuple-element.16), channel_id=1, source_target_pairs={{0,4},{1,5},{2,6},{3,7},{4,0},{5,1},{6,2},{7,3},{8,12},{9,13},{10,... | collective-permute-start | bytes 18440 | tf_op jit(solution)/shard_map/ppermute | solution.py:441
  23.8 3.7 %collective-permute-start.6 = (bf16[24,128]{1,0:T(8,128)(2,1)S(1)}, bf16[24,128]{1,0:T(8,128)(2,1)S(1)}, u32[]{:S(2)}, u32[]{:S(2)}) collective-permute-start(bf16[24,128]{1,0:T(8,128)(2,1)S(1)} %fusion.1), channel_id=1, source_target_pairs={{0,4},{1,5},{2,6},{3,7},{4,0},{5,1},{6,2},{7,3},{8,16},{9,17},{10,... | collective-permute-start | bytes 18440 | tf_op jit(solution)/shard_map/ppermute | solution.py:441
  25.8 3.6 %collective-permute-start.5 = (bf16[24,128]{1,0:T(8,128)(2,1)S(1)}, bf16[24,128]{1,0:T(8,128)(2,1)S(1)}, u32[]{:S(2)}, u32[]{:S(2)}) collective-permute-start(bf16[24,128]{1,0:T(8,128)(2,1)S(1)} %fusion.1), channel_id=1, source_target_pairs={{0,8},{1,9},{2,10},{3,11},{4,12},{5,13},{6,14},{7,15},{8,0},{9,1},... | collective-permute-start | bytes 18440 | tf_op jit(solution)/shard_map/ppermute | solution.py:441
  29.5 1.2 %collective-permute-start.7 = (bf16[3,24,128]{2,1,0:T(8,128)(2,1)S(1)}, bf16[3,24,128]{2,1,0:T(8,128)(2,1)S(1)}, u32[]{:S(2)}, u32[]{:S(2)}) collective-permute-start(bf16[3,24,128]{2,1,0:T(8,128)(2,1)S(1)} %get-tuple-element.21), channel_id=1, source_target_pairs={{0,4},{1,5},{2,6},{3,7},{4,0},{5,1},{6,2},{7,3},{8,12},{9,13},{10,... | collective-permute-start | bytes 55304 | tf_op jit(solution)/shard_map/ppermute | solution.py:441
  30.7 5.5 %collective-permute-start.10 = (bf16[2,3,24,128]{3,2,1,0:T(8,128)(2,1)S(1)}, bf16[2,3,24,128]{3,2,1,0:T(8,128)(2,1)S(1)}, u32[]{:S(2)}, u32[]{:S(2)}) collective-permute-start(bf16[2,3,24,128]{3,2,1,0:T(8,128)(2,1)S(1)} %get-tuple-element.19), channel_id=1, source_target_pairs={{0,2},{1,3},{2,0},{3,1},{4,6},{5,7},{6,4},{7,5},{8,10},{9,11},{10,... | collective-permute-start | bytes 110600 | tf_op jit(solution)/shard_map/ppermute | solution.py:441
  33.5 5.2 %collective-permute-start.9 = (bf16[2,3,24,128]{3,2,1,0:T(8,128)(2,1)S(1)}, bf16[2,3,24,128]{3,2,1,0:T(8,128)(2,1)S(1)}, u32[]{:S(2)}, u32[]{:S(2)}) collective-permute-start(bf16[2,3,24,128]{3,2,1,0:T(8,128)(2,1)S(1)} %get-tuple-element.19), channel_id=1, source_target_pairs={{0,3},{1,2},{2,1},{3,0},{4,7},{5,6},{6,5},{7,4},{8,11},{9,10},{10,... | collective-permute-start | bytes 110600 | tf_op jit(solution)/shard_map/ppermute | solution.py:441
  34.9 4.0 %collective-permute-start.8 = (bf16[2,3,24,128]{3,2,1,0:T(8,128)(2,1)S(1)}, bf16[2,3,24,128]{3,2,1,0:T(8,128)(2,1)S(1)}, u32[]{:S(2)}, u32[]{:S(2)}) collective-permute-start(bf16[2,3,24,128]{3,2,1,0:T(8,128)(2,1)S(1)} %get-tuple-element.19), channel_id=1, source_target_pairs={{0,1},{1,0},{2,3},{3,2},{4,5},{5,4},{6,7},{7,6},{8,9},{9,8},{10,11... | collective-permute-start | bytes 110600 | tf_op jit(solution)/shard_map/ppermute | solution.py:441
